TPU v7x, 32 devices: a whole 2x2x4 slice. The times are simulated.
32 devices in a mesh: gx: 2 (over x), gy: 4 (over z), gz: 4 (over y, core).
Axes of the slice: x: 2, y: 2, z: 4, core: 2. Of those that a mesh axis runs over, the one named last changes fastest.
Arguments:
- phase_field: int32 [32, 32, 512], P('gz', 'gx', 'gy'), may hold values 0 or 1
- thermal: float32 [32, 32, 512], P('gz', 'gx', 'gy'), may hold values from 0.5 to 1.5
- velocity: float32 [3, 32, 32, 512], P(None, 'gz', 'gx', 'gy'), may hold values from -6 to 6
- transfer_slope: float32 [8, 4], replicated, may hold values from -3 to 3
- transfer_offset: float32 [8, 4], replicated, may hold values from -1 to 1
- transfer_gain: float32 [8], replicated, may hold values from 0.5 to 4
Outputs:
- corrected: float32 [3, 32, 32, 512], P(None, 'gz', 'gx', 'gy')
- images: float32 [8, 4, 32, 512], P('gz', None, 'gx', 'gy')
All inputs are finite; a program needn't handle non-finite values. No bound on the sum of `phase_field` on one device may be relied on, other than what follows from the above.
Results may differ from a plain program's by a relative error of at most 0.0001.
Values sent between devices are 32-bit elements; how exact they have to be, the bound alone decides.
No kernel may reach another device: no remote copies, remote signals or barrier semaphores. Data moves between devices by JAX's collectives and lax.ppermute only.
A program may use at most 64 MiB of HBM per device.

v0:
```python
import jax
import jax.numpy as jnp
from jax import lax
from jax.sharding import PartitionSpec as P

ITERS = 4


def padded_2(cells, sides, width):
    for axis, dim in sides:
        count = lax.axis_size(axis)
        ends = count - 1
        head = lax.slice_in_dim(cells, 0, width, axis=dim)
        tail = lax.slice_in_dim(cells, cells.shape[dim] - width, cells.shape[dim], axis=dim)
        cells = jnp.concatenate(
            [
                lax.ppermute(tail, axis, [(i, (i + 1) % count) for i in range(ends)]),
                cells,
                lax.ppermute(head, axis, [((i + 1) % count, i) for i in range(ends)]),
            ],
            axis=dim,
        )
    return cells


def prefix(value, axis, combine, identity):
    devices, here = (lax.axis_size(axis), lax.axis_index(axis))
    everything = lax.all_gather(value, axis)
    start = jnp.broadcast_to(jnp.asarray(identity, value.dtype), value.shape)

    def step(k, before):
        reached = k < here
        new = combine(before, everything[k])
        return jnp.where(reached, new, before)

    return lax.fori_loop(0, devices, step, start)


def inner(padded):
    return padded[1:-1, 1:-1, 1:-1]


def neighbours(padded, which):
    if which == 0:
        return (padded[:-2, 1:-1, 1:-1], padded[2:, 1:-1, 1:-1])
    if which == 1:
        return (padded[1:-1, :-2, 1:-1], padded[1:-1, 2:, 1:-1])
    return (padded[1:-1, 1:-1, :-2], padded[1:-1, 1:-1, 2:])


def local(phase_field, thermal, velocity, transfer_slope, transfer_offset, transfer_gain):
    density = (1.0 + 9.0 * phase_field.astype(jnp.float32)) * thermal
    stacked = jnp.concatenate([density[None], velocity], axis=0)
    padded_in = padded_2(stacked, (("gz", 1), ("gx", 2), ("gy", 3)), 1)
    density_pad = padded_in[0]
    vel_aboves = [neighbours(padded_in[1 + which], which)[1] for which in range(3)]
    lowers = []
    uppers = []
    rhs = jnp.zeros_like(density)
    for which in range(3):
        front, back = neighbours(density_pad, which)
        front = jnp.where(front > 0.0, front, density)
        back = jnp.where(back > 0.0, back, density)
        lowers.append(2.0 / (density + front))
        uppers.append(2.0 / (density + back))
        rhs = rhs - (vel_aboves[which] - velocity[which])
    inverse = 1.0 / (lowers[0] + uppers[0] + lowers[1] + uppers[1] + lowers[2] + uppers[2])

    def operate(field):
        padded = padded_2(field, (("gz", 0), ("gx", 1), ("gy", 2)), 1)
        total = jnp.zeros_like(field)
        for which in range(3):
            front, back = neighbours(padded, which)
            total = total + lowers[which] * (field - front)
            total = total + uppers[which] * (field - back)
        return (total, padded)

    pad_shape = (density.shape[0] + 2, density.shape[1] + 2, density.shape[2] + 2)
    pressure_pad = jnp.zeros(pad_shape, jnp.float32)
    residual = rhs

    def joined_sums(resid, cond, mapped):
        return lax.psum((jnp.sum(resid * cond), jnp.sum(mapped * cond)), ("gz", "gx", "gy"))

    precond = inverse * residual
    mapped, cond_pad = operate(precond)
    gamma, delta = joined_sums(residual, precond, mapped)
    alpha = gamma / delta
    ratio = jnp.float32(0.0)
    dir_pad = cond_pad
    along = mapped
    for iteration in range(ITERS):
        if iteration > 0:
            dir_pad = cond_pad + ratio * dir_pad
            along = mapped + ratio * along
        pressure_pad = pressure_pad + alpha * dir_pad
        residual = residual - alpha * along
        if iteration + 1 < ITERS:
            precond = inverse * residual
            mapped, cond_pad = operate(precond)
            gamma_next, delta = joined_sums(residual, precond, mapped)
            ratio = gamma_next / gamma
            alpha = gamma_next / (delta - ratio * gamma_next / alpha)
            gamma = gamma_next
    pressure = inner(pressure_pad)
    pieces = []
    for which in range(3):
        front, unused = neighbours(pressure_pad, which)
        pieces.append(velocity[which] - lowers[which] * (pressure - front))
    corrected = jnp.stack(pieces)
    scalar = pieces[0] + pieces[1] + pieces[2]
    depth_total = jnp.float32(density.shape[0] * lax.axis_size("gz"))

    def render(index):
        slope = transfer_slope[index]
        offset = transfer_offset[index]
        opacity = transfer_gain[index] / depth_total * jax.nn.sigmoid(slope[3] * scalar + offset[3])
        keep = 1.0 - opacity
        inclusive = jnp.cumprod(keep, axis=0)
        passed = jnp.concatenate([jnp.ones_like(inclusive[:1]), inclusive[:-1]], axis=0)
        weight = passed * opacity
        planes = jnp.stack(
            [
                jnp.sum(weight * jax.nn.sigmoid(slope[channel] * scalar + offset[channel]), axis=0)
                for channel in range(3)
            ]
        )
        return (planes, inclusive[-1])

    colors, through = lax.map(render, jnp.arange(transfer_slope.shape[0]))

    def multiply(earlier, later):
        return earlier * later

    before = prefix(through, "gz", multiply, jnp.ones_like(through))
    terms = jnp.concatenate([before[:, None] * colors, (before * (1.0 - through))[:, None]], axis=1)
    images = lax.psum_scatter(terms, "gz", scatter_dimension=0, tiled=True)
    return (corrected, images)


def solution(mesh):
    return jax.shard_map(
        local,
        mesh=mesh,
        in_specs=(
            P("gz", "gx", "gy"),
            P("gz", "gx", "gy"),
            P(None, "gz", "gx", "gy"),
            P(),
            P(),
            P(),
        ),
        out_specs=(P(None, "gz", "gx", "gy"), P("gz", None, "gx", "gy")),
        check_vma=False,
    )
```

profile of v0, /device:TPU:0, one launch (start us, length us, event | category | flops | bytes accessed | tf_op | source)
XLA Modules:
  0.0 450.6 jit_solution(13179378658986370618)
XLA Ops:
  8.2 2.4 collective-permute-start
  11.9 3.9 collective-permute-done.1
  15.8 3.4 collective-permute-start.2
  20.7 4.2 collective-permute-done.3
  25.2 3.5 collective-permute-start.4
  30.0 10.0 %collective-permute-done.4 = f32[4,10,18,1]{3,2,1,0:T(8,128)S(1)} collective-permute-done((f32[4,10,18,1]{3,2,1,0:T(8,128)S(1)}, f32[4,10,18,1]{3,2,1,0:T(8,128)S(1)}, u32[]{:S(2)}, u32[]{:S(2)}) %collective-permute-start.4) | collective-permute-done | bytes 2912 | tf_op jit(solution)/shard_map/ppermute | solution.py:17
  40.0 4.6 %collective-permute-done.5 = f32[4,10,18,1]{3,2,1,0:T(8,128)S(1)} collective-permute-done((f32[4,10,18,1]{3,2,1,0:T(8,128)S(1)}, f32[4,10,18,1]{3,2,1,0:T(8,128)S(1)}, u32[]{:S(2)}, u32[]{:S(2)}) %collective-permute-start.5) | collective-permute-done | bytes 2912 | tf_op jit(solution)/shard_map/ppermute | solution.py:19
  45.6 2.0 collective-permute-start.6
  48.9 1.8 collective-permute-done.7
  50.6 1.5 collective-permute-start.8
  53.4 4.2 collective-permute-done.9
  57.8 3.5 collective-permute-start.10
  62.5 2.0 collective-permute-done.10
  64.5 4.1 collective-permute-done.11
  69.4 39.5 %all-reduce.4 = (f32[]{:T(128)}, f32[]{:T(128)}) all-reduce(f32[]{:T(128)} %get-tuple-element.150, f32[]{:T(128)} %get-tuple-element.149), channel_id=1, replica_groups=mesh['gx'=2,'gy'=4,'gz'=4] {'gz','gx','gy'}, use_global_device_ids=true, to_apply=%region_1.2 | all-reduce | flops 2 | bytes 16 | tf_op jit(solution)/shard_map/psum | solution.py:83
  112.9 4.5 collective-permute-done.13
  117.3 3.2 collective-permute-start.14
  121.8 4.2 collective-permute-done.15
  126.1 2.3 collective-permute-start.16
  129.7 2.4 collective-permute-done.16
  132.1 4.1 collective-permute-done.17
  137.0 38.7 %all-reduce.3 = (f32[]{:T(128)}, f32[]{:T(128)}) all-reduce(f32[]{:T(128)} %get-tuple-element.148, f32[]{:T(128)} %get-tuple-element.147), channel_id=1, replica_groups=mesh['gx'=2,'gy'=4,'gz'=4] {'gz','gx','gy'}, use_global_device_ids=true, to_apply=%region_5.6 | all-reduce | flops 2 | bytes 16 | tf_op jit(solution)/shard_map/psum | solution.py:83
  182.9 4.5 %collective-permute-done.19 = f32[1,16,128]{2,1,0:T(8,128)S(1)} collective-permute-done((f32[1,16,128]{2,1,0:T(8,128)S(1)}, f32[1,16,128]{2,1,0:T(8,128)S(1)}, u32[]{:S(2)}, u32[]{:S(2)}) %collective-permute-start.19) | collective-permute-done | bytes 8224 | tf_op jit(solution)/shard_map/ppermute | solution.py:19
  187.4 3.2 collective-permute-start.20
  192.0 4.2 collective-permute-done.21
  196.3 3.1 collective-permute-start.22
  200.7 2.4 collective-permute-done.22
  203.1 4.1 collective-permute-done.23
  207.9 38.8 %all-reduce.2 = (f32[]{:T(128)}, f32[]{:T(128)}) all-reduce(f32[]{:T(128)} %get-tuple-element.146, f32[]{:T(128)} %get-tuple-element.145), channel_id=1, replica_groups=mesh['gx'=2,'gy'=4,'gz'=4] {'gz','gx','gy'}, use_global_device_ids=true, to_apply=%region_9.10 | all-reduce | flops 2 | bytes 16 | tf_op jit(solution)/shard_map/psum | solution.py:83
  253.9 4.5 collective-permute-done.25
  258.4 3.2 collective-permute-start.26
  262.9 4.2 collective-permute-done.27
  267.2 3.0 collective-permute-start.28
  271.6 2.4 collective-permute-done.28
  273.9 4.1 collective-permute-done.29
  278.8 38.8 %all-reduce.1 = (f32[]{:T(128)}, f32[]{:T(128)}) all-reduce(f32[]{:T(128)} %get-tuple-element.187, f32[]{:T(128)} %fusion.29), channel_id=1, replica_groups=mesh['gx'=2,'gy'=4,'gz'=4] {'gz','gx','gy'}, use_global_device_ids=true, to_apply=%region_13.14 | all-reduce | flops 2 | bytes 16 | tf_op jit(solution)/shard_map/psum | solution.py:83
  323.1 93.0 %while.28 = (s32[]{:T(128)}, f32[8,3,16,128]{3,2,1,0:T(8,128)S(1)}, f32[8,16,128]{2,1,0:T(8,128)S(1)}, s32[8]{0:T(128)S(1)}, f32[8]{0:T(128)S(1)}, /*index=5*/f3...) while((s32[]{:T(128)}, f32[8,3,16,128]{3,2,1,0:T(8,128)S(1)}, ...), condition=%wide.region_21.22_spmd.clone, body=%wide.region_16.21_spmd.sunk.clone | while | flops 694278 | bytes 459103 | solution.py:130
  328.1 1.3 fusion.138
  329.5 5.2 %multiply_reduce_fusion.12 = (f32[16,128]{1,0:T(8,128)S(1)}, f32[16,128]{1,0:T(8,128)S(1)}, f32[16,128]{1,0:T(8,128)S(1)}) fusion(f32[8,16,128]{2,1,0:T(8,128)S(1)} %get-tuple-element.420, f32[]{:T(128)} %bitcast.81, f32[]{:T(128)} %bitcast.82, f32[]{:T(128)} %bitcast.83, f32[]{:T(128)} %bitcast.84, f32[]{:T(128)} %bitcast.85, ...), kind=kLoop, calls=%fused_computation.2.clone.1.clone | loop fusion | flops 452608 | bytes 147492 | tf_op jit(solution)/shard_map/while/body/eval_jaxpr/reduce_sum | solution.py:124
  341.1 5.2 %multiply_reduce_fusion.12 = (f32[16,128]{1,0:T(8,128)S(1)}, f32[16,128]{1,0:T(8,128)S(1)}, f32[16,128]{1,0:T(8,128)S(1)}) fusion(f32[8,16,128]{2,1,0:T(8,128)S(1)} %get-tuple-element.420, f32[]{:T(128)} %bitcast.81, f32[]{:T(128)} %bitcast.82, f32[]{:T(128)} %bitcast.83, f32[]{:T(128)} %bitcast.84, f32[]{:T(128)} %bitcast.85, ...), kind=kLoop, calls=%fused_computation.2.clone.1.clone | loop fusion | flops 452608 | bytes 147492 | tf_op jit(solution)/shard_map/while/body/eval_jaxpr/reduce_sum | solution.py:124
  352.7 5.2 %multiply_reduce_fusion.12 = (f32[16,128]{1,0:T(8,128)S(1)}, f32[16,128]{1,0:T(8,128)S(1)}, f32[16,128]{1,0:T(8,128)S(1)}) fusion(f32[8,16,128]{2,1,0:T(8,128)S(1)} %get-tuple-element.420, f32[]{:T(128)} %bitcast.81, f32[]{:T(128)} %bitcast.82, f32[]{:T(128)} %bitcast.83, f32[]{:T(128)} %bitcast.84, f32[]{:T(128)} %bitcast.85, ...), kind=kLoop, calls=%fused_computation.2.clone.1.clone | loop fusion | flops 452608 | bytes 147492 | tf_op jit(solution)/shard_map/while/body/eval_jaxpr/reduce_sum | solution.py:124
  364.3 5.2 %multiply_reduce_fusion.12 = (f32[16,128]{1,0:T(8,128)S(1)}, f32[16,128]{1,0:T(8,128)S(1)}, f32[16,128]{1,0:T(8,128)S(1)}) fusion(f32[8,16,128]{2,1,0:T(8,128)S(1)} %get-tuple-element.420, f32[]{:T(128)} %bitcast.81, f32[]{:T(128)} %bitcast.82, f32[]{:T(128)} %bitcast.83, f32[]{:T(128)} %bitcast.84, f32[]{:T(128)} %bitcast.85, ...), kind=kLoop, calls=%fused_computation.2.clone.1.clone | loop fusion | flops 452608 | bytes 147492 | tf_op jit(solution)/shard_map/while/body/eval_jaxpr/reduce_sum | solution.py:124
  376.0 5.2 %multiply_reduce_fusion.12 = (f32[16,128]{1,0:T(8,128)S(1)}, f32[16,128]{1,0:T(8,128)S(1)}, f32[16,128]{1,0:T(8,128)S(1)}) fusion(f32[8,16,128]{2,1,0:T(8,128)S(1)} %get-tuple-element.420, f32[]{:T(128)} %bitcast.81, f32[]{:T(128)} %bitcast.82, f32[]{:T(128)} %bitcast.83, f32[]{:T(128)} %bitcast.84, f32[]{:T(128)} %bitcast.85, ...), kind=kLoop, calls=%fused_computation.2.clone.1.clone | loop fusion | flops 452608 | bytes 147492 | tf_op jit(solution)/shard_map/while/body/eval_jaxpr/reduce_sum | solution.py:124
  387.6 5.2 %multiply_reduce_fusion.12 = (f32[16,128]{1,0:T(8,128)S(1)}, f32[16,128]{1,0:T(8,128)S(1)}, f32[16,128]{1,0:T(8,128)S(1)}) fusion(f32[8,16,128]{2,1,0:T(8,128)S(1)} %get-tuple-element.420, f32[]{:T(128)} %bitcast.81, f32[]{:T(128)} %bitcast.82, f32[]{:T(128)} %bitcast.83, f32[]{:T(128)} %bitcast.84, f32[]{:T(128)} %bitcast.85, ...), kind=kLoop, calls=%fused_computation.2.clone.1.clone | loop fusion | flops 452608 | bytes 147492 | tf_op jit(solution)/shard_map/while/body/eval_jaxpr/reduce_sum | solution.py:124
  399.2 5.2 %multiply_reduce_fusion.12 = (f32[16,128]{1,0:T(8,128)S(1)}, f32[16,128]{1,0:T(8,128)S(1)}, f32[16,128]{1,0:T(8,128)S(1)}) fusion(f32[8,16,128]{2,1,0:T(8,128)S(1)} %get-tuple-element.420, f32[]{:T(128)} %bitcast.81, f32[]{:T(128)} %bitcast.82, f32[]{:T(128)} %bitcast.83, f32[]{:T(128)} %bitcast.84, f32[]{:T(128)} %bitcast.85, ...), kind=kLoop, calls=%fused_computation.2.clone.1.clone | loop fusion | flops 452608 | bytes 147492 | tf_op jit(solution)/shard_map/while/body/eval_jaxpr/reduce_sum | solution.py:124
  410.8 5.2 %multiply_reduce_fusion.12 = (f32[16,128]{1,0:T(8,128)S(1)}, f32[16,128]{1,0:T(8,128)S(1)}, f32[16,128]{1,0:T(8,128)S(1)}) fusion(f32[8,16,128]{2,1,0:T(8,128)S(1)} %get-tuple-element.420, f32[]{:T(128)} %bitcast.81, f32[]{:T(128)} %bitcast.82, f32[]{:T(128)} %bitcast.83, f32[]{:T(128)} %bitcast.84, f32[]{:T(128)} %bitcast.85, ...), kind=kLoop, calls=%fused_computation.2.clone.1.clone | loop fusion | flops 452608 | bytes 147492 | tf_op jit(solution)/shard_map/while/body/eval_jaxpr/reduce_sum | solution.py:124
  416.1 6.8 %all-gather = f32[32,16,128]{2,1,0:T(8,128)S(1)} all-gather(f32[8,16,128]{2,1,0:T(8,128)S(1)} %get-tuple-element.124), channel_id=2, replica_groups=mesh['gx'=2,'gy'=4,'gz'=4] {'gz'}, dimensions={0}, use_global_device_ids=true | all-gather | bytes 327680 | tf_op jit(solution)/shard_map/all_gather | solution.py:28
  424.5 19.3 %reduce-scatter.2.cloned.1.call-done = f32[2,4,16,128]{3,2,1,0:T(8,128)} async-done(((f32[8,4,16,128]{3,2,1,0:T(8,128)}), f32[2,4,16,128]{3,2,1,0:T(8,128)}) %reduce-scatter.2.cloned.1.call-update) | async-done | bytes 65552 | tf_op jit(solution)/shard_map/reduce_scatter | solution.py:137
  (155 shorter events, 62.1 us)
Async XLA Ops:
  7.2 1.0 copy-start
  7.2 436.6 %reduce-scatter.2.cloned.1.call-start = ((), (), s32[]{:S(2)}) async-start(), calls=%async_computation.1 | async-start | bytes 327680 | tf_op jit(solution)/shard_map/reduce_scatter | solution.py:137
  8.2 3.7 collective-permute-start
  10.6 5.2 %collective-permute-start.1 = (f32[4,1,16,128]{3,2,1,0:T(8,128)S(1)}, f32[4,1,16,128]{3,2,1,0:T(8,128)S(1)}, u32[]{:S(2)}, u32[]{:S(2)}) collective-permute-start(f32[4,1,16,128]{3,2,1,0:T(8,128)S(1)} %get-tuple-element.224), channel_id=1, source_target_pairs={{1,0},{2,1},{3,2},{5,4},{6,5},{7,6},{9,8},{10,9},{11,10},{13,12},{... | collective-permute-start | bytes 98312 | tf_op jit(solution)/shard_map/ppermute | solution.py:19
  15.8 4.9 %collective-permute-start.2 = (f32[4,10,1,128]{3,2,1,0:T(1,128)S(1)}, f32[4,10,1,128]{3,2,1,0:T(1,128)S(1)}, u32[]{:S(2)}, u32[]{:S(2)}) collective-permute-start(f32[4,10,1,128]{3,2,1,0:T(1,128)S(1)} %get-tuple-element.221), channel_id=1, source_target_pairs={{0,16},{1,17},{2,18},{3,19},{4,20},{5,21},{6,22},{7,23},{8,24},{9,... | collective-permute-start | bytes 61448 | tf_op jit(solution)/shard_map/ppermute | solution.py:17
  19.2 5.7 %collective-permute-start.3 = (f32[4,10,1,128]{3,2,1,0:T(1,128)S(1)}, f32[4,10,1,128]{3,2,1,0:T(1,128)S(1)}, u32[]{:S(2)}, u32[]{:S(2)}) collective-permute-start(f32[4,10,1,128]{3,2,1,0:T(1,128)S(1)} %get-tuple-element.222), channel_id=1, source_target_pairs={{16,0},{17,1},{18,2},{19,3},{20,4},{21,5},{22,6},{23,7},{24,8},{25... | collective-permute-start | bytes 61448 | tf_op jit(solution)/shard_map/ppermute | solution.py:19
  25.2 14.8 %collective-permute-start.4 = (f32[4,10,18,1]{3,2,1,0:T(8,128)S(1)}, f32[4,10,18,1]{3,2,1,0:T(8,128)S(1)}, u32[]{:S(2)}, u32[]{:S(2)}) collective-permute-start(f32[4,10,18,1]{3,2,1,0:T(8,128)S(1)} %get-tuple-element.219), channel_id=1, source_target_pairs={{0,4},{4,8},{8,12},{1,5},{5,9},{9,13},{2,6},{6,10},{10,14},{3,7},{... | collective-permute-start | bytes 8648 | tf_op jit(solution)/shard_map/ppermute | solution.py:17
  28.7 15.9 %collective-permute-start.5 = (f32[4,10,18,1]{3,2,1,0:T(8,128)S(1)}, f32[4,10,18,1]{3,2,1,0:T(8,128)S(1)}, u32[]{:S(2)}, u32[]{:S(2)}) collective-permute-start(f32[4,10,18,1]{3,2,1,0:T(8,128)S(1)} %get-tuple-element.220), channel_id=1, source_target_pairs={{4,0},{8,4},{12,8},{5,1},{9,5},{13,9},{6,2},{10,6},{14,10},{7,3},{... | collective-permute-start | bytes 8648 | tf_op jit(solution)/shard_map/ppermute | solution.py:19
  45.6 3.3 collective-permute-start.6
  47.5 3.1 collective-permute-start.7
  50.6 2.8 collective-permute-start.8
  52.1 5.5 %collective-permute-start.9 = (f32[10,1,128]{2,1,0:T(1,128)S(1)}, f32[10,1,128]{2,1,0:T(1,128)S(1)}, u32[]{:S(2)}, u32[]{:S(2)}) collective-permute-start(f32[10,1,128]{2,1,0:T(1,128)S(1)} %get-tuple-element.240), channel_id=1, source_target_pairs={{16,0},{17,1},{18,2},{19,3},{20,4},{21,5},{22,6},{23,7},{24,8},{25... | collective-permute-start | bytes 15368 | tf_op jit(solution)/shard_map/ppermute | solution.py:19
  57.8 6.8 %collective-permute-start.10 = (f32[10,18,1]{2,1,0:T(8,128)S(1)}, f32[10,18,1]{2,1,0:T(8,128)S(1)}, u32[]{:S(2)}, u32[]{:S(2)}) collective-permute-start(f32[10,18,1]{2,1,0:T(8,128)S(1)} %get-tuple-element.231), channel_id=1, source_target_pairs={{0,4},{4,8},{8,12},{1,5},{5,9},{9,13},{2,6},{6,10},{10,14},{3,7},{... | collective-permute-start | bytes 2168 | tf_op jit(solution)/shard_map/ppermute | solution.py:17
  61.2 7.4 %collective-permute-start.11 = (f32[10,18,1]{2,1,0:T(8,128)S(1)}, f32[10,18,1]{2,1,0:T(8,128)S(1)}, u32[]{:S(2)}, u32[]{:S(2)}) collective-permute-start(f32[10,18,1]{2,1,0:T(8,128)S(1)} %get-tuple-element.232), channel_id=1, source_target_pairs={{4,0},{8,4},{12,8},{5,1},{9,5},{13,9},{6,2},{10,6},{14,10},{7,3},{... | collective-permute-start | bytes 2168 | tf_op jit(solution)/shard_map/ppermute | solution.py:19
  110.3 2.6 collective-permute-start.12
  111.6 5.8 %collective-permute-start.13 = (f32[1,16,128]{2,1,0:T(8,128)S(1)}, f32[1,16,128]{2,1,0:T(8,128)S(1)}, u32[]{:S(2)}, u32[]{:S(2)}) collective-permute-start(f32[1,16,128]{2,1,0:T(8,128)S(1)} %get-tuple-element.246), channel_id=1, source_target_pairs={{1,0},{2,1},{3,2},{5,4},{6,5},{7,6},{9,8},{10,9},{11,10},{13,12},{... | collective-permute-start | bytes 24584 | tf_op jit(solution)/shard_map/ppermute | solution.py:19
  117.3 4.5 collective-permute-start.14
  120.5 5.5 %collective-permute-start.15 = (f32[10,1,128]{2,1,0:T(1,128)S(1)}, f32[10,1,128]{2,1,0:T(1,128)S(1)}, u32[]{:S(2)}, u32[]{:S(2)}) collective-permute-start(f32[10,1,128]{2,1,0:T(1,128)S(1)} %get-tuple-element.238), channel_id=1, source_target_pairs={{16,0},{17,1},{18,2},{19,3},{20,4},{21,5},{22,6},{23,7},{24,8},{25... | collective-permute-start | bytes 15368 | tf_op jit(solution)/shard_map/ppermute | solution.py:19
  126.1 6.0 %collective-permute-start.16 = (f32[10,18,1]{2,1,0:T(8,128)S(1)}, f32[10,18,1]{2,1,0:T(8,128)S(1)}, u32[]{:S(2)}, u32[]{:S(2)}) collective-permute-start(f32[10,18,1]{2,1,0:T(8,128)S(1)} %get-tuple-element.229), channel_id=1, source_target_pairs={{0,4},{4,8},{8,12},{1,5},{5,9},{9,13},{2,6},{6,10},{10,14},{3,7},{... | collective-permute-start | bytes 2168 | tf_op jit(solution)/shard_map/ppermute | solution.py:17
  128.4 7.8 %collective-permute-start.17 = (f32[10,18,1]{2,1,0:T(8,128)S(1)}, f32[10,18,1]{2,1,0:T(8,128)S(1)}, u32[]{:S(2)}, u32[]{:S(2)}) collective-permute-start(f32[10,18,1]{2,1,0:T(8,128)S(1)} %get-tuple-element.230), channel_id=1, source_target_pairs={{4,0},{8,4},{12,8},{5,1},{9,5},{13,9},{6,2},{10,6},{14,10},{7,3},{... | collective-permute-start | bytes 2168 | tf_op jit(solution)/shard_map/ppermute | solution.py:19
  180.3 2.6 collective-permute-start.18
  181.6 5.8 %collective-permute-start.19 = (f32[1,16,128]{2,1,0:T(8,128)S(1)}, f32[1,16,128]{2,1,0:T(8,128)S(1)}, u32[]{:S(2)}, u32[]{:S(2)}) collective-permute-start(f32[1,16,128]{2,1,0:T(8,128)S(1)} %get-tuple-element.244), channel_id=1, source_target_pairs={{1,0},{2,1},{3,2},{5,4},{6,5},{7,6},{9,8},{10,9},{11,10},{13,12},{... | collective-permute-start | bytes 24584 | tf_op jit(solution)/shard_map/ppermute | solution.py:19
  187.4 4.5 %collective-permute-start.20 = (f32[10,1,128]{2,1,0:T(1,128)S(1)}, f32[10,1,128]{2,1,0:T(1,128)S(1)}, u32[]{:S(2)}, u32[]{:S(2)}) collective-permute-start(f32[10,1,128]{2,1,0:T(1,128)S(1)} %get-tuple-element.235), channel_id=1, source_target_pairs={{0,16},{1,17},{2,18},{3,19},{4,20},{5,21},{6,22},{7,23},{8,24},{9,... | collective-permute-start | bytes 15368 | tf_op jit(solution)/shard_map/ppermute | solution.py:17
  190.7 5.5 %collective-permute-start.21 = (f32[10,1,128]{2,1,0:T(1,128)S(1)}, f32[10,1,128]{2,1,0:T(1,128)S(1)}, u32[]{:S(2)}, u32[]{:S(2)}) collective-permute-start(f32[10,1,128]{2,1,0:T(1,128)S(1)} %get-tuple-element.236), channel_id=1, source_target_pairs={{16,0},{17,1},{18,2},{19,3},{20,4},{21,5},{22,6},{23,7},{24,8},{25... | collective-permute-start | bytes 15368 | tf_op jit(solution)/shard_map/ppermute | solution.py:19
  196.3 6.8 %collective-permute-start.22 = (f32[10,18,1]{2,1,0:T(8,128)S(1)}, f32[10,18,1]{2,1,0:T(8,128)S(1)}, u32[]{:S(2)}, u32[]{:S(2)}) collective-permute-start(f32[10,18,1]{2,1,0:T(8,128)S(1)} %get-tuple-element.227), channel_id=1, source_target_pairs={{0,4},{4,8},{8,12},{1,5},{5,9},{9,13},{2,6},{6,10},{10,14},{3,7},{... | collective-permute-start | bytes 2168 | tf_op jit(solution)/shard_map/ppermute | solution.py:17
  199.4 7.8 %collective-permute-start.23 = (f32[10,18,1]{2,1,0:T(8,128)S(1)}, f32[10,18,1]{2,1,0:T(8,128)S(1)}, u32[]{:S(2)}, u32[]{:S(2)}) collective-permute-start(f32[10,18,1]{2,1,0:T(8,128)S(1)} %get-tuple-element.228), channel_id=1, source_target_pairs={{4,0},{8,4},{12,8},{5,1},{9,5},{13,9},{6,2},{10,6},{14,10},{7,3},{... | collective-permute-start | bytes 2168 | tf_op jit(solution)/shard_map/ppermute | solution.py:19
  251.3 2.6 collective-permute-start.24
  252.6 5.8 %collective-permute-start.25 = (f32[1,16,128]{2,1,0:T(8,128)S(1)}, f32[1,16,128]{2,1,0:T(8,128)S(1)}, u32[]{:S(2)}, u32[]{:S(2)}) collective-permute-start(f32[1,16,128]{2,1,0:T(8,128)S(1)} %get-tuple-element.242), channel_id=1, source_target_pairs={{1,0},{2,1},{3,2},{5,4},{6,5},{7,6},{9,8},{10,9},{11,10},{13,12},{... | collective-permute-start | bytes 24584 | tf_op jit(solution)/shard_map/ppermute | solution.py:19
  258.4 4.5 %collective-permute-start.26 = (f32[10,1,128]{2,1,0:T(1,128)S(1)}, f32[10,1,128]{2,1,0:T(1,128)S(1)}, u32[]{:S(2)}, u32[]{:S(2)}) collective-permute-start(f32[10,1,128]{2,1,0:T(1,128)S(1)} %get-tuple-element.233), channel_id=1, source_target_pairs={{0,16},{1,17},{2,18},{3,19},{4,20},{5,21},{6,22},{7,23},{8,24},{9,... | collective-permute-start | bytes 15368 | tf_op jit(solution)/shard_map/ppermute | solution.py:17
  261.6 5.5 %collective-permute-start.27 = (f32[10,1,128]{2,1,0:T(1,128)S(1)}, f32[10,1,128]{2,1,0:T(1,128)S(1)}, u32[]{:S(2)}, u32[]{:S(2)}) collective-permute-start(f32[10,1,128]{2,1,0:T(1,128)S(1)} %get-tuple-element.234), channel_id=1, source_target_pairs={{16,0},{17,1},{18,2},{19,3},{20,4},{21,5},{22,6},{23,7},{24,8},{25... | collective-permute-start | bytes 15368 | tf_op jit(solution)/shard_map/ppermute | solution.py:19
  267.2 6.7 %collective-permute-start.28 = (f32[10,18,1]{2,1,0:T(8,128)S(1)}, f32[10,18,1]{2,1,0:T(8,128)S(1)}, u32[]{:S(2)}, u32[]{:S(2)}) collective-permute-start(f32[10,18,1]{2,1,0:T(8,128)S(1)} %get-tuple-element.225), channel_id=1, source_target_pairs={{0,4},{4,8},{8,12},{1,5},{5,9},{9,13},{2,6},{6,10},{10,14},{3,7},{... | collective-permute-start | bytes 2168 | tf_op jit(solution)/shard_map/ppermute | solution.py:17
  270.3 7.8 %collective-permute-start.29 = (f32[10,18,1]{2,1,0:T(8,128)S(1)}, f32[10,18,1]{2,1,0:T(8,128)S(1)}, u32[]{:S(2)}, u32[]{:S(2)}) collective-permute-start(f32[10,18,1]{2,1,0:T(8,128)S(1)} %get-tuple-element.226), channel_id=1, source_target_pairs={{4,0},{8,4},{12,8},{5,1},{9,5},{13,9},{6,2},{10,6},{14,10},{7,3},{... | collective-permute-start | bytes 2168 | tf_op jit(solution)/shard_map/ppermute | solution.py:19
  322.3 0.7 copy-start.2
  322.4 0.7 copy-start.1
  322.4 0.7 copy-start.3
Sparse Core Ops, SparseCore 0:
  423.9 19.8 reduce-scatter.1
where the time goes:
time: 453 us; the launch traced here: 451 us
  blocking collectives  163 us (36%)
  waiting for transfers between devices  99.9 us (22%)
  other arithmetic  60.1 us (13%)
  starting transfers between devices  57.5 us (13%)
  between operations  28.3 us (6%)
  loops' own time  21.2 us (5%)
  local copies, waits for them, and re-layouts  21.1 us (5%)
    psum x4, blocking collectives, joined_sums(): lax.psum((jnp.sum(resid * cond), jnp.sum(mapped * cond)), ('gz', 'gx', 'g...  156 us
    ppermute x15, waiting for transfers between devices, padded_2(): lax.ppermute(head, axis, [((i + 1) % count, i) for i in range(ends)])  61.2 us
    reduce_sum x8, other arithmetic, render(): jnp.sum(weight * jax.nn.sigmoid(slope[channel] * scalar + offset[channel]...  41.5 us
    ppermute x15, starting transfers between devices, padded_2(): lax.ppermute(tail, axis, [(i, (i + 1) % count) for i in range(ends)])  38 us
    another operation x1, loops' own time, local(): colors, through = lax.map(render, jnp.arange(transfer_slope.shape[0]))  21.1 us
    ppermute x15, waiting for transfers between devices, padded_2(): lax.ppermute(tail, axis, [(i, (i + 1) % count) for i in range(ends)])  19.4 us
    ppermute x15, starting transfers between devices, padded_2(): lax.ppermute(head, axis, [((i + 1) % count, i) for i in range(ends)])  19.4 us
    reduce_scatter x1, waiting for transfers between devices, local(): images = lax.psum_scatter(terms, 'gz', scatter_dimension=0, tiled=True)  19.3 us
  transfers between devices with their start and end apart: 31, of which 22 were waited for; matrix products, arithmetic and copies ran while one was open for 0% of the time, Pallas kernels for 0%

commit v1 on v0

v1 whole, which is shorter than its diff:
```python
import math

import jax
import jax.numpy as jnp
from jax import lax
from jax.experimental import pallas as pl
from jax.experimental.pallas import tpu as pltpu
from jax.sharding import PartitionSpec as P

ITERS = 4
HALO = ITERS + 1
FIELDS = 4
LANES = 128
LOG2E = math.log2(math.e)
F32 = jnp.float32


def snake(ngx, ngz):
    order = []
    for x in range(ngx):
        depths = range(ngz) if x % 2 == 0 else reversed(range(ngz))
        order.extend((x, z) for z in depths)
    return order


def chain_pairs(ngx, ngy, ngz, hop):
    places = []
    order = snake(ngx, ngz)
    for y in range(ngy):
        for x, z in order if y % 2 == 0 else order[::-1]:
            places.append((x * ngy + y) * ngz + z)
    return list(zip(places[:-hop], places[hop:]))


def roll(value, shift, axis):
    size = value.shape[axis]
    shift = shift % size
    return value if shift == 0 else pltpu.roll(value, shift, axis)


def owner(table, c):
    forward = lax.axis_index("gy") % 2 == 0
    return jnp.where(forward, table[c], table[len(table) - 1 - c])


def pack_kernel(phase_ref, thermal_ref, velocity_ref, out_ref, *, table, chunk):
    zl, xl, yl = thermal_ref.shape
    density = (1.0 + 9.0 * phase_ref[...].astype(F32)) * thermal_ref[...]
    for f in range(FIELDS):
        field = density if f == 0 else velocity_ref[f - 1]
        turned = field.reshape(zl * xl, yl).T
        for c in range(yl // chunk):
            rows = turned[c * chunk : (c + 1) * chunk]
            out_ref[owner(table, c), pl.ds(f, chunk, stride=FIELDS), :] = rows


class Shifts:
    def __init__(self, ngx, ngz, zl, xl):
        self.ngx, self.ngz, self.zl, self.xl = ngx, ngz, zl, xl
        shape = (1, ngx * ngz, zl * xl)
        lane = lax.broadcasted_iota(jnp.int32, shape, 2)
        sub = lax.broadcasted_iota(jnp.int32, shape, 1)
        z, x = lane // xl, lane % xl
        gz, gx = sub // ngx, sub % ngx
        self.z_first, self.z_last = z == 0, z == zl - 1
        self.x_first, self.x_last = x == 0, x == xl - 1
        self.z_low = self.z_first & (gz == 0)
        self.z_high = self.z_last & (gz == ngz - 1)
        self.x_low = self.x_first & (gx == 0)
        self.x_high = self.x_last & (gx == ngx - 1)

    def below_z(self, f):
        near = roll(f, self.xl, 2)
        return jnp.where(self.z_first, roll(near, self.ngx, 1), near)

    def above_z(self, f):
        near = roll(f, -self.xl, 2)
        return jnp.where(self.z_last, roll(near, -self.ngx, 1), near)

    def below_x(self, f):
        far = roll(roll(f, 1 - self.xl, 2), 1, 1)
        return jnp.where(self.x_first, far, roll(f, 1, 2))

    def above_x(self, f):
        far = roll(roll(f, self.xl - 1, 2), -1, 1)
        return jnp.where(self.x_last, far, roll(f, -1, 2))


def krylov_kernel(*refs, ngx, ngz, zl, xl, chunk, hops, margin, step):
    own_ref = refs[0]
    low_refs, high_refs = refs[1 : 1 + hops], refs[1 + hops : 1 + 2 * hops]
    basis_ref, lower_ref, sums_ref, dens, coef, vec, diag, source = refs[1 + 2 * hops :]
    S, L = ngx * ngz, zl * xl
    E = chunk + 2 * HALO
    move = Shifts(ngx, ngz, zl, xl)

    def plane(e, f):
        k = e - HALO
        if 0 <= k < chunk:
            return own_ref[pl.ds(k * FIELDS + f, S, stride=chunk * FIELDS), :]
        far = -k - 1 if k < 0 else k - chunk
        hop, at = far // chunk, far % chunk
        ref = low_refs[hop] if k < 0 else high_refs[hop]
        at = margin - 1 - at if k < 0 else at
        return ref[pl.ds(at * FIELDS + f, S, stride=margin * FIELDS), :]

    def planes(a, b, f):
        return jnp.stack([plane(e, f) for e in range(a, b)])

    def pieces(a, b):
        return [(i, min(i + step, b)) for i in range(a, b, step)]

    for e in range(E):
        dens[e] = plane(e, 0)
    for a, b in pieces(1, E - 1):
        d, before, after = dens[a:b], dens[a - 1 : b - 1], dens[a + 1 : b + 1]
        inside = d > 0.0
        d = jnp.where(inside, d, 1.0)

        def face(missing, other):
            return 2.0 / (d + jnp.where(missing, d, other))

        lz, uz = face(move.z_low, move.below_z(d)), face(move.z_high, move.above_z(d))
        lx, ux = face(move.x_low, move.below_x(d)), face(move.x_high, move.above_x(d))
        ly, uy = face(before <= 0.0, before), face(after <= 0.0, after)
        total = lz + uz + lx + ux + ly + uy
        inverse = jnp.where(inside, 1.0 / total, 0.0)
        coef[0, a:b] = jnp.where(move.z_low, 0.0, inverse * lz)
        coef[1, a:b] = jnp.where(move.z_high, 0.0, inverse * uz)
        coef[2, a:b] = jnp.where(move.x_low, 0.0, inverse * lx)
        coef[3, a:b] = jnp.where(move.x_high, 0.0, inverse * ux)
        coef[4, a:b] = inverse * ly
        coef[5, a:b] = inverse * uy
        vz, vx = planes(a, b, 1), planes(a, b, 2)
        rhs = -(jnp.where(move.z_high, 0.0, move.above_z(vz)) - vz)
        rhs = rhs - (jnp.where(move.x_high, 0.0, move.above_x(vx)) - vx)
        rhs = rhs - (planes(a + 1, b + 1, 3) - planes(a, b, 3))
        vec[0, a:b] = inverse * rhs
        for e in range(max(a, HALO), min(b, HALO + chunk)):
            diag[e - HALO] = total[e - a]
            source[e - HALO] = rhs[e - a]
            for k, faces in enumerate((lz, lx, ly)):
                lower_ref[k, e - HALO] = faces[e - a]

    def applied(k, a, b):
        f = vec[k, a:b]
        out = coef[0, a:b] * move.below_z(f) + coef[1, a:b] * move.above_z(f)
        out = out + (coef[2, a:b] * move.below_x(f) + coef[3, a:b] * move.above_x(f))
        return out + (coef[4, a:b] * vec[k, a - 1 : b - 1] + coef[5, a:b] * vec[k, a + 1 : b + 1])

    for k in range(1, ITERS):
        for a, b in pieces(1 + k, E - 1 - k):
            vec[k, a:b] = applied(k - 1, a, b)

    count = 2 * ITERS - 1
    powers = [0.0] * count
    firsts = [0.0] * ITERS
    steps = [0.0] * (count + 1)
    for a, b in pieces(HALO, HALO + chunk):
        own = slice(a - HALO, b - HALO)
        basis = [vec[k, a:b] for k in range(ITERS)]
        basis.append(applied(ITERS - 1, a, b))
        weight, right = diag[own], source[own]
        gaps = [basis[k] - basis[k + 1] for k in range(ITERS)]
        scaled = [weight * gap for gap in gaps]
        for k in range(count):
            powers[k] = powers[k] + jnp.sum(basis[(k + 1) // 2] * scaled[k // 2], axis=0)
        for k in range(ITERS):
            firsts[k] = firsts[k] + jnp.sum(right * basis[k], axis=0)
        ladder, level = [basis[0], gaps[0]], gaps
        while len(level) > 1:
            level = [level[i] - level[i + 1] for i in range(len(level) - 1)]
            ladder.append(level[0])
        for k in range(2, count + 1):
            steps[k] = steps[k] + jnp.sum(weight * ladder[k // 2] * ladder[(k + 1) // 2], axis=0)
    steps[0], steps[1] = firsts[0], powers[0]
    for k in range(ITERS):
        basis_ref[k] = vec[k, HALO - 1 : HALO + chunk]

    columns = powers + firsts + steps
    rows = [jnp.sum(c, axis=0, keepdims=True) for c in columns]
    high = -(-len(rows) // 8) * 8
    rows = rows + [jnp.zeros((1, L), F32)] * (high - len(rows))
    sums = jnp.sum(jnp.concatenate(rows, axis=0), axis=1, keepdims=True)
    lane = lax.broadcasted_iota(jnp.int32, (high, LANES), 1)
    row = lax.broadcasted_iota(jnp.int32, (high, LANES), 0)
    line = jnp.sum(jnp.where(lane == row, sums, 0.0), axis=0, keepdims=True)
    sums_ref[...] = jnp.broadcast_to(line, sums_ref.shape)


def galerkin(sums):
    n, count = ITERS, 2 * ITERS - 1
    line = jnp.sum(sums, axis=0, keepdims=True)
    lane = lax.broadcasted_iota(jnp.int32, line.shape, 1)

    def pick(k):
        return jnp.sum(jnp.where(lane == k, line, 0.0), axis=1, keepdims=True)

    powers = [pick(k) for k in range(count)]
    firsts = [pick(count + k) for k in range(n)]
    steps = [pick(count + n + k) for k in range(count + 1)]
    matrix = [jnp.concatenate([powers[k], steps[k + 1]], axis=0) for k in range(count)]
    right = [jnp.concatenate([firsts[k], steps[k]], axis=0) for k in range(n)]
    low = [[None] * n for _ in range(n)]
    scale = [None] * n
    quality = None
    for j in range(n):
        pivot = matrix[2 * j]
        for k in range(j):
            pivot = pivot - low[j][k] * low[j][k] * scale[k][0]
        share = pivot / matrix[2 * j]
        fine = share > 1e-7
        quality = jnp.where(fine, share, 0.0) if quality is None else jnp.minimum(quality, jnp.where(fine, share, 0.0))
        inverse = jnp.where(fine, 1.0 / pivot, 0.0)
        scale[j] = (pivot, inverse)
        for r in range(j + 1, n):
            entry = matrix[r + j]
            for k in range(j):
                entry = entry - low[r][k] * low[j][k] * scale[k][0]
            low[r][j] = entry * inverse
    part = list(right)
    for r in range(n):
        for k in range(r):
            part[r] = part[r] - low[r][k] * part[k]
    part = [part[r] * scale[r][1] for r in range(n)]
    for r in reversed(range(n)):
        for k in range(r + 1, n):
            part[r] = part[r] - low[k][r] * part[k]
    first = quality[0:1] >= quality[1:2]
    by_power = [jnp.where(first, p[0:1], 0.0) for p in part]
    by_step = [jnp.where(first, 0.0, p[1:2]) for p in part]
    return by_power, by_step


def render_kernel(
    sums_ref, basis_ref, lower_ref, own_ref, slope_ref, offset_ref, gain_ref, out_ref, press, flat, turned,
    *, ngx, ngz, zl, xl, chunk, step
):
    S, L = ngx * ngz, zl * xl
    yl = S * chunk
    height = out_ref.shape[0] // S
    move = Shifts(ngx, ngz, zl, xl)
    by_power, by_step = galerkin(sums_ref[...])
    by_power = [v.reshape(1, 1, 1) for v in by_power]
    by_step = [v.reshape(1, 1, 1) for v in by_step]
    for a in range(0, chunk + 1, step):
        b = min(a + step, chunk + 1)
        level = [basis_ref[k, a:b] for k in range(ITERS)]
        value = 0.0
        for k in range(ITERS):
            value = value + by_power[k] * level[k]
        value = value + by_step[0] * level[0]
        for k in range(1, ITERS):
            level = [level[i] - level[i + 1] for i in range(len(level) - 1)]
            value = value + by_step[k] * level[0]
        press[a:b] = value
    for a in range(0, chunk, step):
        b = min(a + step, chunk)
        p = press[a + 1 : b + 1]
        fronts = (
            jnp.where(move.z_low, 0.0, move.below_z(p)),
            jnp.where(move.x_low, 0.0, move.below_x(p)),
            press[a:b],
        )
        scalar = None
        for k, front in enumerate(fronts):
            v = jnp.stack([own_ref[pl.ds(c * FIELDS + k + 1, S, stride=chunk * FIELDS), :] for c in range(a, b)])
            corrected = v - lower_ref[k, a:b] * (p - front)
            for c in range(a, b):
                out_ref[pl.ds(k * chunk + c, S, stride=height), :] = corrected[c - a]
            scalar = corrected if scalar is None else scalar + corrected
        for c in range(a, b):
            flat[pl.ds(c, S, stride=chunk), :] = scalar[c - a]
    turned[...] = flat[...].T.reshape(zl, xl, yl)

    group = ngx * chunk
    functions = slope_ref.shape[0] // ngz
    depth = zl * ngz
    lane = lax.broadcasted_iota(jnp.int32, (xl, yl), 1)

    def owned(i, carry):
        images = [jnp.zeros((xl, LANES), F32) for _ in range(ngx)]
        for t in range(functions):
            index = i * functions + t
            rates = [-LOG2E * slope_ref[index, c] for c in range(4)]
            bases = [-LOG2E * offset_ref[index, c] for c in range(4)]
            gain = gain_ref[index] / depth
            through = jnp.ones((xl, yl), F32)
            colors = [jnp.zeros((xl, yl), F32) for _ in range(3)]
            for z in range(zl):
                x = turned[z]
                curves = [1.0 / (1.0 + jnp.exp2(rates[c] * x + bases[c])) for c in range(4)]
                opacity = gain * curves[3]
                weight = through * opacity
                colors = [colors[c] + weight * curves[c] for c in range(3)]
                through = through * (1.0 - opacity)
            planes = list(colors)
            everything = through
            for _ in range(ngz - 1):
                planes = [colors[c] + through * roll(planes[c], -group, 1) for c in range(3)]
                everything = through * roll(everything, -group, 1)
            planes.append(1.0 - everything)
            for c, image in enumerate(planes):
                start = (t * 4 + c) * chunk
                here = (lane >= start) & (lane < start + chunk)
                for k in range(ngx):
                    images[k] = jnp.where(here, roll(image, start - k * chunk, 1), images[k])
        for k in range(ngx):
            place = pl.multiple_of((i * ngx + k) * height + 3 * chunk, 2)
            out_ref[pl.ds(place, xl), :] = images[k]
        return carry

    lax.fori_loop(0, ngz, owned, 0)


def unpack_kernel(in_ref, corrected_ref, images_ref, flat, *, table, chunk):
    zl, xl, yl = corrected_ref.shape[1:]
    functions = images_ref.shape[0]
    pieces = yl // chunk
    for f in range(3):
        for c in range(pieces):
            flat[c * chunk : (c + 1) * chunk, :] = in_ref[owner(table, c), f * chunk : (f + 1) * chunk, :]
        corrected_ref[f] = flat[...].T.reshape(zl, xl, yl)
    lane = lax.broadcasted_iota(jnp.int32, (xl, yl), 1)
    images = [jnp.zeros((xl, yl), F32) for _ in range(functions * 4)]
    for c in range(pieces):
        source = in_ref[owner(table, c), 3 * chunk : 3 * chunk + xl, :]
        here = (lane >= c * chunk) & (lane < (c + 1) * chunk)
        images = [jnp.where(here, roll(source, (c - k) * chunk, 1), image) for k, image in enumerate(images)]
    for k, image in enumerate(images):
        images_ref[k // 4, k % 4] = image


def solution(mesh):
    ngx, ngy, ngz = mesh.shape["gx"], mesh.shape["gy"], mesh.shape["gz"]
    S, devices = ngx * ngz, ngx * ngy * ngz
    table = [z * ngx + x for x, z in snake(ngx, ngz)]

    def local(phase_field, thermal, velocity, transfer_slope, transfer_offset, transfer_gain):
        zl, xl, yl = thermal.shape
        L, chunk = zl * xl, yl // S
        functions = transfer_slope.shape[0] // ngz
        assert yl % S == 0 and L == LANES and yl == LANES and functions * 4 * chunk <= LANES
        hops = -(-HALO // chunk)
        margin = min(chunk, HALO + HALO % 2)
        step = max(1, 4 * 8 // S)

        def call(body, out, scratch=(), **kwargs):
            return pl.pallas_call(
                lambda *refs: body(*refs, **kwargs),
                out_shape=out,
                scratch_shapes=[pltpu.VMEM(s, F32) for s in scratch],
                name=body.__name__,
            )

        def shaped(*shape):
            return jax.ShapeDtypeStruct(shape, F32)

        blocks = call(pack_kernel, shaped(S, chunk * FIELDS, L), table=table, chunk=chunk)(phase_field, thermal, velocity)
        pencils = lax.all_to_all(blocks, ("gz", "gx"), 0, 0, tiled=True)
        first = pencils[:, : margin * FIELDS]
        last = pencils[:, (chunk - margin) * FIELDS :]
        every = ("gx", "gy", "gz")
        pairs = [chain_pairs(ngx, ngy, ngz, hop + 1) for hop in range(hops)]
        lows = [lax.ppermute(last, every, p) for p in pairs]
        highs = [lax.ppermute(first, every, [(b, a) for a, b in p]) for p in pairs]
        own = pencils.reshape(-1, L)
        wide = chunk + 2 * HALO
        basis, lower, sums = call(
            krylov_kernel,
            (shaped(ITERS, chunk + 1, S, L), shaped(3, chunk, S, L), shaped(devices, LANES)),
            ((wide, S, L), (6, wide, S, L), (ITERS, wide, S, L), (chunk, S, L), (chunk, S, L)),
            ngx=ngx, ngz=ngz, zl=zl, xl=xl, chunk=chunk, hops=hops, margin=margin, step=step,
        )(own, *[v.reshape(-1, L) for v in lows + highs])
        sums = lax.all_to_all(sums, every, 0, 0, tiled=True)
        height = 3 * chunk + xl
        height += -height % 8
        smem = pl.BlockSpec(memory_space=pltpu.SMEM)
        vmem = pl.BlockSpec(memory_space=pltpu.VMEM)
        kwargs = dict(ngx=ngx, ngz=ngz, zl=zl, xl=xl, chunk=chunk, step=step)
        packed = pl.pallas_call(
            lambda *refs: render_kernel(*refs, **kwargs),
            out_shape=shaped(S * height, LANES),
            in_specs=[vmem] * 4 + [smem] * 3,
            scratch_shapes=[pltpu.VMEM(s, F32) for s in ((chunk + 1, S, L), (yl, L), (zl, xl, yl))],
            name="render_kernel",
        )(sums, basis, lower, own, transfer_slope, transfer_offset, transfer_gain)
        home = lax.all_to_all(packed.reshape(S, height, LANES), ("gz", "gx"), 0, 0, tiled=True)
        return call(
            unpack_kernel,
            (shaped(3, zl, xl, yl), shaped(functions, 4, xl, yl)),
            ((yl, L),),
            table=table, chunk=chunk,
        )(home)

    return jax.shard_map(
        local,
        mesh=mesh,
        in_specs=(P("gz", "gx", "gy"), P("gz", "gx", "gy"), P(None, "gz", "gx", "gy"), P(), P(), P()),
        out_specs=(P(None, "gz", "gx", "gy"), P("gz", None, "gx", "gy")),
        check_vma=False,
    )
```

time: 453 us -> 55.3 us (0.12)
  blocking collectives: 163 us -> 21.9 us
  waiting for transfers between devices: 99.9 us -> 6.63 us
  other arithmetic: 60.1 us -> 0 us
  starting transfers between devices: 57.5 us -> 12.5 us
  between operations: 28.3 us -> 0.7 us
  loops' own time: 21.2 us -> 0 us
  local copies, waits for them, and re-layouts: 21.1 us -> 2.6 us
  Pallas kernels: 0 us -> 10.5 us
    psum x4 -> x0, blocking collectives: 156 us -> none  [joined_sums(): lax.psum((jnp.sum(resid * cond), jnp.sum(mapped * cond)), ('gz', 'gx', 'g...]
    ppermute x30 -> x2, waiting for transfers between devices: 80.6 us -> 0.9 us  [the longest x1 0.9 us: local(): lows = [lax.ppermute(last, every, p) for p in pairs]]
    ppermute x30 -> x2, starting transfers between devices: 57.4 us -> 4.33 us  [the longest x1 3.04 us: local(): lows = [lax.ppermute(last, every, p) for p in pairs]]
    reduce_sum x13 -> x0, other arithmetic: 45.1 us -> none  [the longest x8 41.5 us: render(): jnp.sum(weight * jax.nn.sigmoid(slope[channel] * scalar + offset[channel]...]
    all_to_all x0 -> x2, blocking collectives: none -> 21.9 us  [the longest x1 11.5 us: local(): pencils = lax.all_to_all(blocks, ('gz', 'gx'), 0, 0, tiled=True)]
    another operation x2 -> x0, loops' own time: 21.2 us -> none  [the longest x1 21.1 us: local(): colors, through = lax.map(render, jnp.arange(transfer_slope.shape[0]))]
    reduce_scatter x1 -> x0, waiting for transfers between devices: 19.3 us -> none  [local(): images = lax.psum_scatter(terms, 'gz', scatter_dimension=0, tiled=True)]
    another operation x10 -> x0, other arithmetic: 11.3 us -> none  [the longest x8 10.6 us: render(): inclusive = jnp.cumprod(keep, axis=0)]
  transfers between devices with their start and end apart: 31 -> 3, of which waited for: 22 -> 2; matrix products, arithmetic and copies ran while one was open for 0% -> 2% of each run, Pallas kernels for 0% -> 0%
where the time goes in v1:
time: 55.3 us; the launch traced here: 54.8 us
  blocking collectives  21.9 us (40%)
  starting transfers between devices  12.5 us (23%)
  Pallas kernels  10.5 us (19%)
  waiting for transfers between devices  6.63 us (12%)
  local copies, waits for them, and re-layouts  2.6 us (5%)
  between operations  0.7 us (1%)
    all_to_all x1, blocking collectives, local(): pencils = lax.all_to_all(blocks, ('gz', 'gx'), 0, 0, tiled=True)  11.5 us
    all_to_all x1, blocking collectives, local(): lax.all_to_all(packed.reshape(S, height, LANES), ('gz', 'gx'), 0, 0, tile...  10.4 us
    all_to_all x1, starting transfers between devices, local(): sums = lax.all_to_all(sums, every, 0, 0, tiled=True)  8.16 us
    all_to_all x1, waiting for transfers between devices, local(): sums = lax.all_to_all(sums, every, 0, 0, tiled=True)  5.73 us
    pallas_call x1, Pallas kernels, local(): pl.pallas_call(lambda *refs: render_kernel(*refs, **kwargs), out_shape=sh...  4.28 us
    ppermute x1, starting transfers between devices, local(): lows = [lax.ppermute(last, every, p) for p in pairs]  3.04 us
    unnamed x14, local copies, waits for them, and re-layouts  2.59 us
    pallas_call x1, Pallas kernels, local(): call(krylov_kernel, (shaped(ITERS, chunk + 1, S, L), shaped(3, chunk, S,...  2.53 us
  transfers between devices with their start and end apart: 3, of which 2 were waited for; matrix products, arithmetic and copies ran while one was open for 2% of the time, Pallas kernels for 0%

profile of v1, /device:TPU:0, one launch (start us, length us, event | category | flops | bytes accessed | tf_op | source)
XLA Modules:
  0.0 54.8 jit_solution(16258488648844137841)
XLA Ops:
  0.6 1.8 %pack_kernel.1 = f32[8,64,128]{2,1,0:T(8,128)} custom-call(s32[8,16,128]{2,1,0:T(8,128)} %refs_0_.1, f32[8,16,128]{2,1,0:T(8,128)} %refs_1_.1, f32[3,8,16,128]{3,2,1,0:T(8,128)} %refs_2_.1), custom_call_target="tpu_custom_call" | custom-call | tf_op jit(solution)/shard_map/pack_kernel/pallas_call | solution.py:359
  2.5 11.5 %all_to_all.21 = f32[8,64,128]{2,1,0:T(8,128)S(1)} all-to-all(f32[8,64,128]{2,1,0:T(8,128)} %pack_kernel.1), channel_id=1, replica_groups=mesh['gx'=2,'gy'=4,'gz'=4] {'gz','gx'}, dimensions={0} | all-to-all | bytes 524288 | tf_op jit(solution)/shard_map/all_to_all | solution.py:360
  14.0 0.0 copy-start
  14.0 1.3 %collective-permute-start.1 = (f32[8,24,128]{2,1,0:T(8,128)S(1)}, f32[8,24,128]{2,1,0:T(8,128)S(1)}, u32[]{:S(2)}, u32[]{:S(2)}) collective-permute-start(f32[8,24,128]{2,1,0:T(8,128)S(1)} %get-tuple-element.8), channel_id=1, source_target_pairs={{1,0},{2,1},{3,2},{19,3},{18,19},{17,18},{16,17},{20,16},{21,20},{... | collective-permute-start | bytes 294920 | tf_op jit(solution)/shard_map/ppermute | solution.py:366
  15.3 3.0 %collective-permute-start = (f32[8,24,128]{2,1,0:T(8,128)S(1)}, f32[8,24,128]{2,1,0:T(8,128)S(1)}, u32[]{:S(2)}, u32[]{:S(2)}) collective-permute-start(f32[8,24,128]{2,1,0:T(8,128)S(1)} %get-tuple-element.9), channel_id=1, source_target_pairs={{0,1},{1,2},{2,3},{3,19},{19,18},{18,17},{17,16},{16,20},{20,21},{... | collective-permute-start | bytes 294920 | tf_op jit(solution)/shard_map/ppermute | solution.py:365
  18.4 0.0 collective-permute-done.1
  18.4 0.0 copy-start.1
  18.4 0.9 %collective-permute-done = f32[8,24,128]{2,1,0:T(8,128)S(1)} collective-permute-done((f32[8,24,128]{2,1,0:T(8,128)S(1)}, f32[8,24,128]{2,1,0:T(8,128)S(1)}, u32[]{:S(2)}, u32[]{:S(2)}) %collective-permute-start) | collective-permute-done | bytes 98336 | tf_op jit(solution)/shard_map/ppermute | solution.py:365
  19.3 0.0 copy-start.2
  19.3 0.0 copy-done
  19.3 0.0 copy-done.1
  19.3 0.6 %copy-done.2 = f32[8,24,128]{2,1,0:T(8,128)} copy-done((f32[8,24,128]{2,1,0:T(8,128)}, f32[8,24,128]{2,1,0:T(8,128)S(1)}, u32[]{:S(2)}) %copy-start.2) | copy-done | bytes 98328
  19.9 2.5 %krylov_kernel.1 = (f32[4,17,8,128]{3,2,1,0:T(8,128)}, f32[3,16,8,128]{3,2,1,0:T(8,128)}, f32[32,128]{1,0:T(8,128)}) custom-call(f32[512,128]{1,0:T(8,128)} %bitcast.8, f32[192,128]{1,0:T(8,128)} %bitcast.12, f32[192,128]{1,0:T(8,128)} %bitcast.11), custom_call_target="tpu_custom_call" | custom-call | tf_op jit(solution)/shard_map/krylov_kernel/pallas_call | solution.py:369
  22.4 0.0 copy-start.4
  22.4 8.2 %all-to-all-start.1 = ((f32[32,1,128]{2,1,0:T(1,128)}), f32[32,1,128]{2,1,0:T(1,128)S(1)}, u32[]{:S(2)}, u32[]{:S(2)}) async-start(f32[32,1,128]{2,1,0:T(1,128)} %bitcast.14), calls=%async_computation.1 | async-start | bytes 32768 | tf_op jit(solution)/shard_map/all_to_all | solution.py:375
  30.6 0.0 copy-done.4
  30.6 0.0 copy-start.5
  30.6 0.7 %copy.11.refs_4_ = f32[8,4]{1,0:T(8,128)} copy(f32[8,4]{0,1:T(4,128)S(1)} %copy-done.4) | data formatting | bytes 256 | tf_op args[3]
  31.3 0.0 copy-done.5
  31.3 0.7 %copy.12.refs_5_ = f32[8,4]{1,0:T(8,128)} copy(f32[8,4]{0,1:T(4,128)S(1)} %copy-done.5) | data formatting | bytes 256 | tf_op args[4]
  32.0 5.7 %all-to-all-done.1 = f32[32,1,128]{2,1,0:T(1,128)S(1)} async-done(((f32[32,1,128]{2,1,0:T(1,128)}), f32[32,1,128]{2,1,0:T(1,128)S(1)}, u32[]{:S(2)}, u32[]{:S(2)}) %all-to-all-start.1) | async-done | bytes 16416 | tf_op jit(solution)/shard_map/all_to_all | solution.py:375
  37.7 0.0 copy-start.3
  37.7 0.6 %copy-done.3 = f32[32,1,128]{2,1,0:T(1,128)} copy-done((f32[32,1,128]{2,1,0:T(1,128)}, f32[32,1,128]{2,1,0:T(1,128)S(1)}, u32[]{:S(2)}) %copy-start.3) | copy-done | bytes 16408
  38.3 4.3 %render_kernel.1 = f32[512,128]{1,0:T(8,128)} custom-call(f32[32,128]{1,0:T(8,128)} %bitcast.13, f32[4,17,8,128]{3,2,1,0:T(8,128)} %get-tuple-element.6.refs_1_, f32[3,16,8,128]{3,2,1,0:T(8,128)} %get-tuple-element.7.refs_2_, f32[512,128]{1,0:T(8,128)} %bitcast.9, f32[8,4]{1,0:T(8,128)} %copy.11.refs_4_, f32[8,4]{1,0:T(8,128)} %copy.12.refs_5_, f32[8]{0:T(128)} %refs_6_.1), custom_call_target="tpu_custom_call" | custom-call | tf_op jit(solution)/shard_map/render_kernel/pallas_call | solution.py:381
  42.6 10.4 %all_to_all.22.refs_0_ = f32[8,64,128]{2,1,0:T(8,128)} all-to-all(f32[8,64,128]{2,1,0:T(8,128)} %bitcast.10), channel_id=1, replica_groups=mesh['gx'=2,'gy'=4,'gz'=4] {'gz','gx'}, dimensions={0} | all-to-all | bytes 524288 | tf_op jit(solution)/shard_map/all_to_all | solution.py:388
  52.9 1.8 %unpack_kernel.1 = (f32[3,8,16,128]{3,2,1,0:T(8,128)}, f32[2,4,16,128]{3,2,1,0:T(8,128)}) custom-call(f32[8,64,128]{2,1,0:T(8,128)} %all_to_all.22.refs_0_), custom_call_target="tpu_custom_call" | custom-call | tf_op jit(solution)/shard_map/unpack_kernel/pallas_call | solution.py:389
  (1 shorter events, 0.0 us)
Async XLA Ops:
  14.0 5.3 %copy-start = (f32[8,64,128]{2,1,0:T(8,128)}, f32[8,64,128]{2,1,0:T(8,128)S(1)}, u32[]{:S(2)}) copy-start(f32[8,64,128]{2,1,0:T(8,128)S(1)} %all_to_all.21) | copy-start | bytes 786436
  14.0 4.3 %collective-permute-start.1 = (f32[8,24,128]{2,1,0:T(8,128)S(1)}, f32[8,24,128]{2,1,0:T(8,128)S(1)}, u32[]{:S(2)}, u32[]{:S(2)}) collective-permute-start(f32[8,24,128]{2,1,0:T(8,128)S(1)} %get-tuple-element.8), channel_id=1, source_target_pairs={{1,0},{2,1},{3,2},{19,3},{18,19},{17,18},{16,17},{20,16},{21,20},{... | collective-permute-start | bytes 294920 | tf_op jit(solution)/shard_map/ppermute | solution.py:366
  15.3 4.0 %collective-permute-start = (f32[8,24,128]{2,1,0:T(8,128)S(1)}, f32[8,24,128]{2,1,0:T(8,128)S(1)}, u32[]{:S(2)}, u32[]{:S(2)}) collective-permute-start(f32[8,24,128]{2,1,0:T(8,128)S(1)} %get-tuple-element.9), channel_id=1, source_target_pairs={{0,1},{1,2},{2,3},{3,19},{19,18},{18,17},{17,16},{16,20},{20,21},{... | collective-permute-start | bytes 294920 | tf_op jit(solution)/shard_map/ppermute | solution.py:365
  18.4 0.9 %copy-start.1 = (f32[8,24,128]{2,1,0:T(8,128)}, f32[8,24,128]{2,1,0:T(8,128)S(1)}, u32[]{:S(2)}) copy-start(f32[8,24,128]{2,1,0:T(8,128)S(1)} %collective-permute-done.1) | copy-start | bytes 294916
  19.3 0.6 %copy-start.2 = (f32[8,24,128]{2,1,0:T(8,128)}, f32[8,24,128]{2,1,0:T(8,128)S(1)}, u32[]{:S(2)}) copy-start(f32[8,24,128]{2,1,0:T(8,128)S(1)} %collective-permute-done) | copy-start | bytes 294916
  22.4 8.2 %copy-start.4 = (f32[8,4]{0,1:T(4,128)S(1)}, f32[8,4]{0,1:T(4,128)}, u32[]{:S(2)}) copy-start(f32[8,4]{0,1:T(4,128)} %param.9) | copy-start | bytes 388
  22.4 15.3 %all-to-all-start.1 = ((f32[32,1,128]{2,1,0:T(1,128)}), f32[32,1,128]{2,1,0:T(1,128)S(1)}, u32[]{:S(2)}, u32[]{:S(2)}) async-start(f32[32,1,128]{2,1,0:T(1,128)} %bitcast.14), calls=%async_computation.1 | async-start | bytes 32768 | tf_op jit(solution)/shard_map/all_to_all | solution.py:375
  30.6 0.7 %copy-start.5 = (f32[8,4]{0,1:T(4,128)S(1)}, f32[8,4]{0,1:T(4,128)}, u32[]{:S(2)}) copy-start(f32[8,4]{0,1:T(4,128)} %param.10) | copy-start | bytes 388
  37.7 0.6 %copy-start.3 = (f32[32,1,128]{2,1,0:T(1,128)}, f32[32,1,128]{2,1,0:T(1,128)S(1)}, u32[]{:S(2)}) copy-start(f32[32,1,128]{2,1,0:T(1,128)S(1)} %all-to-all-done.1) | copy-start | bytes 49156

commit v2 on v1

--- a/solution.py
+++ b/solution.py
@@ -345,18 +345,36 @@
         margin = min(chunk, HALO + HALO % 2)
         step = max(1, 4 * 8 // S)
 
-        def call(body, out, scratch=(), **kwargs):
-            return pl.pallas_call(
+        vmem, smem = (pl.BlockSpec(memory_space=space) for space in (pltpu.VMEM, pltpu.SMEM))
+
+        def call(body, specs, out, scratch=(), **kwargs):
+            kernel = pl.pallas_call(
                 lambda *refs: body(*refs, **kwargs),
+                in_specs=specs,
+                out_specs=jax.tree.map(lambda _: vmem, out),
                 out_shape=out,
                 scratch_shapes=[pltpu.VMEM(s, F32) for s in scratch],
                 name=body.__name__,
             )
 
+            def run(*args):
+                return kernel(*[near(a) if spec is vmem else a for a, spec in zip(args, specs)])
+
+            return run
+
+        def near(array):
+            return pltpu.with_memory_space_constraint(array, pltpu.VMEM)
+
         def shaped(*shape):
             return jax.ShapeDtypeStruct(shape, F32)
 
-        blocks = call(pack_kernel, shaped(S, chunk * FIELDS, L), table=table, chunk=chunk)(phase_field, thermal, velocity)
+        def placed(*shape):
+            return pltpu.VMEM(shape, F32)
+
+        free = pl.BlockSpec()
+        blocks = call(pack_kernel, [free] * 3, placed(S, chunk * FIELDS, L), table=table, chunk=chunk)(
+            phase_field, thermal, velocity
+        )
         pencils = lax.all_to_all(blocks, ("gz", "gx"), 0, 0, tiled=True)
         first = pencils[:, : margin * FIELDS]
         last = pencils[:, (chunk - margin) * FIELDS :]
@@ -368,26 +386,25 @@
         wide = chunk + 2 * HALO
         basis, lower, sums = call(
             krylov_kernel,
-            (shaped(ITERS, chunk + 1, S, L), shaped(3, chunk, S, L), shaped(devices, LANES)),
+            [vmem] * (1 + 2 * hops),
+            (placed(ITERS, chunk + 1, S, L), placed(3, chunk, S, L), placed(devices, LANES)),
             ((wide, S, L), (6, wide, S, L), (ITERS, wide, S, L), (chunk, S, L), (chunk, S, L)),
             ngx=ngx, ngz=ngz, zl=zl, xl=xl, chunk=chunk, hops=hops, margin=margin, step=step,
         )(own, *[v.reshape(-1, L) for v in lows + highs])
         sums = lax.all_to_all(sums, every, 0, 0, tiled=True)
         height = 3 * chunk + xl
         height += -height % 8
-        smem = pl.BlockSpec(memory_space=pltpu.SMEM)
-        vmem = pl.BlockSpec(memory_space=pltpu.VMEM)
-        kwargs = dict(ngx=ngx, ngz=ngz, zl=zl, xl=xl, chunk=chunk, step=step)
-        packed = pl.pallas_call(
-            lambda *refs: render_kernel(*refs, **kwargs),
-            out_shape=shaped(S * height, LANES),
-            in_specs=[vmem] * 4 + [smem] * 3,
-            scratch_shapes=[pltpu.VMEM(s, F32) for s in ((chunk + 1, S, L), (yl, L), (zl, xl, yl))],
-            name="render_kernel",
+        packed = call(
+            render_kernel,
+            [vmem] * 4 + [smem] * 3,
+            placed(S * height, LANES),
+            ((chunk + 1, S, L), (yl, L), (zl, xl, yl)),
+            ngx=ngx, ngz=ngz, zl=zl, xl=xl, chunk=chunk, step=step,
         )(sums, basis, lower, own, transfer_slope, transfer_offset, transfer_gain)
         home = lax.all_to_all(packed.reshape(S, height, LANES), ("gz", "gx"), 0, 0, tiled=True)
         return call(
             unpack_kernel,
+            [vmem],
             (shaped(3, zl, xl, yl), shaped(functions, 4, xl, yl)),
             ((yl, L),),
             table=table, chunk=chunk,

time: 55.3 us -> 48.4 us (0.88)
  Pallas kernels: 10.5 us -> 6.75 us
  blocking collectives: 21.9 us -> 20.1 us
  local copies, waits for them, and re-layouts: 2.6 us -> 1.36 us
    pallas_call x4, Pallas kernels: 10.5 us -> 6.75 us  [run(): kernel(*[near(a) if spec is vmem else a for a, spec in zip(args, specs)])]
    all_to_all x1, blocking collectives: 10.4 us -> 8.74 us  [local(): lax.all_to_all(packed.reshape(S, height, LANES), ('gz', 'gx'), 0, 0, tile...]
    unnamed x14 -> x6, local copies, waits for them, and re-layouts: 2.59 us -> 1.35 us
  transfers between devices with their start and end apart: 3 -> 3, of which waited for: 2 -> 2; matrix products, arithmetic and copies ran while one was open for 2% -> 3% of each run, Pallas kernels for 0% -> 0%
where the time goes in v2:
time: 48.4 us; the launch traced here: 48 us
  blocking collectives  20.1 us (42%)
  starting transfers between devices  12.5 us (26%)
  Pallas kernels  6.75 us (14%)
  waiting for transfers between devices  6.65 us (14%)
  local copies, waits for them, and re-layouts  1.36 us (3%)
  between operations  0.7 us (1%)
    all_to_all x1, blocking collectives, local(): pencils = lax.all_to_all(blocks, ('gz', 'gx'), 0, 0, tiled=True)  11.3 us
    all_to_all x1, blocking collectives, local(): lax.all_to_all(packed.reshape(S, height, LANES), ('gz', 'gx'), 0, 0, tile...  8.74 us
    all_to_all x1, starting transfers between devices, local(): sums = lax.all_to_all(sums, every, 0, 0, tiled=True)  8.16 us
    pallas_call x4, Pallas kernels, run(): kernel(*[near(a) if spec is vmem else a for a, spec in zip(args, specs)])  6.75 us
    all_to_all x1, waiting for transfers between devices, local(): sums = lax.all_to_all(sums, every, 0, 0, tiled=True)  5.74 us
    ppermute x1, starting transfers between devices, local(): lows = [lax.ppermute(last, every, p) for p in pairs]  3.04 us
    unnamed x6, local copies, waits for them, and re-layouts  1.35 us
    ppermute x1, starting transfers between devices, local(): highs = [lax.ppermute(first, every, [(b, a) for a, b in p]) for p in pairs]  1.29 us
  transfers between devices with their start and end apart: 3, of which 2 were waited for; matrix products, arithmetic and copies ran while one was open for 3% of the time, Pallas kernels for 0%

profile of v2, /device:TPU:0, one launch (start us, length us, event | category | flops | bytes accessed | tf_op | source)
XLA Modules:
  0.0 48.0 jit_solution(14125139789118530547)
XLA Ops:
  0.6 1.1 %pack_kernel.1 = f32[8,64,128]{2,1,0:T(8,128)S(1)} custom-call(s32[8,16,128]{2,1,0:T(8,128)} %refs_0_.1, f32[8,16,128]{2,1,0:T(8,128)} %refs_1_.1, f32[3,8,16,128]{3,2,1,0:T(8,128)} %refs_2_.1), custom_call_target="tpu_custom_call" | custom-call | tf_op jit(solution)/shard_map/pack_kernel/pallas_call | solution.py:361
  1.8 11.3 %all_to_all.21 = f32[8,64,128]{2,1,0:T(8,128)S(1)} all-to-all(f32[8,64,128]{2,1,0:T(8,128)S(1)} %pack_kernel.1), channel_id=1, replica_groups=mesh['gx'=2,'gy'=4,'gz'=4] {'gz','gx'}, dimensions={0} | all-to-all | bytes 524288 | tf_op jit(solution)/shard_map/all_to_all | solution.py:378
  13.1 1.3 %collective-permute-start.1 = (f32[8,24,128]{2,1,0:T(8,128)S(1)}, f32[8,24,128]{2,1,0:T(8,128)S(1)}, u32[]{:S(2)}, u32[]{:S(2)}) collective-permute-start(f32[8,24,128]{2,1,0:T(8,128)S(1)} %get-tuple-element.8), channel_id=1, source_target_pairs={{1,0},{2,1},{3,2},{19,3},{18,19},{17,18},{16,17},{20,16},{21,20},{... | collective-permute-start | bytes 294920 | tf_op jit(solution)/shard_map/ppermute | solution.py:384
  14.4 3.0 %collective-permute-start = (f32[8,24,128]{2,1,0:T(8,128)S(1)}, f32[8,24,128]{2,1,0:T(8,128)S(1)}, u32[]{:S(2)}, u32[]{:S(2)}) collective-permute-start(f32[8,24,128]{2,1,0:T(8,128)S(1)} %get-tuple-element.9), channel_id=1, source_target_pairs={{0,1},{1,2},{2,3},{3,19},{19,18},{18,17},{17,16},{16,20},{20,21},{... | collective-permute-start | bytes 294920 | tf_op jit(solution)/shard_map/ppermute | solution.py:383
  17.5 0.0 collective-permute-done.1
  17.5 0.9 %collective-permute-done = f32[8,24,128]{2,1,0:T(8,128)S(1)} collective-permute-done((f32[8,24,128]{2,1,0:T(8,128)S(1)}, f32[8,24,128]{2,1,0:T(8,128)S(1)}, u32[]{:S(2)}, u32[]{:S(2)}) %collective-permute-start) | collective-permute-done | bytes 98336 | tf_op jit(solution)/shard_map/ppermute | solution.py:383
  18.4 1.5 %krylov_kernel.1 = (f32[4,17,8,128]{3,2,1,0:T(8,128)S(1)}, f32[3,16,8,128]{3,2,1,0:T(8,128)S(1)}, f32[32,128]{1,0:T(8,128)}) custom-call(f32[512,128]{1,0:T(8,128)S(1)} %bitcast.8, f32[192,128]{1,0:T(8,128)S(1)} %bitcast.12, f32[192,128]{1,0:T(8,128)S(1)} %bitcast.11), custom_call_target="tpu_custom_call" | custom-call | tf_op jit(solution)/shard_map/krylov_kernel/pallas_call | solution.py:361
  19.9 0.0 copy-start
  19.9 8.2 %all-to-all-start.1 = ((f32[32,1,128]{2,1,0:T(1,128)}), f32[32,1,128]{2,1,0:T(1,128)S(1)}, u32[]{:S(2)}, u32[]{:S(2)}) async-start(f32[32,1,128]{2,1,0:T(1,128)} %bitcast.4), calls=%async_computation.1 | async-start | bytes 32768 | tf_op jit(solution)/shard_map/all_to_all | solution.py:394
  28.1 0.0 copy-done
  28.1 0.0 copy-start.1
  28.1 0.7 %copy.11.refs_4_ = f32[8,4]{1,0:T(8,128)} copy(f32[8,4]{0,1:T(4,128)S(1)} %copy-done) | data formatting | bytes 256 | tf_op args[3]
  28.8 0.0 copy-done.1
  28.8 0.7 %copy.12.refs_5_ = f32[8,4]{1,0:T(8,128)} copy(f32[8,4]{0,1:T(4,128)S(1)} %copy-done.1) | data formatting | bytes 256 | tf_op args[4]
  29.4 5.7 %all-to-all-done.1 = f32[32,1,128]{2,1,0:T(1,128)S(1)} async-done(((f32[32,1,128]{2,1,0:T(1,128)}), f32[32,1,128]{2,1,0:T(1,128)S(1)}, u32[]{:S(2)}, u32[]{:S(2)}) %all-to-all-start.1) | async-done | bytes 16416 | tf_op jit(solution)/shard_map/all_to_all | solution.py:394
  35.2 3.2 %render_kernel.1 = f32[512,128]{1,0:T(8,128)S(1)} custom-call(f32[32,128]{1,0:T(8,128)S(1)} %bitcast.13, f32[4,17,8,128]{3,2,1,0:T(8,128)S(1)} %get-tuple-element.6.refs_1_, f32[3,16,8,128]{3,2,1,0:T(8,128)S(1)} %get-tuple-element.7.refs_2_, f32[512,128]{1,0:T(8,128)S(1)} %bitcast.9, f32[8,4]{1,0:T(8,128)} %copy.11.refs_4_, f32[8,4]{1,0:T(8,128)} %copy.12.refs_5_, ...), custom_call_target="tpu_custom_call" | custom-call | tf_op jit(solution)/shard_map/render_kernel/pallas_call | solution.py:361
  38.4 8.7 %all_to_all.22.refs_0_ = f32[8,64,128]{2,1,0:T(8,128)S(1)} all-to-all(f32[8,64,128]{2,1,0:T(8,128)S(1)} %bitcast.10), channel_id=1, replica_groups=mesh['gx'=2,'gy'=4,'gz'=4] {'gz','gx'}, dimensions={0} | all-to-all | bytes 524288 | tf_op jit(solution)/shard_map/all_to_all | solution.py:404
  47.1 0.9 %unpack_kernel.1 = (f32[3,8,16,128]{3,2,1,0:T(8,128)}, f32[2,4,16,128]{3,2,1,0:T(8,128)}) custom-call(f32[8,64,128]{2,1,0:T(8,128)S(1)} %all_to_all.22.refs_0_), custom_call_target="tpu_custom_call" | custom-call | tf_op jit(solution)/shard_map/unpack_kernel/pallas_call | solution.py:361
  (1 shorter events, 0.0 us)
Async XLA Ops:
  13.1 4.3 %collective-permute-start.1 = (f32[8,24,128]{2,1,0:T(8,128)S(1)}, f32[8,24,128]{2,1,0:T(8,128)S(1)}, u32[]{:S(2)}, u32[]{:S(2)}) collective-permute-start(f32[8,24,128]{2,1,0:T(8,128)S(1)} %get-tuple-element.8), channel_id=1, source_target_pairs={{1,0},{2,1},{3,2},{19,3},{18,19},{17,18},{16,17},{20,16},{21,20},{... | collective-permute-start | bytes 294920 | tf_op jit(solution)/shard_map/ppermute | solution.py:384
  14.4 4.0 %collective-permute-start = (f32[8,24,128]{2,1,0:T(8,128)S(1)}, f32[8,24,128]{2,1,0:T(8,128)S(1)}, u32[]{:S(2)}, u32[]{:S(2)}) collective-permute-start(f32[8,24,128]{2,1,0:T(8,128)S(1)} %get-tuple-element.9), channel_id=1, source_target_pairs={{0,1},{1,2},{2,3},{3,19},{19,18},{18,17},{17,16},{16,20},{20,21},{... | collective-permute-start | bytes 294920 | tf_op jit(solution)/shard_map/ppermute | solution.py:383
  19.9 8.2 %copy-start = (f32[8,4]{0,1:T(4,128)S(1)}, f32[8,4]{0,1:T(4,128)}, u32[]{:S(2)}) copy-start(f32[8,4]{0,1:T(4,128)} %param.9) | copy-start | bytes 388
  19.9 15.3 %all-to-all-start.1 = ((f32[32,1,128]{2,1,0:T(1,128)}), f32[32,1,128]{2,1,0:T(1,128)S(1)}, u32[]{:S(2)}, u32[]{:S(2)}) async-start(f32[32,1,128]{2,1,0:T(1,128)} %bitcast.4), calls=%async_computation.1 | async-start | bytes 32768 | tf_op jit(solution)/shard_map/all_to_all | solution.py:394
  28.1 0.7 %copy-start.1 = (f32[8,4]{0,1:T(4,128)S(1)}, f32[8,4]{0,1:T(4,128)}, u32[]{:S(2)}) copy-start(f32[8,4]{0,1:T(4,128)} %param.10) | copy-start | bytes 388

commit v3 on v2

--- a/solution.py
+++ b/solution.py
@@ -23,13 +23,22 @@
     return order
 
 
-def chain_pairs(ngx, ngy, ngz, hop):
+def chain_swaps(ngx, ngy, ngz, hop, odd):
     places = []
     order = snake(ngx, ngz)
     for y in range(ngy):
         for x, z in order if y % 2 == 0 else order[::-1]:
             places.append((x * ngy + y) * ngz + z)
-    return list(zip(places[:-hop], places[hop:]))
+    firsts = [i for i in range(len(places) - hop) if i // hop % 2 == odd]
+    pairs = [(places[i], places[i + hop]) for i in firsts]
+    return pairs + [(b, a) for a, b in pairs]
+
+
+def chain_place(ngx, ngz):
+    x, y, z = lax.axis_index("gx"), lax.axis_index("gy"), lax.axis_index("gz")
+    within = x * ngz + jnp.where(x % 2 == 0, z, ngz - 1 - z)
+    group = ngx * ngz
+    return y * group + jnp.where(y % 2 == 0, within, group - 1 - within)
 
 
 def roll(value, shift, axis):
@@ -274,7 +283,7 @@
     turned[...] = flat[...].T.reshape(zl, xl, yl)
 
     group = ngx * chunk
-    functions = slope_ref.shape[0] // ngz
+    functions = slope_ref.shape[1] // ngz
     depth = zl * ngz
     lane = lax.broadcasted_iota(jnp.int32, (xl, yl), 1)
 
@@ -282,8 +291,8 @@
         images = [jnp.zeros((xl, LANES), F32) for _ in range(ngx)]
         for t in range(functions):
             index = i * functions + t
-            rates = [-LOG2E * slope_ref[index, c] for c in range(4)]
-            bases = [-LOG2E * offset_ref[index, c] for c in range(4)]
+            rates = [-LOG2E * slope_ref[c, index] for c in range(4)]
+            bases = [-LOG2E * offset_ref[c, index] for c in range(4)]
             gain = gain_ref[index] / depth
             through = jnp.ones((xl, yl), F32)
             colors = [jnp.zeros((xl, yl), F32) for _ in range(3)]
@@ -379,9 +388,14 @@
         first = pencils[:, : margin * FIELDS]
         last = pencils[:, (chunk - margin) * FIELDS :]
         every = ("gx", "gy", "gz")
-        pairs = [chain_pairs(ngx, ngy, ngz, hop + 1) for hop in range(hops)]
-        lows = [lax.ppermute(last, every, p) for p in pairs]
-        highs = [lax.ppermute(first, every, [(b, a) for a, b in p]) for p in pairs]
+        place = chain_place(ngx, ngz)
+        lows, highs = [], []
+        for hop in range(1, hops + 1):
+            even = place // hop % 2 == 0
+            ahead = lax.ppermute(jnp.where(even, last, first), every, chain_swaps(ngx, ngy, ngz, hop, 0))
+            behind = lax.ppermute(jnp.where(even, first, last), every, chain_swaps(ngx, ngy, ngz, hop, 1))
+            lows.append(jnp.where(even, behind, ahead))
+            highs.append(jnp.where(even, ahead, behind))
         own = pencils.reshape(-1, L)
         wide = chunk + 2 * HALO
         basis, lower, sums = call(
@@ -400,7 +414,7 @@
             placed(S * height, LANES),
             ((chunk + 1, S, L), (yl, L), (zl, xl, yl)),
             ngx=ngx, ngz=ngz, zl=zl, xl=xl, chunk=chunk, step=step,
-        )(sums, basis, lower, own, transfer_slope, transfer_offset, transfer_gain)
+        )(sums, basis, lower, own, transfer_slope.T, transfer_offset.T, transfer_gain)
         home = lax.all_to_all(packed.reshape(S, height, LANES), ("gz", "gx"), 0, 0, tiled=True)
         return call(
             unpack_kernel,

time: 48.4 us -> 46.2 us (0.955)
  starting transfers between devices: 12.5 us -> 6.03 us
  blocking collectives: 20.1 us -> 25.5 us
  local copies, waits for them, and re-layouts: 1.36 us -> 0 us
    all_to_all x1, blocking collectives: 11.3 us -> 16.7 us  [local(): sums = lax.all_to_all(sums, every, 0, 0, tiled=True)]
    ppermute x2, starting transfers between devices: 4.33 us -> 0.84 us  [the longest x1 0.65 us: local(): lax.ppermute(jnp.where(even, first, last), every, chain_swaps(ngx, ngy, n...]
    all_to_all x1, starting transfers between devices: 8.16 us -> 5.2 us  [local(): pencils = lax.all_to_all(blocks, ('gz', 'gx'), 0, 0, tiled=True)]
    unnamed x6 -> x0, local copies, waits for them, and re-layouts: 1.35 us -> none
    all_to_all x1, waiting for transfers between devices: 5.74 us -> 6.33 us  [local(): pencils = lax.all_to_all(blocks, ('gz', 'gx'), 0, 0, tiled=True)]
  transfers between devices with their start and end apart: 3 -> 3, of which waited for: 2 -> 2; matrix products, arithmetic and copies ran while one was open for 3% -> 0% of each run, Pallas kernels for 0% -> 0%
where the time goes in v3:
time: 46.2 us; the launch traced here: 45.8 us
  blocking collectives  25.5 us (55%)
  waiting for transfers between devices  6.85 us (15%)
  Pallas kernels  6.78 us (15%)
  starting transfers between devices  6.03 us (13%)
  between operations  0.66 us (1%)
    all_to_all x1, blocking collectives, local(): sums = lax.all_to_all(sums, every, 0, 0, tiled=True)  16.7 us
    all_to_all x1, blocking collectives, local(): lax.all_to_all(packed.reshape(S, height, LANES), ('gz', 'gx'), 0, 0, tile...  8.74 us
    pallas_call x4, Pallas kernels, run(): kernel(*[near(a) if spec is vmem else a for a, spec in zip(args, specs)])  6.78 us
    all_to_all x1, waiting for transfers between devices, local(): pencils = lax.all_to_all(blocks, ('gz', 'gx'), 0, 0, tiled=True)  6.33 us
    all_to_all x1, starting transfers between devices, local(): pencils = lax.all_to_all(blocks, ('gz', 'gx'), 0, 0, tiled=True)  5.2 us
  transfers between devices with their start and end apart: 3, of which 2 were waited for; matrix products, arithmetic and copies ran while one was open for 0% of the time, Pallas kernels for 0%

profile of v3, /device:TPU:0, one launch (start us, length us, event | category | flops | bytes accessed | tf_op | source)
XLA Modules:
  0.0 45.8 jit_solution(5785378614176912355)
XLA Ops:
  0.6 1.8 %pack_kernel.1 = f32[8,64,128]{2,1,0:T(8,128)} custom-call(s32[8,16,128]{2,1,0:T(8,128)} %refs_0_.1, f32[8,16,128]{2,1,0:T(8,128)} %refs_1_.1, f32[3,8,16,128]{3,2,1,0:T(8,128)} %refs_2_.1), custom_call_target="tpu_custom_call" | custom-call | tf_op jit(solution)/shard_map/pack_kernel/pallas_call | solution.py:370
  2.5 5.2 %all-to-all-start = ((f32[8,64,128]{2,1,0:T(8,128)}), f32[8,64,128]{2,1,0:T(8,128)S(1)}, u32[]{:S(2)}, u32[]{:S(2)}) async-start(f32[8,64,128]{2,1,0:T(8,128)} %pack_kernel.1), calls=%async_computation | async-start | bytes 524288 | tf_op jit(solution)/shard_map/all_to_all | solution.py:387
  7.7 6.3 %all-to-all-done = f32[8,64,128]{2,1,0:T(8,128)S(1)} async-done(((f32[8,64,128]{2,1,0:T(8,128)}), f32[8,64,128]{2,1,0:T(8,128)S(1)}, u32[]{:S(2)}, u32[]{:S(2)}) %all-to-all-start) | async-done | bytes 262176 | tf_op jit(solution)/shard_map/all_to_all | solution.py:387
  14.0 0.2 collective-permute-start.1
  14.2 0.7 %collective-permute-start = (f32[8,24,128]{2,1,0:T(8,128)S(1)}, f32[8,24,128]{2,1,0:T(8,128)S(1)}, u32[]{:S(2)}, u32[]{:S(2)}) collective-permute-start(f32[8,24,128]{2,1,0:T(8,128)S(1)} %get-tuple-element.9), channel_id=1, source_target_pairs={{1,2},{3,19},{18,17},{16,20},{21,22},{23,7},{6,5},{4,8},{9,10},{11... | collective-permute-start | bytes 294920 | tf_op jit(solution)/shard_map/ppermute | solution.py:396
  14.9 0.5 %collective-permute-done.1 = f32[8,24,128]{2,1,0:T(8,128)S(1)} collective-permute-done((f32[8,24,128]{2,1,0:T(8,128)S(1)}, f32[8,24,128]{2,1,0:T(8,128)S(1)}, u32[]{:S(2)}, u32[]{:S(2)}) %collective-permute-start.1) | collective-permute-done | bytes 98336 | tf_op jit(solution)/shard_map/ppermute | solution.py:395
  15.4 0.0 collective-permute-done
  15.4 0.9 %krylov_kernel.1 = (f32[4,17,8,128]{3,2,1,0:T(8,128)S(1)}, f32[3,16,8,128]{3,2,1,0:T(8,128)S(1)}, f32[32,128]{1,0:T(8,128)S(1)}) custom-call(f32[512,128]{1,0:T(8,128)S(1)} %bitcast.10, f32[192,128]{1,0:T(8,128)S(1)} %bitcast.14, f32[192,128]{1,0:T(8,128)S(1)} %bitcast.13), custom_call_target="tpu_custom_call" | custom-call | tf_op jit(solution)/shard_map/krylov_kernel/pallas_call | solution.py:370
  16.3 16.7 %all_to_all.21 = f32[32,1,128]{2,1,0:T(1,128)S(1)} all-to-all(f32[32,1,128]{2,1,0:T(1,128)S(1)} %bitcast.16), channel_id=1, replica_groups=mesh['gx'=2,'gy'=4,'gz'=4] {'gx','gy','gz'}, dimensions={0} | all-to-all | bytes 32768 | tf_op jit(solution)/shard_map/all_to_all | solution.py:408
  33.1 3.2 %render_kernel.1 = f32[512,128]{1,0:T(8,128)S(1)} custom-call(f32[32,128]{1,0:T(8,128)S(1)} %bitcast.15, f32[4,17,8,128]{3,2,1,0:T(8,128)S(1)} %get-tuple-element.6.refs_1_, f32[3,16,8,128]{3,2,1,0:T(8,128)S(1)} %get-tuple-element.7.refs_2_, f32[512,128]{1,0:T(8,128)S(1)} %bitcast.11, f32[4,8]{1,0:T(4,128)} %bitcast.17, f32[4,8]{1,0:T(4,128)} %bitcast.18, ...), custom_call_target="tpu_custom_call" | custom-call | tf_op jit(solution)/shard_map/render_kernel/pallas_call | solution.py:370
  36.2 8.7 %all_to_all.22.refs_0_ = f32[8,64,128]{2,1,0:T(8,128)S(1)} all-to-all(f32[8,64,128]{2,1,0:T(8,128)S(1)} %bitcast.12), channel_id=1, replica_groups=mesh['gx'=2,'gy'=4,'gz'=4] {'gz','gx'}, dimensions={0} | all-to-all | bytes 524288 | tf_op jit(solution)/shard_map/all_to_all | solution.py:418
  45.0 0.9 %unpack_kernel.1 = (f32[3,8,16,128]{3,2,1,0:T(8,128)}, f32[2,4,16,128]{3,2,1,0:T(8,128)}) custom-call(f32[8,64,128]{2,1,0:T(8,128)S(1)} %all_to_all.22.refs_0_), custom_call_target="tpu_custom_call" | custom-call | tf_op jit(solution)/shard_map/unpack_kernel/pallas_call | solution.py:370
  (2 shorter events, 0.0 us)
Async XLA Ops:
  2.5 11.5 %all-to-all-start = ((f32[8,64,128]{2,1,0:T(8,128)}), f32[8,64,128]{2,1,0:T(8,128)S(1)}, u32[]{:S(2)}, u32[]{:S(2)}) async-start(f32[8,64,128]{2,1,0:T(8,128)} %pack_kernel.1), calls=%async_computation | async-start | bytes 524288 | tf_op jit(solution)/shard_map/all_to_all | solution.py:387
  14.0 1.4 %collective-permute-start.1 = (f32[8,24,128]{2,1,0:T(8,128)S(1)}, f32[8,24,128]{2,1,0:T(8,128)S(1)}, u32[]{:S(2)}, u32[]{:S(2)}) collective-permute-start(f32[8,24,128]{2,1,0:T(8,128)S(1)} %get-tuple-element.8), channel_id=1, source_target_pairs={{0,1},{2,3},{19,18},{17,16},{20,21},{22,23},{7,6},{5,4},{8,9},{10,... | collective-permute-start | bytes 294920 | tf_op jit(solution)/shard_map/ppermute | solution.py:395
  14.2 1.2 %collective-permute-start = (f32[8,24,128]{2,1,0:T(8,128)S(1)}, f32[8,24,128]{2,1,0:T(8,128)S(1)}, u32[]{:S(2)}, u32[]{:S(2)}) collective-permute-start(f32[8,24,128]{2,1,0:T(8,128)S(1)} %get-tuple-element.9), channel_id=1, source_target_pairs={{1,2},{3,19},{18,17},{16,20},{21,22},{23,7},{6,5},{4,8},{9,10},{11... | collective-permute-start | bytes 294920 | tf_op jit(solution)/shard_map/ppermute | solution.py:396

commit v4 on v3

--- a/solution.py
+++ b/solution.py
@@ -52,7 +52,7 @@
     return jnp.where(forward, table[c], table[len(table) - 1 - c])
 
 
-def pack_kernel(phase_ref, thermal_ref, velocity_ref, out_ref, *, table, chunk):
+def pack_kernel(phase_ref, thermal_ref, velocity_ref, slope_ref, offset_ref, gain_ref, out_ref, curves_ref, *, table, chunk, depth):
     zl, xl, yl = thermal_ref.shape
     density = (1.0 + 9.0 * phase_ref[...].astype(F32)) * thermal_ref[...]
     for f in range(FIELDS):
@@ -61,6 +61,22 @@
         for c in range(yl // chunk):
             rows = turned[c * chunk : (c + 1) * chunk]
             out_ref[owner(table, c), pl.ds(f, chunk, stride=FIELDS), :] = rows
+    for t in range(curves_ref.shape[0]):
+        curves_ref[t, 0:4, :] = jnp.broadcast_to(-LOG2E * slope_ref[:, t : t + 1], (4, LANES))
+        curves_ref[t, 4:8, :] = jnp.broadcast_to(-LOG2E * offset_ref[:, t : t + 1], (4, LANES))
+        curves_ref[t, 8:9, :] = jnp.broadcast_to(gain_ref[:, t : t + 1] / depth, (1, LANES))
+
+
+def even_place(ngx, ngz, hop):
+    return chain_place(ngx, ngz) // hop % 2 == 0
+
+
+def edges_kernel(own_ref, *out_refs, ngx, ngz, rows):
+    for h in range(len(out_refs) // 2):
+        high = own_ref.shape[1] - rows
+        even = even_place(ngx, ngz, h + 1)
+        for ref, start in zip(out_refs[2 * h : 2 * h + 2], (jnp.where(even, high, 0), jnp.where(even, 0, high))):
+            ref[...] = own_ref[:, pl.ds(pl.multiple_of(start, 8), rows), :]
 
 
 class Shifts:
@@ -96,9 +112,20 @@
 
 
 def krylov_kernel(*refs, ngx, ngz, zl, xl, chunk, hops, margin, step):
-    own_ref = refs[0]
-    low_refs, high_refs = refs[1 : 1 + hops], refs[1 + hops : 1 + 2 * hops]
-    basis_ref, lower_ref, sums_ref, dens, coef, vec, diag, source = refs[1 + 2 * hops :]
+    own_ref, swapped = refs[0], refs[1 : 1 + 2 * hops]
+    basis_ref, lower_ref, sums_ref, lows, highs, dens, coef, vec, diag, source = refs[1 + 2 * hops :]
+    for h in range(hops):
+        ahead_ref, behind_ref = swapped[2 * h : 2 * h + 2]
+        even = even_place(ngx, ngz, h + 1)
+
+        @pl.when(even)
+        def _():
+            lows[h], highs[h] = behind_ref[...], ahead_ref[...]
+
+        @pl.when(jnp.logical_not(even))
+        def _():
+            lows[h], highs[h] = ahead_ref[...], behind_ref[...]
+
     S, L = ngx * ngz, zl * xl
     E = chunk + 2 * HALO
     move = Shifts(ngx, ngz, zl, xl)
@@ -109,9 +136,9 @@
             return own_ref[pl.ds(k * FIELDS + f, S, stride=chunk * FIELDS), :]
         far = -k - 1 if k < 0 else k - chunk
         hop, at = far // chunk, far % chunk
-        ref = low_refs[hop] if k < 0 else high_refs[hop]
+        ref = lows if k < 0 else highs
         at = margin - 1 - at if k < 0 else at
-        return ref[pl.ds(at * FIELDS + f, S, stride=margin * FIELDS), :]
+        return ref[hop, pl.ds(at * FIELDS + f, S, stride=margin * FIELDS), :]
 
     def planes(a, b, f):
         return jnp.stack([plane(e, f) for e in range(a, b)])
@@ -242,7 +269,7 @@
 
 
 def render_kernel(
-    sums_ref, basis_ref, lower_ref, own_ref, slope_ref, offset_ref, gain_ref, out_ref, press, flat, turned,
+    sums_ref, basis_ref, lower_ref, own_ref, table_ref, out_ref, press, flat, turned,
     *, ngx, ngz, zl, xl, chunk, step
 ):
     S, L = ngx * ngz, zl * xl
@@ -283,17 +310,15 @@
     turned[...] = flat[...].T.reshape(zl, xl, yl)
 
     group = ngx * chunk
-    functions = slope_ref.shape[1] // ngz
-    depth = zl * ngz
+    functions = table_ref.shape[0] // ngz
     lane = lax.broadcasted_iota(jnp.int32, (xl, yl), 1)
 
     def owned(i, carry):
         images = [jnp.zeros((xl, LANES), F32) for _ in range(ngx)]
         for t in range(functions):
             index = i * functions + t
-            rates = [-LOG2E * slope_ref[c, index] for c in range(4)]
-            bases = [-LOG2E * offset_ref[c, index] for c in range(4)]
-            gain = gain_ref[index] / depth
+            rows = [jnp.broadcast_to(table_ref[index, r : r + 1, :], (xl, yl)) for r in range(9)]
+            rates, bases, gain = rows[:4], rows[4:8], rows[8]
             through = jnp.ones((xl, yl), F32)
             colors = [jnp.zeros((xl, yl), F32) for _ in range(3)]
             for z in range(zl):
@@ -354,7 +379,7 @@
         margin = min(chunk, HALO + HALO % 2)
         step = max(1, 4 * 8 // S)
 
-        vmem, smem = (pl.BlockSpec(memory_space=space) for space in (pltpu.VMEM, pltpu.SMEM))
+        vmem = pl.BlockSpec(memory_space=pltpu.VMEM)
 
         def call(body, specs, out, scratch=(), **kwargs):
             kernel = pl.pallas_call(
@@ -381,40 +406,44 @@
             return pltpu.VMEM(shape, F32)
 
         free = pl.BlockSpec()
-        blocks = call(pack_kernel, [free] * 3, placed(S, chunk * FIELDS, L), table=table, chunk=chunk)(
-            phase_field, thermal, velocity
-        )
+        tables = (transfer_slope.T, transfer_offset.T, transfer_gain[None, :])
+        blocks, curves = call(
+            pack_kernel,
+            [free] * 6,
+            (placed(S, chunk * FIELDS, L), placed(transfer_gain.shape[0], 16, LANES)),
+            table=table, chunk=chunk, depth=zl * ngz,
+        )(phase_field, thermal, velocity, *tables)
         pencils = lax.all_to_all(blocks, ("gz", "gx"), 0, 0, tiled=True)
-        first = pencils[:, : margin * FIELDS]
-        last = pencils[:, (chunk - margin) * FIELDS :]
         every = ("gx", "gy", "gz")
-        place = chain_place(ngx, ngz)
-        lows, highs = [], []
-        for hop in range(1, hops + 1):
-            even = place // hop % 2 == 0
-            ahead = lax.ppermute(jnp.where(even, last, first), every, chain_swaps(ngx, ngy, ngz, hop, 0))
-            behind = lax.ppermute(jnp.where(even, first, last), every, chain_swaps(ngx, ngy, ngz, hop, 1))
-            lows.append(jnp.where(even, behind, ahead))
-            highs.append(jnp.where(even, ahead, behind))
+        messages = call(
+            edges_kernel,
+            [vmem],
+            [placed(S, margin * FIELDS, L)] * (2 * hops),
+            ngx=ngx, ngz=ngz, rows=margin * FIELDS,
+        )(pencils)
+        swapped = [
+            lax.ppermute(message, every, chain_swaps(ngx, ngy, ngz, i // 2 + 1, i % 2)).reshape(-1, L)
+            for i, message in enumerate(messages)
+        ]
         own = pencils.reshape(-1, L)
         wide = chunk + 2 * HALO
         basis, lower, sums = call(
             krylov_kernel,
             [vmem] * (1 + 2 * hops),
             (placed(ITERS, chunk + 1, S, L), placed(3, chunk, S, L), placed(devices, LANES)),
-            ((wide, S, L), (6, wide, S, L), (ITERS, wide, S, L), (chunk, S, L), (chunk, S, L)),
+            ((hops, S * margin * FIELDS, L),) * 2 + ((wide, S, L), (6, wide, S, L), (ITERS, wide, S, L), (chunk, S, L), (chunk, S, L)),
             ngx=ngx, ngz=ngz, zl=zl, xl=xl, chunk=chunk, hops=hops, margin=margin, step=step,
-        )(own, *[v.reshape(-1, L) for v in lows + highs])
+        )(own, *swapped)
         sums = lax.all_to_all(sums, every, 0, 0, tiled=True)
         height = 3 * chunk + xl
         height += -height % 8
         packed = call(
             render_kernel,
-            [vmem] * 4 + [smem] * 3,
+            [vmem] * 5,
             placed(S * height, LANES),
             ((chunk + 1, S, L), (yl, L), (zl, xl, yl)),
             ngx=ngx, ngz=ngz, zl=zl, xl=xl, chunk=chunk, step=step,
-        )(sums, basis, lower, own, transfer_slope.T, transfer_offset.T, transfer_gain)
+        )(sums, basis, lower, own, curves)
         home = lax.all_to_all(packed.reshape(S, height, LANES), ("gz", "gx"), 0, 0, tiled=True)
         return call(
             unpack_kernel,

time: 46.2 us -> 44.5 us (0.963)
  blocking collectives: 25.5 us -> 36.8 us
  waiting for transfers between devices: 6.85 us -> 0.53 us
  starting transfers between devices: 6.03 us -> 0.84 us
  Pallas kernels: 6.78 us -> 5.44 us
    all_to_all x0 -> x1, blocking collectives: none -> 11.3 us  [local(): pencils = lax.all_to_all(blocks, ('gz', 'gx'), 0, 0, tiled=True)]
    all_to_all x1 -> x0, waiting for transfers between devices: 6.33 us -> none  [local(): pencils = lax.all_to_all(blocks, ('gz', 'gx'), 0, 0, tiled=True)]
    all_to_all x1 -> x0, starting transfers between devices: 5.2 us -> none  [local(): pencils = lax.all_to_all(blocks, ('gz', 'gx'), 0, 0, tiled=True)]
    pallas_call x4 -> x5, Pallas kernels: 6.78 us -> 5.44 us  [run(): kernel(*[near(a) if spec is vmem else a for a, spec in zip(args, specs)])]
  transfers between devices with their start and end apart: 3 -> 2, of which waited for: 2 -> 1; matrix products, arithmetic and copies ran while one was open for 0% -> 0% of each run, Pallas kernels for 0% -> 0%
where the time goes in v4:
time: 44.5 us; the launch traced here: 44.3 us
  blocking collectives  36.8 us (83%)
  Pallas kernels  5.44 us (12%)
  starting transfers between devices  0.84 us (2%)
  between operations  0.66 us (1%)
  waiting for transfers between devices  0.53 us (1%)
    all_to_all x1, blocking collectives, local(): sums = lax.all_to_all(sums, every, 0, 0, tiled=True)  16.7 us
    all_to_all x1, blocking collectives, local(): pencils = lax.all_to_all(blocks, ('gz', 'gx'), 0, 0, tiled=True)  11.3 us
    all_to_all x1, blocking collectives, local(): lax.all_to_all(packed.reshape(S, height, LANES), ('gz', 'gx'), 0, 0, tile...  8.74 us
    pallas_call x5, Pallas kernels, run(): kernel(*[near(a) if spec is vmem else a for a, spec in zip(args, specs)])  5.44 us
  transfers between devices with their start and end apart: 2, of which 1 were waited for; matrix products, arithmetic and copies ran while one was open for 0% of the time, Pallas kernels for 0%

profile of v4, /device:TPU:0, one launch (start us, length us, event | category | flops | bytes accessed | tf_op | source)
XLA Modules:
  0.0 44.3 jit_solution(3687983640163109056)
XLA Ops:
  0.6 1.2 %pack_kernel.1 = (f32[8,64,128]{2,1,0:T(8,128)S(1)}, f32[8,16,128]{2,1,0:T(8,128)S(1)}) custom-call(s32[8,16,128]{2,1,0:T(8,128)} %refs_0_.1, f32[8,16,128]{2,1,0:T(8,128)} %refs_1_.1, f32[3,8,16,128]{3,2,1,0:T(8,128)} %refs_2_.1, f32[4,8]{1,0:T(4,128)} %bitcast.18, f32[4,8]{1,0:T(4,128)} %bitcast.19, f32[1,8]{1,0:T(1,128)} %bitcast.20), custom_call_target="tpu_custom_call" | custom-call | tf_op jit(solution)/shard_map/pack_kernel/pallas_call | solution.py:395
  1.8 11.3 %all_to_all.21.refs_0_ = f32[8,64,128]{2,1,0:T(8,128)S(1)} all-to-all(f32[8,64,128]{2,1,0:T(8,128)S(1)} %get-tuple-element.9), channel_id=1, replica_groups=mesh['gx'=2,'gy'=4,'gz'=4] {'gz','gx'}, dimensions={0} | all-to-all | bytes 524288 | tf_op jit(solution)/shard_map/all_to_all | solution.py:416
  13.2 0.2 collective-permute-start
  13.4 0.7 %collective-permute-start.1 = (f32[8,24,128]{2,1,0:T(8,128)S(1)}, f32[8,24,128]{2,1,0:T(8,128)S(1)}, u32[]{:S(2)}, u32[]{:S(2)}) collective-permute-start(f32[8,24,128]{2,1,0:T(8,128)S(1)} %get-tuple-element.11), channel_id=1, source_target_pairs={{1,2},{3,19},{18,17},{16,20},{21,22},{23,7},{6,5},{4,8},{9,10},{11... | collective-permute-start | bytes 294920 | tf_op jit(solution)/shard_map/ppermute | solution.py:425
  14.0 0.5 %collective-permute-done = f32[8,24,128]{2,1,0:T(8,128)S(1)} collective-permute-done((f32[8,24,128]{2,1,0:T(8,128)S(1)}, f32[8,24,128]{2,1,0:T(8,128)S(1)}, u32[]{:S(2)}, u32[]{:S(2)}) %collective-permute-start) | collective-permute-done | bytes 98336 | tf_op jit(solution)/shard_map/ppermute | solution.py:425
  14.5 0.0 collective-permute-done.1
  14.5 0.9 %krylov_kernel.1 = (f32[4,17,8,128]{3,2,1,0:T(8,128)S(1)}, f32[3,16,8,128]{3,2,1,0:T(8,128)S(1)}, f32[32,128]{1,0:T(8,128)S(1)}) custom-call(f32[512,128]{1,0:T(8,128)S(1)} %bitcast.11, f32[192,128]{1,0:T(8,128)S(1)} %bitcast.14, f32[192,128]{1,0:T(8,128)S(1)} %bitcast.15), custom_call_target="tpu_custom_call" | custom-call | tf_op jit(solution)/shard_map/krylov_kernel/pallas_call | solution.py:395
  15.5 16.7 %all_to_all.22 = f32[32,1,128]{2,1,0:T(1,128)S(1)} all-to-all(f32[32,1,128]{2,1,0:T(1,128)S(1)} %bitcast.17), channel_id=1, replica_groups=mesh['gx'=2,'gy'=4,'gz'=4] {'gx','gy','gz'}, dimensions={0} | all-to-all | bytes 32768 | tf_op jit(solution)/shard_map/all_to_all | solution.py:437
  32.2 2.4 %render_kernel.1 = f32[512,128]{1,0:T(8,128)S(1)} custom-call(f32[32,128]{1,0:T(8,128)S(1)} %bitcast.16, f32[4,17,8,128]{3,2,1,0:T(8,128)S(1)} %get-tuple-element.13.refs_1_, f32[3,16,8,128]{3,2,1,0:T(8,128)S(1)} %get-tuple-element.14.refs_2_, f32[512,128]{1,0:T(8,128)S(1)} %bitcast.12, f32[8,16,128]{2,1,0:T(8,128)S(1)} %get-tuple-element.15.refs_4_), custom_call_target="tpu_custom_call" | custom-call | tf_op jit(solution)/shard_map/render_kernel/pallas_call | solution.py:395
  34.6 8.7 %all_to_all.23.refs_0_ = f32[8,64,128]{2,1,0:T(8,128)S(1)} all-to-all(f32[8,64,128]{2,1,0:T(8,128)S(1)} %bitcast.13), channel_id=1, replica_groups=mesh['gx'=2,'gy'=4,'gz'=4] {'gz','gx'}, dimensions={0} | all-to-all | bytes 524288 | tf_op jit(solution)/shard_map/all_to_all | solution.py:447
  43.4 0.9 %unpack_kernel.1 = (f32[3,8,16,128]{3,2,1,0:T(8,128)}, f32[2,4,16,128]{3,2,1,0:T(8,128)}) custom-call(f32[8,64,128]{2,1,0:T(8,128)S(1)} %all_to_all.23.refs_0_), custom_call_target="tpu_custom_call" | custom-call | tf_op jit(solution)/shard_map/unpack_kernel/pallas_call | solution.py:395
  (1 shorter events, 0.0 us)
Async XLA Ops:
  13.2 1.4 %collective-permute-start = (f32[8,24,128]{2,1,0:T(8,128)S(1)}, f32[8,24,128]{2,1,0:T(8,128)S(1)}, u32[]{:S(2)}, u32[]{:S(2)}) collective-permute-start(f32[8,24,128]{2,1,0:T(8,128)S(1)} %get-tuple-element.10), channel_id=1, source_target_pairs={{0,1},{2,3},{19,18},{17,16},{20,21},{22,23},{7,6},{5,4},{8,9},{10,... | collective-permute-start | bytes 294920 | tf_op jit(solution)/shard_map/ppermute | solution.py:425
  13.4 1.2 %collective-permute-start.1 = (f32[8,24,128]{2,1,0:T(8,128)S(1)}, f32[8,24,128]{2,1,0:T(8,128)S(1)}, u32[]{:S(2)}, u32[]{:S(2)}) collective-permute-start(f32[8,24,128]{2,1,0:T(8,128)S(1)} %get-tuple-element.11), channel_id=1, source_target_pairs={{1,2},{3,19},{18,17},{16,20},{21,22},{23,7},{6,5},{4,8},{9,10},{11... | collective-permute-start | bytes 294920 | tf_op jit(solution)/shard_map/ppermute | solution.py:425

commit v5 on v4

--- a/solution.py
+++ b/solution.py
@@ -23,15 +23,33 @@
     return order
 
 
-def chain_swaps(ngx, ngy, ngz, hop, odd):
+def chain(ngx, ngy, ngz):
     places = []
     order = snake(ngx, ngz)
     for y in range(ngy):
         for x, z in order if y % 2 == 0 else order[::-1]:
             places.append((x * ngy + y) * ngz + z)
-    firsts = [i for i in range(len(places) - hop) if i // hop % 2 == odd]
-    pairs = [(places[i], places[i + hop]) for i in firsts]
+    return places
+
+
+def both_ways(places, pairs):
+    pairs = [(places[a], places[b]) for a, b in pairs]
     return pairs + [(b, a) for a, b in pairs]
+
+
+def hop_swaps(places, hop, odd):
+    return both_ways(places, [(i, i + hop) for i in range(len(places) - hop) if i // hop % 2 == odd])
+
+
+def run_swaps(places, run, start):
+    pairs, rest = [], list(range(start))
+    while start + run <= len(places):
+        pairs.append((start, start + run - 1))
+        pairs.extend((i, i + 1) for i in range(start + 1, start + run - 1, 2))
+        start += run
+    rest.extend(range(start, len(places)))
+    pairs.extend((i, i + 1) for i in rest if i % 2 == 0)
+    return both_ways(places, pairs)
 
 
 def chain_place(ngx, ngz):
@@ -69,14 +87,6 @@
 
 def even_place(ngx, ngz, hop):
     return chain_place(ngx, ngz) // hop % 2 == 0
-
-
-def edges_kernel(own_ref, *out_refs, ngx, ngz, rows):
-    for h in range(len(out_refs) // 2):
-        high = own_ref.shape[1] - rows
-        even = even_place(ngx, ngz, h + 1)
-        for ref, start in zip(out_refs[2 * h : 2 * h + 2], (jnp.where(even, high, 0), jnp.where(even, 0, high))):
-            ref[...] = own_ref[:, pl.ds(pl.multiple_of(start, 8), rows), :]
 
 
 class Shifts:
@@ -111,72 +121,154 @@
         return jnp.where(self.x_last, far, roll(f, -1, 2))
 
 
-def krylov_kernel(*refs, ngx, ngz, zl, xl, chunk, hops, margin, step):
-    own_ref, swapped = refs[0], refs[1 : 1 + 2 * hops]
-    basis_ref, lower_ref, sums_ref, lows, highs, dens, coef, vec, diag, source = refs[1 + 2 * hops :]
-    for h in range(hops):
-        ahead_ref, behind_ref = swapped[2 * h : 2 * h + 2]
+def divergence(move, velocity, after):
+    vz, vx, vy = velocity
+    out = -(jnp.where(move.z_high, 0.0, move.above_z(vz)) - vz)
+    out = out - (jnp.where(move.x_high, 0.0, move.above_x(vx)) - vx)
+    return out + vy if after is None else out - (after - vy)
+
+
+def column_reader(own_ref, S, chunk):
+    def read(k, f):
+        return own_ref[pl.ds(k * FIELDS + f, S, stride=chunk * FIELDS), :][None]
+
+    return read
+
+
+def column(move, read, k, chunk):
+    velocity = [read(k, f) for f in (1, 2, 3)]
+    return velocity, divergence(move, velocity, read(k + 1, 3) if k + 1 < chunk else None)
+
+
+def edges_kernel(own_ref, *out_refs, ngx, ngz, zl, xl, chunk, margin):
+    move = Shifts(ngx, ngz, zl, xl)
+    read = column_reader(own_ref, ngx * ngz, chunk)
+    messages = []
+    for start in (0, chunk - margin):
+        planes = [read(k, 0) for k in range(start, start + margin)]
+        planes += [column(move, read, k, chunk)[1] for k in range(start, start + margin)]
+        messages.append(jnp.concatenate(planes + [read(0, 3)], axis=0))
+    first, last = messages
+    for h in range(len(out_refs) // 2):
+        ahead_ref, behind_ref = out_refs[2 * h : 2 * h + 2]
         even = even_place(ngx, ngz, h + 1)
 
         @pl.when(even)
         def _():
-            lows[h], highs[h] = behind_ref[...], ahead_ref[...]
+            ahead_ref[...], behind_ref[...] = last, first
 
         @pl.when(jnp.logical_not(even))
         def _():
-            lows[h], highs[h] = ahead_ref[...], behind_ref[...]
-
+            ahead_ref[...], behind_ref[...] = first, last
+
+
+def shared_faces(move, d):
+    def face(missing, other):
+        return 2.0 / (d + jnp.where(missing, d, other))
+
+    return (
+        face(move.z_low, move.below_z(d)),
+        face(move.z_high, move.above_z(d)),
+        face(move.x_low, move.below_x(d)),
+        face(move.x_high, move.above_x(d)),
+    )
+
+
+def own_kernel(own_ref, density_ref, source_ref, velocity_ref, faces_ref, *, ngx, ngz, zl, xl, chunk, step):
+    move = Shifts(ngx, ngz, zl, xl)
+    read = column_reader(own_ref, ngx * ngz, chunk)
+    for k in range(chunk):
+        d = read(k, 0)
+        velocity, source = column(move, read, k, chunk)
+        density_ref[k : k + 1], source_ref[k : k + 1] = d, source
+        for f, v in enumerate(velocity):
+            velocity_ref[f, k : k + 1] = v
+        for f, v in enumerate(shared_faces(move, d)):
+            faces_ref[f, k : k + 1] = v
+
+
+def krylov_kernel(*refs, ngx, ngz, zl, xl, chunk, hops, margin, step, places, runs):
+    density_ref, source_ref, velocity_ref, faces_ref = refs[:4]
+    count = 2 * hops + runs
+    swapped = refs[4 : 4 + count]
+    basis_ref, lower_ref, sums_ref, sides, dens, coef, vec, diag, source = refs[4 + count :]
     S, L = ngx * ngz, zl * xl
     E = chunk + 2 * HALO
     move = Shifts(ngx, ngz, zl, xl)
 
-    def plane(e, f):
-        k = e - HALO
-        if 0 <= k < chunk:
-            return own_ref[pl.ds(k * FIELDS + f, S, stride=chunk * FIELDS), :]
-        far = -k - 1 if k < 0 else k - chunk
-        hop, at = far // chunk, far % chunk
-        ref = lows if k < 0 else highs
-        at = margin - 1 - at if k < 0 else at
-        return ref[hop, pl.ds(at * FIELDS + f, S, stride=margin * FIELDS), :]
-
-    def planes(a, b, f):
-        return jnp.stack([plane(e, f) for e in range(a, b)])
+    place = chain_place(ngx, ngz)
+    for h in range(hops):
+        even = even_place(ngx, ngz, h + 1)
+        sides[jnp.where(even, 1, 0), h] = swapped[2 * h][...]
+        other = jnp.where(even, 0, 1)
+        if not runs:
+            sides[other, h] = swapped[2 * h + 1][...]
+            continue
+        within = place % (2 * S)
+        border = (within == 0) | (within == 2 * S - 1)
+        end = (place == 0) | (place == places - 1)
+
+        @pl.when(jnp.logical_not(border))
+        def _():
+            sides[other, h] = swapped[1][...]
+
+        @pl.when(border & jnp.logical_not(end))
+        def _():
+            sides[other, h] = swapped[2][...]
+
+        @pl.when(end)
+        def _():
+            sides[other, h] = jnp.zeros(sides.shape[2:], F32)
 
     def pieces(a, b):
         return [(i, min(i + step, b)) for i in range(a, b, step)]
 
-    for e in range(E):
-        dens[e] = plane(e, 0)
-    for a, b in pieces(1, E - 1):
+    def outer(j, up):
+        hop, at = j // chunk, j % chunk
+        index = at if up else margin - 1 - at
+        rhs = sides[up, hop, margin + index]
+        if not up and at == 0:
+            rhs = rhs - (velocity_ref[2, 0] if hop == 0 else sides[0, hop - 1, 2 * margin])
+        if up and at == chunk - 1 and hop + 1 < hops:
+            rhs = rhs - sides[1, hop + 1, 2 * margin]
+        return sides[up, hop, index], rhs
+
+    for j in range(HALO):
+        dens[HALO - 1 - j], low_rhs = outer(j, 0)
+        dens[HALO + chunk + j], high_rhs = outer(j, 1)
+        source[HALO - 1 - j], source[HALO + chunk + j] = low_rhs, high_rhs
+    for a, b in pieces(0, chunk):
+        dens[HALO + a : HALO + b] = density_ref[a:b]
+        source[HALO + a : HALO + b] = source_ref[a:b]
+    top = HALO + chunk - 1
+    source[top] = source[top] - sides[1, 0, 2 * margin]
+
+    spans = pieces(1, HALO) + pieces(HALO, HALO + chunk) + pieces(HALO + chunk, E - 1)
+    for a, b in spans:
         d, before, after = dens[a:b], dens[a - 1 : b - 1], dens[a + 1 : b + 1]
+        owned = a >= HALO and b <= HALO + chunk
         inside = d > 0.0
-        d = jnp.where(inside, d, 1.0)
-
-        def face(missing, other):
-            return 2.0 / (d + jnp.where(missing, d, other))
-
-        lz, uz = face(move.z_low, move.below_z(d)), face(move.z_high, move.above_z(d))
-        lx, ux = face(move.x_low, move.below_x(d)), face(move.x_high, move.above_x(d))
-        ly, uy = face(before <= 0.0, before), face(after <= 0.0, after)
+        if owned:
+            lz, uz, lx, ux = (faces_ref[f, a - HALO : b - HALO] for f in range(4))
+        else:
+            d = jnp.where(inside, d, 1.0)
+            lz, uz, lx, ux = shared_faces(move, d)
+        ly = 2.0 / (d + jnp.where(before > 0.0, before, d))
+        uy = 2.0 / (d + jnp.where(after > 0.0, after, d))
         total = lz + uz + lx + ux + ly + uy
-        inverse = jnp.where(inside, 1.0 / total, 0.0)
+        inverse = 1.0 / total
+        if owned:
+            diag[a - HALO : b - HALO] = total
+            lower_ref[a - HALO : b - HALO] = ly
+        else:
+            inverse = jnp.where(inside, inverse, 0.0)
         coef[0, a:b] = jnp.where(move.z_low, 0.0, inverse * lz)
         coef[1, a:b] = jnp.where(move.z_high, 0.0, inverse * uz)
         coef[2, a:b] = jnp.where(move.x_low, 0.0, inverse * lx)
         coef[3, a:b] = jnp.where(move.x_high, 0.0, inverse * ux)
         coef[4, a:b] = inverse * ly
         coef[5, a:b] = inverse * uy
-        vz, vx = planes(a, b, 1), planes(a, b, 2)
-        rhs = -(jnp.where(move.z_high, 0.0, move.above_z(vz)) - vz)
-        rhs = rhs - (jnp.where(move.x_high, 0.0, move.above_x(vx)) - vx)
-        rhs = rhs - (planes(a + 1, b + 1, 3) - planes(a, b, 3))
-        vec[0, a:b] = inverse * rhs
-        for e in range(max(a, HALO), min(b, HALO + chunk)):
-            diag[e - HALO] = total[e - a]
-            source[e - HALO] = rhs[e - a]
-            for k, faces in enumerate((lz, lx, ly)):
-                lower_ref[k, e - HALO] = faces[e - a]
+        vec[0, a:b] = inverse * source[a:b]
 
     def applied(k, a, b):
         f = vec[k, a:b]
@@ -196,7 +288,7 @@
         own = slice(a - HALO, b - HALO)
         basis = [vec[k, a:b] for k in range(ITERS)]
         basis.append(applied(ITERS - 1, a, b))
-        weight, right = diag[own], source[own]
+        weight, right = diag[own], source[a:b]
         gaps = [basis[k] - basis[k + 1] for k in range(ITERS)]
         scaled = [weight * gap for gap in gaps]
         for k in range(count):
@@ -269,7 +361,7 @@
 
 
 def render_kernel(
-    sums_ref, basis_ref, lower_ref, own_ref, table_ref, out_ref, press, flat, turned,
+    sums_ref, basis_ref, faces_ref, lower_ref, velocity_ref, table_ref, out_ref, press, flat, turned, parts,
     *, ngx, ngz, zl, xl, chunk, step
 ):
     S, L = ngx * ngz, zl * xl
@@ -300,8 +392,8 @@
         )
         scalar = None
         for k, front in enumerate(fronts):
-            v = jnp.stack([own_ref[pl.ds(c * FIELDS + k + 1, S, stride=chunk * FIELDS), :] for c in range(a, b)])
-            corrected = v - lower_ref[k, a:b] * (p - front)
+            lower = lower_ref[a:b] if k == 2 else faces_ref[2 * k, a:b]
+            corrected = velocity_ref[k, a:b] - lower * (p - front)
             for c in range(a, b):
                 out_ref[pl.ds(k * chunk + c, S, stride=height), :] = corrected[c - a]
             scalar = corrected if scalar is None else scalar + corrected
@@ -313,21 +405,28 @@
     functions = table_ref.shape[0] // ngz
     lane = lax.broadcasted_iota(jnp.int32, (xl, yl), 1)
 
-    def owned(i, carry):
+    def curve_sums(index, carry):
+        rows = [jnp.broadcast_to(table_ref[index, r : r + 1, :], (xl, yl)) for r in range(9)]
+        rates, bases, gain = rows[:4], rows[4:8], rows[8]
+        through = jnp.ones((xl, yl), F32)
+        colors = [jnp.zeros((xl, yl), F32) for _ in range(3)]
+        for z in range(zl):
+            x = turned[z]
+            curves = [1.0 / (1.0 + jnp.exp2(rates[c] * x + bases[c])) for c in range(4)]
+            opacity = gain * curves[3]
+            weight = through * opacity
+            colors = [colors[c] + weight * curves[c] for c in range(3)]
+            through = through * (1.0 - opacity)
+        for c, value in enumerate(colors + [through]):
+            parts[index, c] = value
+        return carry
+
+    lax.fori_loop(0, table_ref.shape[0], curve_sums, 0)
+    for i in range(ngz):
         images = [jnp.zeros((xl, LANES), F32) for _ in range(ngx)]
         for t in range(functions):
-            index = i * functions + t
-            rows = [jnp.broadcast_to(table_ref[index, r : r + 1, :], (xl, yl)) for r in range(9)]
-            rates, bases, gain = rows[:4], rows[4:8], rows[8]
-            through = jnp.ones((xl, yl), F32)
-            colors = [jnp.zeros((xl, yl), F32) for _ in range(3)]
-            for z in range(zl):
-                x = turned[z]
-                curves = [1.0 / (1.0 + jnp.exp2(rates[c] * x + bases[c])) for c in range(4)]
-                opacity = gain * curves[3]
-                weight = through * opacity
-                colors = [colors[c] + weight * curves[c] for c in range(3)]
-                through = through * (1.0 - opacity)
+            colors = [parts[i * functions + t, c] for c in range(3)]
+            through = parts[i * functions + t, 3]
             planes = list(colors)
             everything = through
             for _ in range(ngz - 1):
@@ -340,11 +439,8 @@
                 for k in range(ngx):
                     images[k] = jnp.where(here, roll(image, start - k * chunk, 1), images[k])
         for k in range(ngx):
-            place = pl.multiple_of((i * ngx + k) * height + 3 * chunk, 2)
-            out_ref[pl.ds(place, xl), :] = images[k]
-        return carry
-
-    lax.fori_loop(0, ngz, owned, 0)
+            place = (i * ngx + k) * height + 3 * chunk
+            out_ref[place : place + xl, :] = images[k]
 
 
 def unpack_kernel(in_ref, corrected_ref, images_ref, flat, *, table, chunk):
@@ -369,6 +465,7 @@
     ngx, ngy, ngz = mesh.shape["gx"], mesh.shape["gy"], mesh.shape["gz"]
     S, devices = ngx * ngz, ngx * ngy * ngz
     table = [z * ngx + x for x, z in snake(ngx, ngz)]
+    places = chain(ngx, ngy, ngz)
 
     def local(phase_field, thermal, velocity, transfer_slope, transfer_offset, transfer_gain):
         zl, xl, yl = thermal.shape
@@ -376,7 +473,7 @@
         functions = transfer_slope.shape[0] // ngz
         assert yl % S == 0 and L == LANES and yl == LANES and functions * 4 * chunk <= LANES
         hops = -(-HALO // chunk)
-        margin = min(chunk, HALO + HALO % 2)
+        margin = min(chunk, HALO)
         step = max(1, 4 * 8 // S)
 
         vmem = pl.BlockSpec(memory_space=pltpu.VMEM)
@@ -415,35 +512,39 @@
         )(phase_field, thermal, velocity, *tables)
         pencils = lax.all_to_all(blocks, ("gz", "gx"), 0, 0, tiled=True)
         every = ("gx", "gy", "gz")
-        messages = call(
-            edges_kernel,
+        own = pencils.reshape(-1, L)
+        sizes = dict(ngx=ngx, ngz=ngz, zl=zl, xl=xl, chunk=chunk)
+        message = (2 * margin + 1, S, L)
+        messages = call(edges_kernel, [vmem], [placed(*message)] * (2 * hops), margin=margin, **sizes)(own)
+        swaps = [(messages[i], hop_swaps(places, i // 2 + 1, i % 2)) for i in range(2 * hops)]
+        runs = hops == 1 and ngy % 2 == 0 and S % 2 == 0
+        if runs:
+            swaps = [swaps[0]] + [(messages[1], run_swaps(places, 2 * S, start)) for start in (0, S)]
+        swapped = [lax.ppermute(value, every, pairs) for value, pairs in swaps[::-1]][::-1]
+        density, source, velocities, faces = call(
+            own_kernel,
             [vmem],
-            [placed(S, margin * FIELDS, L)] * (2 * hops),
-            ngx=ngx, ngz=ngz, rows=margin * FIELDS,
-        )(pencils)
-        swapped = [
-            lax.ppermute(message, every, chain_swaps(ngx, ngy, ngz, i // 2 + 1, i % 2)).reshape(-1, L)
-            for i, message in enumerate(messages)
-        ]
-        own = pencils.reshape(-1, L)
+            (placed(chunk, S, L), placed(chunk, S, L), placed(3, chunk, S, L), placed(4, chunk, S, L)),
+            step=step, **sizes,
+        )(own)
         wide = chunk + 2 * HALO
         basis, lower, sums = call(
             krylov_kernel,
-            [vmem] * (1 + 2 * hops),
-            (placed(ITERS, chunk + 1, S, L), placed(3, chunk, S, L), placed(devices, LANES)),
-            ((hops, S * margin * FIELDS, L),) * 2 + ((wide, S, L), (6, wide, S, L), (ITERS, wide, S, L), (chunk, S, L), (chunk, S, L)),
-            ngx=ngx, ngz=ngz, zl=zl, xl=xl, chunk=chunk, hops=hops, margin=margin, step=step,
-        )(own, *swapped)
+            [vmem] * (4 + len(swapped)),
+            (placed(ITERS, chunk + 1, S, L), placed(chunk, S, L), placed(devices, LANES)),
+            ((2, hops) + message, (wide, S, L), (6, wide, S, L), (ITERS, wide, S, L), (chunk, S, L), (wide, S, L)),
+            hops=hops, margin=margin, step=step, places=devices, runs=int(runs), **sizes,
+        )(density, source, velocities, faces, *swapped)
         sums = lax.all_to_all(sums, every, 0, 0, tiled=True)
         height = 3 * chunk + xl
         height += -height % 8
         packed = call(
             render_kernel,
-            [vmem] * 5,
+            [vmem] * 6,
             placed(S * height, LANES),
-            ((chunk + 1, S, L), (yl, L), (zl, xl, yl)),
-            ngx=ngx, ngz=ngz, zl=zl, xl=xl, chunk=chunk, step=step,
-        )(sums, basis, lower, own, curves)
+            ((chunk + 1, S, L), (yl, L), (zl, xl, yl), (curves.shape[0], 4, xl, yl)),
+            step=step, **sizes,
+        )(sums, basis, faces, lower, velocities, curves)
         home = lax.all_to_all(packed.reshape(S, height, LANES), ("gz", "gx"), 0, 0, tiled=True)
         return call(
             unpack_kernel,

time: 44.5 us -> 41.9 us (0.942)
  blocking collectives: 36.8 us -> 30.9 us
  starting transfers between devices: 0.84 us -> 3.33 us
  waiting for transfers between devices: 0.53 us -> 1.77 us
    all_to_all x1, blocking collectives: 16.7 us -> 10.8 us  [local(): sums = lax.all_to_all(sums, every, 0, 0, tiled=True)]
    ppermute x2 -> x3, starting transfers between devices: 0.84 us -> 3.33 us  [local(): lax.ppermute(value, every, pairs)]
    ppermute x2 -> x3, waiting for transfers between devices: 0.53 us -> 1.77 us  [local(): lax.ppermute(value, every, pairs)]
    pallas_call x5 -> x6, Pallas kernels: 5.44 us -> 5.03 us  [run(): kernel(*[near(a) if spec is vmem else a for a, spec in zip(args, specs)])]
  transfers between devices with their start and end apart: 2 -> 3, of which waited for: 1 -> 1; matrix products, arithmetic and copies ran while one was open for 0% -> 0% of each run, Pallas kernels for 0% -> 1%
where the time goes in v5:
time: 41.9 us; the launch traced here: 41.7 us
  blocking collectives  30.9 us (74%)
  Pallas kernels  5.03 us (12%)
  starting transfers between devices  3.33 us (8%)
  waiting for transfers between devices  1.77 us (4%)
  between operations  0.67 us (2%)
    all_to_all x1, blocking collectives, local(): pencils = lax.all_to_all(blocks, ('gz', 'gx'), 0, 0, tiled=True)  11.3 us
    all_to_all x1, blocking collectives, local(): sums = lax.all_to_all(sums, every, 0, 0, tiled=True)  10.8 us
    all_to_all x1, blocking collectives, local(): lax.all_to_all(packed.reshape(S, height, LANES), ('gz', 'gx'), 0, 0, tile...  8.74 us
    pallas_call x6, Pallas kernels, run(): kernel(*[near(a) if spec is vmem else a for a, spec in zip(args, specs)])  5.03 us
    ppermute x3, starting transfers between devices, local(): lax.ppermute(value, every, pairs)  3.33 us
    ppermute x3, waiting for transfers between devices, local(): lax.ppermute(value, every, pairs)  1.77 us
  transfers between devices with their start and end apart: 3, of which 1 were waited for; matrix products, arithmetic and copies ran while one was open for 0% of the time, Pallas kernels for 1%

profile of v5, /device:TPU:0, one launch (start us, length us, event | category | flops | bytes accessed | tf_op | source)
XLA Modules:
  0.0 41.7 jit_solution(11019185301376054012)
XLA Ops:
  0.6 1.2 %pack_kernel.1 = (f32[8,64,128]{2,1,0:T(8,128)S(1)}, f32[8,16,128]{2,1,0:T(8,128)S(1)}) custom-call(s32[8,16,128]{2,1,0:T(8,128)} %refs_0_.1, f32[8,16,128]{2,1,0:T(8,128)} %refs_1_.1, f32[3,8,16,128]{3,2,1,0:T(8,128)} %refs_2_.1, f32[4,8]{1,0:T(4,128)} %bitcast.14, f32[4,8]{1,0:T(4,128)} %bitcast.15, f32[1,8]{1,0:T(1,128)} %bitcast.16), custom_call_target="tpu_custom_call" | custom-call | tf_op jit(solution)/shard_map/pack_kernel/pallas_call | solution.py:492
  1.8 11.3 %all_to_all.21 = f32[8,64,128]{2,1,0:T(8,128)S(1)} all-to-all(f32[8,64,128]{2,1,0:T(8,128)S(1)} %get-tuple-element.13), channel_id=1, replica_groups=mesh['gx'=2,'gy'=4,'gz'=4] {'gz','gx'}, dimensions={0} | all-to-all | bytes 524288 | tf_op jit(solution)/shard_map/all_to_all | solution.py:513
  13.2 0.1 edges_kernel.1
  13.3 0.2 collective-permute-start
  13.5 0.4 collective-permute-start.2
  13.9 2.8 %collective-permute-start.1 = (f32[11,8,128]{2,1,0:T(8,128)S(1)}, f32[11,8,128]{2,1,0:T(8,128)S(1)}, u32[]{:S(2)}, u32[]{:S(2)}) collective-permute-start(f32[11,8,128]{2,1,0:T(8,128)S(1)} %get-tuple-element.19), channel_id=1, source_target_pairs={{0,4},{1,2},{3,19},{18,17},{16,20},{21,22},{23,7},{6,5},{8,12},{9,... | collective-permute-start | bytes 135176 | tf_op jit(solution)/shard_map/ppermute | solution.py:523
  16.6 0.2 own_kernel.1
  16.9 0.0 collective-permute-done.refs_4_
  16.9 0.0 collective-permute-done.2.refs_6_
  16.9 1.8 %collective-permute-done.1.refs_5_ = f32[11,8,128]{2,1,0:T(8,128)S(1)} collective-permute-done((f32[11,8,128]{2,1,0:T(8,128)S(1)}, f32[11,8,128]{2,1,0:T(8,128)S(1)}, u32[]{:S(2)}, u32[]{:S(2)}) %collective-permute-start.1) | collective-permute-done | bytes 45088 | tf_op jit(solution)/shard_map/ppermute | solution.py:523
  18.7 0.8 %krylov_kernel.1 = (f32[4,17,8,128]{3,2,1,0:T(8,128)S(1)}, f32[16,8,128]{2,1,0:T(8,128)S(1)}, f32[32,128]{1,0:T(8,128)S(1)}) custom-call(f32[16,8,128]{2,1,0:T(8,128)S(1)} %get-tuple-element.14.refs_0_, f32[16,8,128]{2,1,0:T(8,128)S(1)} %get-tuple-element.15.refs_1_, f32[3,16,8,128]{3,2,1,0:T(8,128)S(1)} %get-tuple-element.16.refs_2_.refs_4_, ...), custom_call_target="tpu_custom_call" | custom-call | tf_op jit(solution)/shard_map/krylov_kernel/pallas_call | solution.py:492
  19.4 10.8 %all_to_all.22 = f32[32,1,128]{2,1,0:T(1,128)S(1)} all-to-all(f32[32,1,128]{2,1,0:T(1,128)S(1)} %bitcast.13), channel_id=1, replica_groups=mesh['gx'=2,'gy'=4,'gz'=4] {'gx','gy','gz'}, dimensions={0} | all-to-all | bytes 32768 | tf_op jit(solution)/shard_map/all_to_all | solution.py:538
  30.2 1.8 %render_kernel.1 = f32[512,128]{1,0:T(8,128)S(1)} custom-call(f32[32,128]{1,0:T(8,128)S(1)} %bitcast.12, f32[4,17,8,128]{3,2,1,0:T(8,128)S(1)} %get-tuple-element.21.refs_1_, f32[4,16,8,128]{3,2,1,0:T(8,128)S(1)} %get-tuple-element.17.refs_3_.refs_2_, f32[16,8,128]{2,1,0:T(8,128)S(1)} %get-tuple-element.22.refs_3_, ...), custom_call_target="tpu_custom_call" | custom-call | tf_op jit(solution)/shard_map/render_kernel/pallas_call | solution.py:492
  32.0 8.7 %all_to_all.23.refs_0_ = f32[8,64,128]{2,1,0:T(8,128)S(1)} all-to-all(f32[8,64,128]{2,1,0:T(8,128)S(1)} %bitcast.11), channel_id=1, replica_groups=mesh['gx'=2,'gy'=4,'gz'=4] {'gz','gx'}, dimensions={0} | all-to-all | bytes 524288 | tf_op jit(solution)/shard_map/all_to_all | solution.py:548
  40.8 0.9 %unpack_kernel.1 = (f32[3,8,16,128]{3,2,1,0:T(8,128)}, f32[2,4,16,128]{3,2,1,0:T(8,128)}) custom-call(f32[8,64,128]{2,1,0:T(8,128)S(1)} %all_to_all.23.refs_0_), custom_call_target="tpu_custom_call" | custom-call | tf_op jit(solution)/shard_map/unpack_kernel/pallas_call | solution.py:492
Async XLA Ops:
  13.3 3.6 %collective-permute-start = (f32[11,8,128]{2,1,0:T(8,128)S(1)}, f32[11,8,128]{2,1,0:T(8,128)S(1)}, u32[]{:S(2)}, u32[]{:S(2)}) collective-permute-start(f32[11,8,128]{2,1,0:T(8,128)S(1)} %get-tuple-element.18), channel_id=1, source_target_pairs={{0,1},{2,3},{19,18},{17,16},{20,21},{22,23},{7,6},{5,4},{8,9},{10,... | collective-permute-start | bytes 135176 | tf_op jit(solution)/shard_map/ppermute | solution.py:523
  13.5 3.4 %collective-permute-start.2 = (f32[11,8,128]{2,1,0:T(8,128)S(1)}, f32[11,8,128]{2,1,0:T(8,128)S(1)}, u32[]{:S(2)}, u32[]{:S(2)}) collective-permute-start(f32[11,8,128]{2,1,0:T(8,128)S(1)} %get-tuple-element.19), channel_id=1, source_target_pairs={{20,24},{21,22},{23,7},{6,5},{4,8},{9,10},{11,27},{26,25},{0,1},{2... | collective-permute-start | bytes 135176 | tf_op jit(solution)/shard_map/ppermute | solution.py:523
  13.9 4.8 %collective-permute-start.1 = (f32[11,8,128]{2,1,0:T(8,128)S(1)}, f32[11,8,128]{2,1,0:T(8,128)S(1)}, u32[]{:S(2)}, u32[]{:S(2)}) collective-permute-start(f32[11,8,128]{2,1,0:T(8,128)S(1)} %get-tuple-element.19), channel_id=1, source_target_pairs={{0,4},{1,2},{3,19},{18,17},{16,20},{21,22},{23,7},{6,5},{8,12},{9,... | collective-permute-start | bytes 135176 | tf_op jit(solution)/shard_map/ppermute | solution.py:523

commit v6 on v5

--- a/solution.py
+++ b/solution.py
@@ -70,9 +70,12 @@
     return jnp.where(forward, table[c], table[len(table) - 1 - c])
 
 
-def pack_kernel(phase_ref, thermal_ref, velocity_ref, slope_ref, offset_ref, gain_ref, out_ref, curves_ref, *, table, chunk, depth):
+def pack_kernel(phase_ref, thermal_ref, velocity_ref, slope_ref, offset_ref, gain_ref, *outs, table, chunk, depth):
+    out_ref, curves_ref, density_ref, kept_ref = outs
     zl, xl, yl = thermal_ref.shape
     density = (1.0 + 9.0 * phase_ref[...].astype(F32)) * thermal_ref[...]
+    density_ref[...] = density
+    kept_ref[...] = velocity_ref[...]
     for f in range(FIELDS):
         field = density if f == 0 else velocity_ref[f - 1]
         turned = field.reshape(zl * xl, yl).T
@@ -83,6 +86,19 @@
         curves_ref[t, 0:4, :] = jnp.broadcast_to(-LOG2E * slope_ref[:, t : t + 1], (4, LANES))
         curves_ref[t, 4:8, :] = jnp.broadcast_to(-LOG2E * offset_ref[:, t : t + 1], (4, LANES))
         curves_ref[t, 8:9, :] = jnp.broadcast_to(gain_ref[:, t : t + 1] / depth, (1, LANES))
+
+
+class Slot:
+    def __init__(self, zl, xl, chunk):
+        self.width = 1
+        while self.width < zl + xl:
+            self.width *= 2
+        groups = LANES // self.width
+        self.faces = chunk
+        self.deep = -(-chunk // groups)
+        self.side = chunk + self.deep
+        self.images = -(-(self.side + 1) // 8) * 8
+        self.height = -(-(self.images + xl) // 8) * 8
 
 
 def even_place(ngx, ngz, hop):
@@ -174,7 +190,11 @@
     )
 
 
-def own_kernel(own_ref, density_ref, source_ref, velocity_ref, faces_ref, *, ngx, ngz, zl, xl, chunk, step):
+def own_kernel(own_ref, home_ref, density_ref, source_ref, velocity_ref, faces_ref, lower_ref, *, ngx, ngz, zl, xl, chunk):
+    d = home_ref[...]
+    lower_ref[0] = 2.0 / (d + jnp.concatenate([d[:1], d[:-1]], axis=0))
+    lower_ref[1] = 2.0 / (d + roll(d, 1, 1))
+    lower_ref[2] = 2.0 / (d + roll(d, 1, 2))
     move = Shifts(ngx, ngz, zl, xl)
     read = column_reader(own_ref, ngx * ngz, chunk)
     for k in range(chunk):
@@ -366,7 +386,8 @@
 ):
     S, L = ngx * ngz, zl * xl
     yl = S * chunk
-    height = out_ref.shape[0] // S
+    slot = Slot(zl, xl, chunk)
+    height = slot.height
     move = Shifts(ngx, ngz, zl, xl)
     by_power, by_step = galerkin(sums_ref[...])
     by_power = [v.reshape(1, 1, 1) for v in by_power]
@@ -382,6 +403,8 @@
             level = [level[i] - level[i + 1] for i in range(len(level) - 1)]
             value = value + by_step[k] * level[0]
         press[a:b] = value
+    spot = lax.broadcasted_iota(jnp.int32, (S, L), 1)
+    sides = [jnp.zeros((S, L), F32) for _ in range(slot.deep)]
     for a in range(0, chunk, step):
         b = min(a + step, chunk)
         p = press[a + 1 : b + 1]
@@ -390,18 +413,28 @@
             jnp.where(move.x_low, 0.0, move.below_x(p)),
             press[a:b],
         )
-        scalar = None
+        pieces = []
         for k, front in enumerate(fronts):
             lower = lower_ref[a:b] if k == 2 else faces_ref[2 * k, a:b]
-            corrected = velocity_ref[k, a:b] - lower * (p - front)
-            for c in range(a, b):
-                out_ref[pl.ds(k * chunk + c, S, stride=height), :] = corrected[c - a]
-            scalar = corrected if scalar is None else scalar + corrected
+            pieces.append(velocity_ref[k, a:b] - lower * (p - front))
+        scalar = pieces[0] + pieces[1] + pieces[2]
+        if a == 0:
+            out_ref[pl.ds(slot.side, S, stride=height), :] = pieces[2][0]
         for c in range(a, b):
+            out_ref[pl.ds(c, S, stride=height), :] = p[c - a]
             flat[pl.ds(c, S, stride=chunk), :] = scalar[c - a]
+            base = c // slot.deep * slot.width
+            deep = roll(pieces[0][c - a], base, 1)
+            where = (spot - (base + xl)) * xl
+            wide = jnp.take_along_axis(pieces[1][c - a], jnp.clip(where, 0, L - 1), axis=1, mode="promise_in_bounds")
+            r = c % slot.deep
+            sides[r] = jnp.where(spot >= base, jnp.where(spot >= base + xl, wide, deep), sides[r])
+    for r, side in enumerate(sides):
+        out_ref[pl.ds(slot.faces + r, S, stride=height), :] = side
     turned[...] = flat[...].T.reshape(zl, xl, yl)
 
     group = ngx * chunk
+    band = LANES // 4
     functions = table_ref.shape[0] // ngz
     lane = lax.broadcasted_iota(jnp.int32, (xl, yl), 1)
 
@@ -425,40 +458,59 @@
     for i in range(ngz):
         images = [jnp.zeros((xl, LANES), F32) for _ in range(ngx)]
         for t in range(functions):
-            colors = [parts[i * functions + t, c] for c in range(3)]
-            through = parts[i * functions + t, 3]
-            planes = list(colors)
-            everything = through
-            for _ in range(ngz - 1):
-                planes = [colors[c] + through * roll(planes[c], -group, 1) for c in range(3)]
-                everything = through * roll(everything, -group, 1)
-            planes.append(1.0 - everything)
-            for c, image in enumerate(planes):
-                start = (t * 4 + c) * chunk
-                here = (lane >= start) & (lane < start + chunk)
-                for k in range(ngx):
-                    images[k] = jnp.where(here, roll(image, start - k * chunk, 1), images[k])
+            planes = [parts[i * functions + t, c] for c in range(4)]
+            span = 1
+            while span < ngz:
+                behind = [roll(plane, -span * group, 1) for plane in planes]
+                planes = [planes[c] + planes[3] * behind[c] for c in range(3)] + [planes[3] * behind[3]]
+                span *= 2
+            planes[3] = 1.0 - planes[3]
+            merged = planes[0]
+            for c in range(1, 4):
+                merged = jnp.where(lane >= c * band, roll(planes[c], c * band, 1), merged)
+            for k in range(ngx):
+                here = (lane % band) // chunk == t
+                images[k] = jnp.where(here, roll(merged, (t - k) * chunk, 1), images[k])
         for k in range(ngx):
-            place = (i * ngx + k) * height + 3 * chunk
+            place = (i * ngx + k) * height + slot.images
             out_ref[place : place + xl, :] = images[k]
 
 
-def unpack_kernel(in_ref, corrected_ref, images_ref, flat, *, table, chunk):
+def unpack_kernel(in_ref, lower_ref, velocity_ref, corrected_ref, images_ref, flat, sides, *, table, chunk):
     zl, xl, yl = corrected_ref.shape[1:]
+    slot = Slot(zl, xl, chunk)
     functions = images_ref.shape[0]
-    pieces = yl // chunk
-    for f in range(3):
-        for c in range(pieces):
-            flat[c * chunk : (c + 1) * chunk, :] = in_ref[owner(table, c), f * chunk : (f + 1) * chunk, :]
-        corrected_ref[f] = flat[...].T.reshape(zl, xl, yl)
+    band = LANES // 4
     lane = lax.broadcasted_iota(jnp.int32, (xl, yl), 1)
     images = [jnp.zeros((xl, yl), F32) for _ in range(functions * 4)]
-    for c in range(pieces):
-        source = in_ref[owner(table, c), 3 * chunk : 3 * chunk + xl, :]
+    for c in range(yl // chunk):
+        place = owner(table, c)
+        flat[c * chunk : (c + 1) * chunk, :] = in_ref[place, :chunk, :]
+        faces = in_ref[place, slot.faces : slot.faces + 8, :]
+        for g in range(-(-chunk // slot.deep)):
+            rows = min(slot.deep, chunk - g * slot.deep)
+            start = c * chunk + g * slot.deep
+            sides[start : start + rows, :] = roll(faces, -g * slot.width, 1)[:rows]
+        source = in_ref[place, slot.images : slot.images + xl, :]
         here = (lane >= c * chunk) & (lane < (c + 1) * chunk)
-        images = [jnp.where(here, roll(source, (c - k) * chunk, 1), image) for k, image in enumerate(images)]
+        for k in range(functions * 4):
+            shift = c * chunk - (k % 4 * band + k // 4 * chunk)
+            images[k] = jnp.where(here, roll(source, shift, 1), images[k])
     for k, image in enumerate(images):
         images_ref[k // 4, k % 4] = image
+    p = flat[...].T.reshape(zl, xl, yl)
+    faces = sides[...].T
+    deep, wide = faces[:xl], faces[xl : xl + zl]
+    front = in_ref[owner(table, 0), slot.side : slot.side + 1, :]
+    high = jnp.broadcast_to(front, (yl, zl * xl)).T.reshape(zl, xl, yl)
+    x = lax.broadcasted_iota(jnp.int32, (zl, xl, yl), 1)
+    y = lax.broadcasted_iota(jnp.int32, (zl, xl, yl), 2)
+    inner = velocity_ref[0, 1:] - lower_ref[0, 1:] * (p[1:] - p[:-1])
+    corrected_ref[0, 0], corrected_ref[0, 1:] = deep, inner
+    inner = velocity_ref[1] - lower_ref[1] * (p - roll(p, 1, 1))
+    corrected_ref[1] = jnp.where(x == 0, wide[:, None, :], inner)
+    inner = velocity_ref[2] - lower_ref[2] * (p - roll(p, 1, 2))
+    corrected_ref[2] = jnp.where(y == 0, high, inner)
 
 
 def solution(mesh):
@@ -471,7 +523,8 @@
         zl, xl, yl = thermal.shape
         L, chunk = zl * xl, yl // S
         functions = transfer_slope.shape[0] // ngz
-        assert yl % S == 0 and L == LANES and yl == LANES and functions * 4 * chunk <= LANES
+        assert yl % S == 0 and L == LANES and yl == LANES and max(ngx, functions) * 4 * chunk <= LANES
+        assert ngz & (ngz - 1) == 0
         hops = -(-HALO // chunk)
         margin = min(chunk, HALO)
         step = max(1, 4 * 8 // S)
@@ -504,10 +557,11 @@
 
         free = pl.BlockSpec()
         tables = (transfer_slope.T, transfer_offset.T, transfer_gain[None, :])
-        blocks, curves = call(
+        block = (zl, xl, yl)
+        blocks, curves, home_density, kept = call(
             pack_kernel,
             [free] * 6,
-            (placed(S, chunk * FIELDS, L), placed(transfer_gain.shape[0], 16, LANES)),
+            (placed(S, chunk * FIELDS, L), placed(transfer_gain.shape[0], 16, LANES), placed(*block), placed(3, *block)),
             table=table, chunk=chunk, depth=zl * ngz,
         )(phase_field, thermal, velocity, *tables)
         pencils = lax.all_to_all(blocks, ("gz", "gx"), 0, 0, tiled=True)
@@ -521,12 +575,12 @@
         if runs:
             swaps = [swaps[0]] + [(messages[1], run_swaps(places, 2 * S, start)) for start in (0, S)]
         swapped = [lax.ppermute(value, every, pairs) for value, pairs in swaps[::-1]][::-1]
-        density, source, velocities, faces = call(
+        density, source, velocities, faces, home_lower = call(
             own_kernel,
-            [vmem],
-            (placed(chunk, S, L), placed(chunk, S, L), placed(3, chunk, S, L), placed(4, chunk, S, L)),
-            step=step, **sizes,
-        )(own)
+            [vmem] * 2,
+            (placed(chunk, S, L), placed(chunk, S, L), placed(3, chunk, S, L), placed(4, chunk, S, L), placed(3, *block)),
+            **sizes,
+        )(own, home_density)
         wide = chunk + 2 * HALO
         basis, lower, sums = call(
             krylov_kernel,
@@ -536,8 +590,7 @@
             hops=hops, margin=margin, step=step, places=devices, runs=int(runs), **sizes,
         )(density, source, velocities, faces, *swapped)
         sums = lax.all_to_all(sums, every, 0, 0, tiled=True)
-        height = 3 * chunk + xl
-        height += -height % 8
+        height = Slot(zl, xl, chunk).height
         packed = call(
             render_kernel,
             [vmem] * 6,
@@ -548,11 +601,11 @@
         home = lax.all_to_all(packed.reshape(S, height, LANES), ("gz", "gx"), 0, 0, tiled=True)
         return call(
             unpack_kernel,
-            [vmem],
-            (shaped(3, zl, xl, yl), shaped(functions, 4, xl, yl)),
-            ((yl, L),),
+            [vmem] * 3,
+            (shaped(3, *block), shaped(functions, 4, xl, yl)),
+            ((yl, L), (yl, LANES)),
             table=table, chunk=chunk,
-        )(home)
+        )(home, home_lower, kept)
 
     return jax.shard_map(
         local,

time: 41.9 us -> 40.8 us (0.974)
  blocking collectives: 30.9 us -> 29.9 us
    all_to_all x1, blocking collectives: 8.74 us -> 7.8 us  [local(): lax.all_to_all(packed.reshape(S, height, LANES), ('gz', 'gx'), 0, 0, tile...]
where the time goes in v6:
time: 40.8 us; the launch traced here: 40.6 us
  blocking collectives  29.9 us (73%)
  Pallas kernels  4.9 us (12%)
  starting transfers between devices  3.33 us (8%)
  waiting for transfers between devices  1.75 us (4%)
  between operations  0.67 us (2%)
    all_to_all x1, blocking collectives, local(): pencils = lax.all_to_all(blocks, ('gz', 'gx'), 0, 0, tiled=True)  11.3 us
    all_to_all x1, blocking collectives, local(): sums = lax.all_to_all(sums, every, 0, 0, tiled=True)  10.8 us
    all_to_all x1, blocking collectives, local(): lax.all_to_all(packed.reshape(S, height, LANES), ('gz', 'gx'), 0, 0, tile...  7.8 us
    pallas_call x6, Pallas kernels, run(): kernel(*[near(a) if spec is vmem else a for a, spec in zip(args, specs)])  4.9 us
    ppermute x3, starting transfers between devices, local(): lax.ppermute(value, every, pairs)  3.33 us
    ppermute x3, waiting for transfers between devices, local(): lax.ppermute(value, every, pairs)  1.75 us
  transfers between devices with their start and end apart: 3, of which 1 were waited for; matrix products, arithmetic and copies ran while one was open for 0% of the time, Pallas kernels for 1%

profile of v6, /device:TPU:0, one launch (start us, length us, event | category | flops | bytes accessed | tf_op | source)
XLA Modules:
  0.0 40.6 jit_solution(17752210323884426365)
XLA Ops:
  0.6 1.2 %pack_kernel.1 = (f32[8,64,128]{2,1,0:T(8,128)S(1)}, f32[8,16,128]{2,1,0:T(8,128)S(1)}, f32[8,16,128]{2,1,0:T(8,128)S(1)}, f32[3,8,16,128]{3,2,1,0:T(8,128)S(1)}) custom-call(s32[8,16,128]{2,1,0:T(8,128)} %refs_0_.1, f32[8,16,128]{2,1,0:T(8,128)} %refs_1_.1, f32[3,8,16,128]{3,2,1,0:T(8,128)} %refs_2_.1, f32[4,8]{1,0:T(4,128)} %bitcast.14, f32[4,8]{1,0:T(4,128)} %bitcast.15, ...), custom_call_target="tpu_custom_call" | custom-call | tf_op jit(solution)/shard_map/pack_kernel/pallas_call | solution.py:545
  1.8 11.3 %all_to_all.21 = f32[8,64,128]{2,1,0:T(8,128)S(1)} all-to-all(f32[8,64,128]{2,1,0:T(8,128)S(1)} %get-tuple-element.16), channel_id=1, replica_groups=mesh['gx'=2,'gy'=4,'gz'=4] {'gz','gx'}, dimensions={0} | all-to-all | bytes 524288 | tf_op jit(solution)/shard_map/all_to_all | solution.py:567
  13.2 0.1 edges_kernel.1
  13.3 0.2 collective-permute-start
  13.5 0.4 collective-permute-start.2
  13.9 2.8 %collective-permute-start.1 = (f32[11,8,128]{2,1,0:T(8,128)S(1)}, f32[11,8,128]{2,1,0:T(8,128)S(1)}, u32[]{:S(2)}, u32[]{:S(2)}) collective-permute-start(f32[11,8,128]{2,1,0:T(8,128)S(1)} %get-tuple-element.23), channel_id=1, source_target_pairs={{0,4},{1,2},{3,19},{18,17},{16,20},{21,22},{23,7},{6,5},{8,12},{9,... | collective-permute-start | bytes 135176 | tf_op jit(solution)/shard_map/ppermute | solution.py:577
  16.6 0.3 own_kernel.1
  16.9 0.0 collective-permute-done.refs_4_
  16.9 0.0 collective-permute-done.2.refs_6_
  16.9 1.7 %collective-permute-done.1.refs_5_ = f32[11,8,128]{2,1,0:T(8,128)S(1)} collective-permute-done((f32[11,8,128]{2,1,0:T(8,128)S(1)}, f32[11,8,128]{2,1,0:T(8,128)S(1)}, u32[]{:S(2)}, u32[]{:S(2)}) %collective-permute-start.1) | collective-permute-done | bytes 45088 | tf_op jit(solution)/shard_map/ppermute | solution.py:577
  18.7 0.8 %krylov_kernel.1 = (f32[4,17,8,128]{3,2,1,0:T(8,128)S(1)}, f32[16,8,128]{2,1,0:T(8,128)S(1)}, f32[32,128]{1,0:T(8,128)S(1)}) custom-call(f32[16,8,128]{2,1,0:T(8,128)S(1)} %get-tuple-element.18.refs_0_, f32[16,8,128]{2,1,0:T(8,128)S(1)} %get-tuple-element.19.refs_1_, f32[3,16,8,128]{3,2,1,0:T(8,128)S(1)} %get-tuple-element.20.refs_2_.refs_4_, ...), custom_call_target="tpu_custom_call" | custom-call | tf_op jit(solution)/shard_map/krylov_kernel/pallas_call | solution.py:545
  19.5 10.8 %all_to_all.22 = f32[32,1,128]{2,1,0:T(1,128)S(1)} all-to-all(f32[32,1,128]{2,1,0:T(1,128)S(1)} %bitcast.13), channel_id=1, replica_groups=mesh['gx'=2,'gy'=4,'gz'=4] {'gx','gy','gz'}, dimensions={0} | all-to-all | bytes 32768 | tf_op jit(solution)/shard_map/all_to_all | solution.py:592
  30.2 1.5 %render_kernel.1 = f32[320,128]{1,0:T(8,128)S(1)} custom-call(f32[32,128]{1,0:T(8,128)S(1)} %bitcast.12, f32[4,17,8,128]{3,2,1,0:T(8,128)S(1)} %get-tuple-element.25.refs_1_, f32[4,16,8,128]{3,2,1,0:T(8,128)S(1)} %get-tuple-element.21.refs_3_.refs_2_, f32[16,8,128]{2,1,0:T(8,128)S(1)} %get-tuple-element.26.refs_3_, ...), custom_call_target="tpu_custom_call" | custom-call | tf_op jit(solution)/shard_map/render_kernel/pallas_call | solution.py:545
  31.7 7.8 %all_to_all.23.refs_0_ = f32[8,40,128]{2,1,0:T(8,128)S(1)} all-to-all(f32[8,40,128]{2,1,0:T(8,128)S(1)} %bitcast.11), channel_id=1, replica_groups=mesh['gx'=2,'gy'=4,'gz'=4] {'gz','gx'}, dimensions={0} | all-to-all | bytes 327680 | tf_op jit(solution)/shard_map/all_to_all | solution.py:601
  39.6 1.0 %unpack_kernel.1 = (f32[3,8,16,128]{3,2,1,0:T(8,128)}, f32[2,4,16,128]{3,2,1,0:T(8,128)}) custom-call(f32[8,40,128]{2,1,0:T(8,128)S(1)} %all_to_all.23.refs_0_, f32[3,8,16,128]{3,2,1,0:T(8,128)S(1)} %get-tuple-element.28.refs_1_, f32[3,8,16,128]{3,2,1,0:T(8,128)S(1)} %get-tuple-element.29.refs_2_), custom_call_target="tpu_custom_call" | custom-call | tf_op jit(solution)/shard_map/unpack_kernel/pallas_call | solution.py:545
Async XLA Ops:
  13.3 3.6 %collective-permute-start = (f32[11,8,128]{2,1,0:T(8,128)S(1)}, f32[11,8,128]{2,1,0:T(8,128)S(1)}, u32[]{:S(2)}, u32[]{:S(2)}) collective-permute-start(f32[11,8,128]{2,1,0:T(8,128)S(1)} %get-tuple-element.22), channel_id=1, source_target_pairs={{0,1},{2,3},{19,18},{17,16},{20,21},{22,23},{7,6},{5,4},{8,9},{10,... | collective-permute-start | bytes 135176 | tf_op jit(solution)/shard_map/ppermute | solution.py:577
  13.5 3.4 %collective-permute-start.2 = (f32[11,8,128]{2,1,0:T(8,128)S(1)}, f32[11,8,128]{2,1,0:T(8,128)S(1)}, u32[]{:S(2)}, u32[]{:S(2)}) collective-permute-start(f32[11,8,128]{2,1,0:T(8,128)S(1)} %get-tuple-element.23), channel_id=1, source_target_pairs={{20,24},{21,22},{23,7},{6,5},{4,8},{9,10},{11,27},{26,25},{0,1},{2... | collective-permute-start | bytes 135176 | tf_op jit(solution)/shard_map/ppermute | solution.py:577
  13.9 4.8 %collective-permute-start.1 = (f32[11,8,128]{2,1,0:T(8,128)S(1)}, f32[11,8,128]{2,1,0:T(8,128)S(1)}, u32[]{:S(2)}, u32[]{:S(2)}) collective-permute-start(f32[11,8,128]{2,1,0:T(8,128)S(1)} %get-tuple-element.23), channel_id=1, source_target_pairs={{0,4},{1,2},{3,19},{18,17},{16,20},{21,22},{23,7},{6,5},{8,12},{9,... | collective-permute-start | bytes 135176 | tf_op jit(solution)/shard_map/ppermute | solution.py:577

commit v7 on v6

--- a/solution.py
+++ b/solution.py
@@ -11,6 +11,7 @@
 HALO = ITERS + 1
 FIELDS = 4
 LANES = 128
+VMEM_LIMIT = 24 << 20
 LOG2E = math.log2(math.e)
 F32 = jnp.float32
 
@@ -190,11 +191,65 @@
     )
 
 
-def own_kernel(own_ref, home_ref, density_ref, source_ref, velocity_ref, faces_ref, lower_ref, *, ngx, ngz, zl, xl, chunk):
-    d = home_ref[...]
-    lower_ref[0] = 2.0 / (d + jnp.concatenate([d[:1], d[:-1]], axis=0))
-    lower_ref[1] = 2.0 / (d + roll(d, 1, 1))
-    lower_ref[2] = 2.0 / (d + roll(d, 1, 2))
+class Operator:
+    def __init__(self, move, coef, vec):
+        self.move, self.coef, self.vec = move, coef, vec
+
+    def set(self, a, b, faces, d, before, after, source, inside=None):
+        move = self.move
+        lz, uz, lx, ux = faces
+        ly = 2.0 / (d + jnp.where(before > 0.0, before, d))
+        uy = 2.0 / (d + jnp.where(after > 0.0, after, d))
+        total = lz + uz + lx + ux + ly + uy
+        inverse = 1.0 / total
+        if inside is not None:
+            inverse = jnp.where(inside, inverse, 0.0)
+        self.coef[0, a:b] = jnp.where(move.z_low, 0.0, inverse * lz)
+        self.coef[1, a:b] = jnp.where(move.z_high, 0.0, inverse * uz)
+        self.coef[2, a:b] = jnp.where(move.x_low, 0.0, inverse * lx)
+        self.coef[3, a:b] = jnp.where(move.x_high, 0.0, inverse * ux)
+        self.coef[4, a:b] = inverse * ly
+        self.coef[5, a:b] = inverse * uy
+        self.vec[0, a:b] = inverse * source
+        return total, ly
+
+    def apply(self, k, a, b):
+        move, coef, vec = self.move, self.coef, self.vec
+        f = vec[k, a:b]
+        out = coef[0, a:b] * move.below_z(f) + coef[1, a:b] * move.above_z(f)
+        out = out + (coef[2, a:b] * move.below_x(f) + coef[3, a:b] * move.above_x(f))
+        return out + (coef[4, a:b] * vec[k, a - 1 : b - 1] + coef[5, a:b] * vec[k, a + 1 : b + 1])
+
+    def add_sums(self, sums, a, b, weight, right):
+        basis = [self.vec[k, a:b] for k in range(ITERS)]
+        basis.append(self.apply(ITERS - 1, a, b))
+        gaps = [basis[k] - basis[k + 1] for k in range(ITERS)]
+        scaled = [weight * gap for gap in gaps]
+        terms = [basis[(k + 1) // 2] * scaled[k // 2] for k in range(2 * ITERS - 1)]
+        terms += [right * basis[k] for k in range(ITERS)]
+        ladder, level = [basis[0], gaps[0]], gaps
+        while len(level) > 1:
+            level = [level[i] - level[i + 1] for i in range(len(level) - 1)]
+            ladder.append(level[0])
+        terms += [weight * ladder[k // 2] * ladder[(k + 1) // 2] for k in range(2, 2 * ITERS)]
+        return [total + jnp.sum(term, axis=0) for total, term in zip(sums, terms)]
+
+
+SUMS = 2 * ITERS - 1 + ITERS + 2 * ITERS - 2
+
+
+def pieces(a, b, step):
+    return [(i, min(i + step, b)) for i in range(a, b, step)]
+
+
+def inner(k, chunk):
+    return (k + 1, chunk - 1 - k) if chunk - 1 - k > k + 1 else (0, 0)
+
+
+def own_kernel(
+    own_ref, home_ref, density_ref, source_ref, velocity_ref, faces_ref, coef_ref, vec_ref, diag_ref, side_ref, sums_ref, lower_ref,
+    *, ngx, ngz, zl, xl, chunk, step
+):
     move = Shifts(ngx, ngz, zl, xl)
     read = column_reader(own_ref, ngx * ngz, chunk)
     for k in range(chunk):
@@ -205,13 +260,30 @@
             velocity_ref[f, k : k + 1] = v
         for f, v in enumerate(shared_faces(move, d)):
             faces_ref[f, k : k + 1] = v
+    operator = Operator(move, coef_ref, vec_ref)
+    for a, b in pieces(*inner(0, chunk), step):
+        faces = [faces_ref[f, a:b] for f in range(4)]
+        d, before, after = density_ref[a:b], density_ref[a - 1 : b - 1], density_ref[a + 1 : b + 1]
+        diag_ref[a:b], side_ref[a:b] = operator.set(a, b, faces, d, before, after, source_ref[a:b])
+    for k in range(1, ITERS):
+        for a, b in pieces(*inner(k, chunk), step):
+            vec_ref[k, a:b] = operator.apply(k - 1, a, b)
+    sums = [jnp.zeros(sums_ref.shape[1:], F32)] * SUMS
+    for a, b in pieces(*inner(ITERS, chunk), step):
+        sums = operator.add_sums(sums, a, b, diag_ref[a:b], source_ref[a:b])
+    for k, value in enumerate(sums):
+        sums_ref[k] = value
+    d = home_ref[...]
+    lower_ref[0] = 2.0 / (d + jnp.concatenate([d[:1], d[:-1]], axis=0))
+    lower_ref[1] = 2.0 / (d + roll(d, 1, 1))
+    lower_ref[2] = 2.0 / (d + roll(d, 1, 2))
 
 
 def krylov_kernel(*refs, ngx, ngz, zl, xl, chunk, hops, margin, step, places, runs):
-    density_ref, source_ref, velocity_ref, faces_ref = refs[:4]
+    density_ref, source_ref, velocity_ref, faces_ref, own_coef, own_vec, own_diag, own_side, own_sums = refs[:9]
     count = 2 * hops + runs
-    swapped = refs[4 : 4 + count]
-    basis_ref, lower_ref, sums_ref, sides, dens, coef, vec, diag, source = refs[4 + count :]
+    swapped = refs[9 : 9 + count]
+    vec, lower_ref, sums_ref, sides, dens, coef, diag, source = refs[9 + count :]
     S, L = ngx * ngz, zl * xl
     E = chunk + 2 * HALO
     move = Shifts(ngx, ngz, zl, xl)
@@ -240,8 +312,12 @@
         def _():
             sides[other, h] = jnp.zeros(sides.shape[2:], F32)
 
-    def pieces(a, b):
-        return [(i, min(i + step, b)) for i in range(a, b, step)]
+    def ring(k):
+        low, high = inner(k, chunk)
+        if low == high:
+            return pieces(1 + k, E - 1 - k, step)
+        low, high = HALO + low, HALO + high
+        return pieces(1 + k, low, step) + pieces(high, E - 1 - k, step)
 
     def outer(j, up):
         hop, at = j // chunk, j % chunk
@@ -257,73 +333,40 @@
         dens[HALO - 1 - j], low_rhs = outer(j, 0)
         dens[HALO + chunk + j], high_rhs = outer(j, 1)
         source[HALO - 1 - j], source[HALO + chunk + j] = low_rhs, high_rhs
-    for a, b in pieces(0, chunk):
-        dens[HALO + a : HALO + b] = density_ref[a:b]
-        source[HALO + a : HALO + b] = source_ref[a:b]
+    dens[HALO : HALO + chunk] = density_ref[...]
+    source[HALO : HALO + chunk] = source_ref[...]
     top = HALO + chunk - 1
     source[top] = source[top] - sides[1, 0, 2 * margin]
-
-    spans = pieces(1, HALO) + pieces(HALO, HALO + chunk) + pieces(HALO + chunk, E - 1)
-    for a, b in spans:
-        d, before, after = dens[a:b], dens[a - 1 : b - 1], dens[a + 1 : b + 1]
-        owned = a >= HALO and b <= HALO + chunk
-        inside = d > 0.0
-        if owned:
-            lz, uz, lx, ux = (faces_ref[f, a - HALO : b - HALO] for f in range(4))
-        else:
-            d = jnp.where(inside, d, 1.0)
-            lz, uz, lx, ux = shared_faces(move, d)
-        ly = 2.0 / (d + jnp.where(before > 0.0, before, d))
-        uy = 2.0 / (d + jnp.where(after > 0.0, after, d))
-        total = lz + uz + lx + ux + ly + uy
-        inverse = 1.0 / total
-        if owned:
-            diag[a - HALO : b - HALO] = total
-            lower_ref[a - HALO : b - HALO] = ly
-        else:
-            inverse = jnp.where(inside, inverse, 0.0)
-        coef[0, a:b] = jnp.where(move.z_low, 0.0, inverse * lz)
-        coef[1, a:b] = jnp.where(move.z_high, 0.0, inverse * uz)
-        coef[2, a:b] = jnp.where(move.x_low, 0.0, inverse * lx)
-        coef[3, a:b] = jnp.where(move.x_high, 0.0, inverse * ux)
-        coef[4, a:b] = inverse * ly
-        coef[5, a:b] = inverse * uy
-        vec[0, a:b] = inverse * source[a:b]
-
-    def applied(k, a, b):
-        f = vec[k, a:b]
-        out = coef[0, a:b] * move.below_z(f) + coef[1, a:b] * move.above_z(f)
-        out = out + (coef[2, a:b] * move.below_x(f) + coef[3, a:b] * move.above_x(f))
-        return out + (coef[4, a:b] * vec[k, a - 1 : b - 1] + coef[5, a:b] * vec[k, a + 1 : b + 1])
-
+    for k in range(ITERS):
+        a, b = inner(k, chunk)
+        if a < b:
+            vec[k, HALO + a : HALO + b] = own_vec[k, a:b]
+    a, b = inner(0, chunk)
+    if a < b:
+        coef[:, HALO + a : HALO + b] = own_coef[:, a:b]
+        lower_ref[a:b], diag[a:b] = own_side[a:b], own_diag[a:b]
+
+    operator = Operator(move, coef, vec)
+    for start, stop in ring(0):
+        edges = sorted({start, stop, *(e for e in (HALO, HALO + chunk) if start < e < stop)})
+        for a, b in zip(edges[:-1], edges[1:]):
+            d, before, after = dens[a:b], dens[a - 1 : b - 1], dens[a + 1 : b + 1]
+            if HALO <= a < HALO + chunk:
+                own = slice(a - HALO, b - HALO)
+                faces = [faces_ref[f, own] for f in range(4)]
+                diag[own], lower_ref[own] = operator.set(a, b, faces, d, before, after, source[a:b])
+            else:
+                inside = d > 0.0
+                d = jnp.where(inside, d, 1.0)
+                operator.set(a, b, shared_faces(move, d), d, before, after, source[a:b], inside)
     for k in range(1, ITERS):
-        for a, b in pieces(1 + k, E - 1 - k):
-            vec[k, a:b] = applied(k - 1, a, b)
-
-    count = 2 * ITERS - 1
-    powers = [0.0] * count
-    firsts = [0.0] * ITERS
-    steps = [0.0] * (count + 1)
-    for a, b in pieces(HALO, HALO + chunk):
-        own = slice(a - HALO, b - HALO)
-        basis = [vec[k, a:b] for k in range(ITERS)]
-        basis.append(applied(ITERS - 1, a, b))
-        weight, right = diag[own], source[a:b]
-        gaps = [basis[k] - basis[k + 1] for k in range(ITERS)]
-        scaled = [weight * gap for gap in gaps]
-        for k in range(count):
-            powers[k] = powers[k] + jnp.sum(basis[(k + 1) // 2] * scaled[k // 2], axis=0)
-        for k in range(ITERS):
-            firsts[k] = firsts[k] + jnp.sum(right * basis[k], axis=0)
-        ladder, level = [basis[0], gaps[0]], gaps
-        while len(level) > 1:
-            level = [level[i] - level[i + 1] for i in range(len(level) - 1)]
-            ladder.append(level[0])
-        for k in range(2, count + 1):
-            steps[k] = steps[k] + jnp.sum(weight * ladder[k // 2] * ladder[(k + 1) // 2], axis=0)
-    steps[0], steps[1] = firsts[0], powers[0]
-    for k in range(ITERS):
-        basis_ref[k] = vec[k, HALO - 1 : HALO + chunk]
+        for a, b in ring(k):
+            vec[k, a:b] = operator.apply(k - 1, a, b)
+    sums = [own_sums[k] for k in range(SUMS)]
+    for a, b in ring(ITERS):
+        sums = operator.add_sums(sums, a, b, diag[a - HALO : b - HALO], source[a:b])
+    powers, firsts = sums[: 2 * ITERS - 1], sums[2 * ITERS - 1 : 3 * ITERS - 1]
+    steps = [firsts[0], powers[0]] + sums[3 * ITERS - 1 :]
 
     columns = powers + firsts + steps
     rows = [jnp.sum(c, axis=0, keepdims=True) for c in columns]
@@ -394,7 +437,7 @@
     by_step = [v.reshape(1, 1, 1) for v in by_step]
     for a in range(0, chunk + 1, step):
         b = min(a + step, chunk + 1)
-        level = [basis_ref[k, a:b] for k in range(ITERS)]
+        level = [basis_ref[k, HALO - 1 + a : HALO - 1 + b] for k in range(ITERS)]
         value = 0.0
         for k in range(ITERS):
             value = value + by_power[k] * level[k]
@@ -531,13 +574,14 @@
 
         vmem = pl.BlockSpec(memory_space=pltpu.VMEM)
 
-        def call(body, specs, out, scratch=(), **kwargs):
+        def call(body, specs, out, scratch=(), limit=None, **kwargs):
             kernel = pl.pallas_call(
                 lambda *refs: body(*refs, **kwargs),
                 in_specs=specs,
                 out_specs=jax.tree.map(lambda _: vmem, out),
                 out_shape=out,
                 scratch_shapes=[pltpu.VMEM(s, F32) for s in scratch],
+                compiler_params=pltpu.CompilerParams(vmem_limit_bytes=limit),
                 name=body.__name__,
             )
 
@@ -575,20 +619,25 @@
         if runs:
             swaps = [swaps[0]] + [(messages[1], run_swaps(places, 2 * S, start)) for start in (0, S)]
         swapped = [lax.ppermute(value, every, pairs) for value, pairs in swaps[::-1]][::-1]
-        density, source, velocities, faces, home_lower = call(
+        *own_values, home_lower = call(
             own_kernel,
             [vmem] * 2,
-            (placed(chunk, S, L), placed(chunk, S, L), placed(3, chunk, S, L), placed(4, chunk, S, L), placed(3, *block)),
-            **sizes,
+            (
+                *[placed(*lead, chunk, S, L) for lead in ((), (), (3,), (4,), (6,), (ITERS,), (), ())],
+                placed(SUMS, S, L),
+                placed(3, *block),
+            ),
+            limit=VMEM_LIMIT, step=step, **sizes,
         )(own, home_density)
+        velocities, faces = own_values[2:4]
         wide = chunk + 2 * HALO
         basis, lower, sums = call(
             krylov_kernel,
-            [vmem] * (4 + len(swapped)),
-            (placed(ITERS, chunk + 1, S, L), placed(chunk, S, L), placed(devices, LANES)),
-            ((2, hops) + message, (wide, S, L), (6, wide, S, L), (ITERS, wide, S, L), (chunk, S, L), (wide, S, L)),
-            hops=hops, margin=margin, step=step, places=devices, runs=int(runs), **sizes,
-        )(density, source, velocities, faces, *swapped)
+            [vmem] * (9 + len(swapped)),
+            (placed(ITERS, wide, S, L), placed(chunk, S, L), placed(devices, LANES)),
+            ((2, hops) + message, (wide, S, L), (6, wide, S, L), (chunk, S, L), (wide, S, L)),
+            limit=VMEM_LIMIT, hops=hops, margin=margin, step=step, places=devices, runs=int(runs), **sizes,
+        )(*own_values, *swapped)
         sums = lax.all_to_all(sums, every, 0, 0, tiled=True)
         height = Slot(zl, xl, chunk).height
         packed = call(

time: 40.8 us -> 40.6 us (level)
  transfers between devices with their start and end apart: 3 -> 3, of which waited for: 1 -> 1; matrix products, arithmetic and copies ran while one was open for 0% -> 0% of each run, Pallas kernels for 1% -> 2%
where the time goes in v7:
time: 40.6 us; the launch traced here: 40.4 us
  blocking collectives  29.9 us (74%)
  Pallas kernels  5.11 us (13%)
  starting transfers between devices  3.33 us (8%)
  waiting for transfers between devices  1.36 us (3%)
  between operations  0.67 us (2%)
    all_to_all x1, blocking collectives, local(): pencils = lax.all_to_all(blocks, ('gz', 'gx'), 0, 0, tiled=True)  11.3 us
    all_to_all x1, blocking collectives, local(): sums = lax.all_to_all(sums, every, 0, 0, tiled=True)  10.8 us
    all_to_all x1, blocking collectives, local(): lax.all_to_all(packed.reshape(S, height, LANES), ('gz', 'gx'), 0, 0, tile...  7.8 us
    pallas_call x6, Pallas kernels, run(): kernel(*[near(a) if spec is vmem else a for a, spec in zip(args, specs)])  5.11 us
    ppermute x3, starting transfers between devices, local(): lax.ppermute(value, every, pairs)  3.33 us
    ppermute x3, waiting for transfers between devices, local(): lax.ppermute(value, every, pairs)  1.36 us
  transfers between devices with their start and end apart: 3, of which 1 were waited for; matrix products, arithmetic and copies ran while one was open for 0% of the time, Pallas kernels for 2%

profile of v7, /device:TPU:0, one launch (start us, length us, event | category | flops | bytes accessed | tf_op | source)
XLA Modules:
  0.0 40.4 jit_solution(7819370345295803146)
XLA Ops:
  0.6 1.2 %pack_kernel.1 = (f32[8,64,128]{2,1,0:T(8,128)S(1)}, f32[8,16,128]{2,1,0:T(8,128)S(1)}, f32[8,16,128]{2,1,0:T(8,128)S(1)}, f32[3,8,16,128]{3,2,1,0:T(8,128)S(1)}) custom-call(s32[8,16,128]{2,1,0:T(8,128)} %refs_0_.1, f32[8,16,128]{2,1,0:T(8,128)} %refs_1_.1, f32[3,8,16,128]{3,2,1,0:T(8,128)} %refs_2_.1, f32[4,8]{1,0:T(4,128)} %bitcast.14, f32[4,8]{1,0:T(4,128)} %bitcast.15, ...), custom_call_target="tpu_custom_call" | custom-call | tf_op jit(solution)/shard_map/pack_kernel/pallas_call | solution.py:589
  1.8 11.3 %all_to_all.21 = f32[8,64,128]{2,1,0:T(8,128)S(1)} all-to-all(f32[8,64,128]{2,1,0:T(8,128)S(1)} %get-tuple-element.21), channel_id=1, replica_groups=mesh['gx'=2,'gy'=4,'gz'=4] {'gz','gx'}, dimensions={0} | all-to-all | bytes 524288 | tf_op jit(solution)/shard_map/all_to_all | solution.py:611
  13.2 0.1 edges_kernel.1
  13.3 0.2 collective-permute-start
  13.5 0.4 collective-permute-start.2
  13.9 2.8 %collective-permute-start.1 = (f32[11,8,128]{2,1,0:T(8,128)S(1)}, f32[11,8,128]{2,1,0:T(8,128)S(1)}, u32[]{:S(2)}, u32[]{:S(2)}) collective-permute-start(f32[11,8,128]{2,1,0:T(8,128)S(1)} %get-tuple-element.33), channel_id=1, source_target_pairs={{0,4},{1,2},{3,19},{18,17},{16,20},{21,22},{23,7},{6,5},{8,12},{9,... | collective-permute-start | bytes 135176 | tf_op jit(solution)/shard_map/ppermute | solution.py:621
  16.6 0.6 %own_kernel.1 = (f32[16,8,128]{2,1,0:T(8,128)S(1)}, f32[16,8,128]{2,1,0:T(8,128)S(1)}, f32[3,16,8,128]{3,2,1,0:T(8,128)S(1)}, f32[4,16,8,128]{3,2,1,0:T(8,128)S(...) custom-call(f32[512,128]{1,0:T(8,128)S(1)} %bitcast.10, ...), custom_call_target="tpu_custom_call" | custom-call | tf_op jit(solution)/shard_map/own_kernel/pallas_call | solution.py:589
  17.3 0.0 collective-permute-done.refs_9_
  17.3 0.0 collective-permute-done.2.refs_11_
  17.3 1.4 %collective-permute-done.1.refs_10_ = f32[11,8,128]{2,1,0:T(8,128)S(1)} collective-permute-done((f32[11,8,128]{2,1,0:T(8,128)S(1)}, f32[11,8,128]{2,1,0:T(8,128)S(1)}, u32[]{:S(2)}, u32[]{:S(2)}) %collective-permute-start.1) | collective-permute-done | bytes 45088 | tf_op jit(solution)/shard_map/ppermute | solution.py:621
  18.7 0.6 %krylov_kernel.1 = (f32[4,26,8,128]{3,2,1,0:T(8,128)S(1)}, f32[16,8,128]{2,1,0:T(8,128)S(1)}, f32[32,128]{1,0:T(8,128)S(1)}) custom-call(f32[16,8,128]{2,1,0:T(8,128)S(1)} %get-tuple-element.23.refs_0_, f32[16,8,128]{2,1,0:T(8,128)S(1)} %get-tuple-element.24.refs_1_, f32[3,16,8,128]{3,2,1,0:T(8,128)S(1)} %get-tuple-element.25.refs_2_.refs_4_, ...), custom_call_target="tpu_custom_call" | custom-call | tf_op jit(solution)/shard_map/krylov_kernel/pallas_call | solution.py:589
  19.3 10.8 %all_to_all.22 = f32[32,1,128]{2,1,0:T(1,128)S(1)} all-to-all(f32[32,1,128]{2,1,0:T(1,128)S(1)} %bitcast.13), channel_id=1, replica_groups=mesh['gx'=2,'gy'=4,'gz'=4] {'gx','gy','gz'}, dimensions={0} | all-to-all | bytes 32768 | tf_op jit(solution)/shard_map/all_to_all | solution.py:641
  30.1 1.5 %render_kernel.1 = f32[320,128]{1,0:T(8,128)S(1)} custom-call(f32[32,128]{1,0:T(8,128)S(1)} %bitcast.12, f32[4,26,8,128]{3,2,1,0:T(8,128)S(1)} %get-tuple-element.35.refs_1_, f32[4,16,8,128]{3,2,1,0:T(8,128)S(1)} %get-tuple-element.26.refs_3_.refs_2_, f32[16,8,128]{2,1,0:T(8,128)S(1)} %get-tuple-element.36.refs_3_, ...), custom_call_target="tpu_custom_call" | custom-call | tf_op jit(solution)/shard_map/render_kernel/pallas_call | solution.py:589
  31.6 7.8 %all_to_all.23.refs_0_ = f32[8,40,128]{2,1,0:T(8,128)S(1)} all-to-all(f32[8,40,128]{2,1,0:T(8,128)S(1)} %bitcast.11), channel_id=1, replica_groups=mesh['gx'=2,'gy'=4,'gz'=4] {'gz','gx'}, dimensions={0} | all-to-all | bytes 327680 | tf_op jit(solution)/shard_map/all_to_all | solution.py:650
  39.4 1.0 %unpack_kernel.1 = (f32[3,8,16,128]{3,2,1,0:T(8,128)}, f32[2,4,16,128]{3,2,1,0:T(8,128)}) custom-call(f32[8,40,128]{2,1,0:T(8,128)S(1)} %all_to_all.23.refs_0_, f32[3,8,16,128]{3,2,1,0:T(8,128)S(1)} %get-tuple-element.38.refs_1_, f32[3,8,16,128]{3,2,1,0:T(8,128)S(1)} %get-tuple-element.39.refs_2_), custom_call_target="tpu_custom_call" | custom-call | tf_op jit(solution)/shard_map/unpack_kernel/pallas_call | solution.py:589
Async XLA Ops:
  13.3 4.0 %collective-permute-start = (f32[11,8,128]{2,1,0:T(8,128)S(1)}, f32[11,8,128]{2,1,0:T(8,128)S(1)}, u32[]{:S(2)}, u32[]{:S(2)}) collective-permute-start(f32[11,8,128]{2,1,0:T(8,128)S(1)} %get-tuple-element.32), channel_id=1, source_target_pairs={{0,1},{2,3},{19,18},{17,16},{20,21},{22,23},{7,6},{5,4},{8,9},{10,... | collective-permute-start | bytes 135176 | tf_op jit(solution)/shard_map/ppermute | solution.py:621
  13.5 3.8 %collective-permute-start.2 = (f32[11,8,128]{2,1,0:T(8,128)S(1)}, f32[11,8,128]{2,1,0:T(8,128)S(1)}, u32[]{:S(2)}, u32[]{:S(2)}) collective-permute-start(f32[11,8,128]{2,1,0:T(8,128)S(1)} %get-tuple-element.33), channel_id=1, source_target_pairs={{20,24},{21,22},{23,7},{6,5},{4,8},{9,10},{11,27},{26,25},{0,1},{2... | collective-permute-start | bytes 135176 | tf_op jit(solution)/shard_map/ppermute | solution.py:621
  13.9 4.8 %collective-permute-start.1 = (f32[11,8,128]{2,1,0:T(8,128)S(1)}, f32[11,8,128]{2,1,0:T(8,128)S(1)}, u32[]{:S(2)}, u32[]{:S(2)}) collective-permute-start(f32[11,8,128]{2,1,0:T(8,128)S(1)} %get-tuple-element.33), channel_id=1, source_target_pairs={{0,4},{1,2},{3,19},{18,17},{16,20},{21,22},{23,7},{6,5},{8,12},{9,... | collective-permute-start | bytes 135176 | tf_op jit(solution)/shard_map/ppermute | solution.py:621

commit v8 on v7

--- a/solution.py
+++ b/solution.py
@@ -191,6 +191,15 @@
     )
 
 
+def differences(levels):
+    basis, gaps = [], []
+    while len(levels) > 1:
+        basis.append(levels[0])
+        gaps.append(levels[1])
+        levels = [levels[i] - levels[i + 1] for i in range(len(levels) - 1)]
+    return basis + levels, gaps
+
+
 class Operator:
     def __init__(self, move, coef, vec):
         self.move, self.coef, self.vec = move, coef, vec
@@ -210,28 +219,28 @@
         self.coef[3, a:b] = jnp.where(move.x_high, 0.0, inverse * ux)
         self.coef[4, a:b] = inverse * ly
         self.coef[5, a:b] = inverse * uy
+        rim = jnp.where(move.z_low, lz, 0.0) + jnp.where(move.z_high, uz, 0.0)
+        rim = rim + (jnp.where(move.x_low, lx, 0.0) + jnp.where(move.x_high, ux, 0.0))
+        self.coef[6, a:b] = inverse * rim
         self.vec[0, a:b] = inverse * source
         return total, ly
 
     def apply(self, k, a, b):
         move, coef, vec = self.move, self.coef, self.vec
         f = vec[k, a:b]
-        out = coef[0, a:b] * move.below_z(f) + coef[1, a:b] * move.above_z(f)
-        out = out + (coef[2, a:b] * move.below_x(f) + coef[3, a:b] * move.above_x(f))
-        return out + (coef[4, a:b] * vec[k, a - 1 : b - 1] + coef[5, a:b] * vec[k, a + 1 : b + 1])
+        out = coef[0, a:b] * (f - move.below_z(f)) + coef[1, a:b] * (f - move.above_z(f))
+        out = out + (coef[2, a:b] * (f - move.below_x(f)) + coef[3, a:b] * (f - move.above_x(f)))
+        out = out + (coef[4, a:b] * (f - vec[k, a - 1 : b - 1]) + coef[5, a:b] * (f - vec[k, a + 1 : b + 1]))
+        return out + coef[6, a:b] * f
 
     def add_sums(self, sums, a, b, weight, right):
-        basis = [self.vec[k, a:b] for k in range(ITERS)]
-        basis.append(self.apply(ITERS - 1, a, b))
-        gaps = [basis[k] - basis[k + 1] for k in range(ITERS)]
+        levels = [self.vec[k, a:b] for k in range(ITERS)]
+        levels.append(self.apply(ITERS - 1, a, b))
+        basis, gaps = differences(levels)
         scaled = [weight * gap for gap in gaps]
         terms = [basis[(k + 1) // 2] * scaled[k // 2] for k in range(2 * ITERS - 1)]
         terms += [right * basis[k] for k in range(ITERS)]
-        ladder, level = [basis[0], gaps[0]], gaps
-        while len(level) > 1:
-            level = [level[i] - level[i + 1] for i in range(len(level) - 1)]
-            ladder.append(level[0])
-        terms += [weight * ladder[k // 2] * ladder[(k + 1) // 2] for k in range(2, 2 * ITERS)]
+        terms += [weight * levels[k // 2] * levels[(k + 1) // 2] for k in range(2, 2 * ITERS)]
         return [total + jnp.sum(term, axis=0) for total, term in zip(sums, terms)]
 
 
@@ -424,7 +433,7 @@
 
 
 def render_kernel(
-    sums_ref, basis_ref, faces_ref, lower_ref, velocity_ref, table_ref, out_ref, press, flat, turned, parts,
+    sums_ref, vec_ref, faces_ref, lower_ref, velocity_ref, table_ref, out_ref, press, flat, turned,
     *, ngx, ngz, zl, xl, chunk, step
 ):
     S, L = ngx * ngz, zl * xl
@@ -437,14 +446,11 @@
     by_step = [v.reshape(1, 1, 1) for v in by_step]
     for a in range(0, chunk + 1, step):
         b = min(a + step, chunk + 1)
-        level = [basis_ref[k, HALO - 1 + a : HALO - 1 + b] for k in range(ITERS)]
+        levels = [vec_ref[k, HALO - 1 + a : HALO - 1 + b] for k in range(ITERS)]
+        basis = differences(levels)[0]
         value = 0.0
         for k in range(ITERS):
-            value = value + by_power[k] * level[k]
-        value = value + by_step[0] * level[0]
-        for k in range(1, ITERS):
-            level = [level[i] - level[i + 1] for i in range(len(level) - 1)]
-            value = value + by_step[k] * level[0]
+            value = value + by_power[k] * basis[k] + by_step[k] * levels[k]
         press[a:b] = value
     spot = lax.broadcasted_iota(jnp.int32, (S, L), 1)
     sides = [jnp.zeros((S, L), F32) for _ in range(slot.deep)]
@@ -481,7 +487,7 @@
     functions = table_ref.shape[0] // ngz
     lane = lax.broadcasted_iota(jnp.int32, (xl, yl), 1)
 
-    def curve_sums(index, carry):
+    def curve_sums(index):
         rows = [jnp.broadcast_to(table_ref[index, r : r + 1, :], (xl, yl)) for r in range(9)]
         rates, bases, gain = rows[:4], rows[4:8], rows[8]
         through = jnp.ones((xl, yl), F32)
@@ -493,15 +499,12 @@
             weight = through * opacity
             colors = [colors[c] + weight * curves[c] for c in range(3)]
             through = through * (1.0 - opacity)
-        for c, value in enumerate(colors + [through]):
-            parts[index, c] = value
-        return carry
-
-    lax.fori_loop(0, table_ref.shape[0], curve_sums, 0)
+        return colors + [through]
+
     for i in range(ngz):
         images = [jnp.zeros((xl, LANES), F32) for _ in range(ngx)]
         for t in range(functions):
-            planes = [parts[i * functions + t, c] for c in range(4)]
+            planes = curve_sums(i * functions + t)
             span = 1
             while span < ngz:
                 behind = [roll(plane, -span * group, 1) for plane in planes]
@@ -623,7 +626,7 @@
             own_kernel,
             [vmem] * 2,
             (
-                *[placed(*lead, chunk, S, L) for lead in ((), (), (3,), (4,), (6,), (ITERS,), (), ())],
+                *[placed(*lead, chunk, S, L) for lead in ((), (), (3,), (4,), (7,), (ITERS,), (), ())],
                 placed(SUMS, S, L),
                 placed(3, *block),
             ),
@@ -631,11 +634,11 @@
         )(own, home_density)
         velocities, faces = own_values[2:4]
         wide = chunk + 2 * HALO
-        basis, lower, sums = call(
+        levels, lower, sums = call(
             krylov_kernel,
             [vmem] * (9 + len(swapped)),
             (placed(ITERS, wide, S, L), placed(chunk, S, L), placed(devices, LANES)),
-            ((2, hops) + message, (wide, S, L), (6, wide, S, L), (chunk, S, L), (wide, S, L)),
+            ((2, hops) + message, (wide, S, L), (7, wide, S, L), (chunk, S, L), (wide, S, L)),
             limit=VMEM_LIMIT, hops=hops, margin=margin, step=step, places=devices, runs=int(runs), **sizes,
         )(*own_values, *swapped)
         sums = lax.all_to_all(sums, every, 0, 0, tiled=True)
@@ -644,9 +647,9 @@
             render_kernel,
             [vmem] * 6,
             placed(S * height, LANES),
-            ((chunk + 1, S, L), (yl, L), (zl, xl, yl), (curves.shape[0], 4, xl, yl)),
+            ((chunk + 1, S, L), (yl, L), (zl, xl, yl)),
             step=step, **sizes,
-        )(sums, basis, faces, lower, velocities, curves)
+        )(sums, levels, faces, lower, velocities, curves)
         home = lax.all_to_all(packed.reshape(S, height, LANES), ("gz", "gx"), 0, 0, tiled=True)
         return call(
             unpack_kernel,

time: 40.6 us -> 40.4 us (level)
  no operation moved by 1% of the time
where the time goes in v8:
time: 40.4 us; the launch traced here: 40.2 us
  blocking collectives  29.9 us (74%)
  Pallas kernels  4.86 us (12%)
  starting transfers between devices  3.33 us (8%)
  waiting for transfers between devices  1.37 us (3%)
  between operations  0.67 us (2%)
    all_to_all x1, blocking collectives, local(): pencils = lax.all_to_all(blocks, ('gz', 'gx'), 0, 0, tiled=True)  11.3 us
    all_to_all x1, blocking collectives, local(): sums = lax.all_to_all(sums, every, 0, 0, tiled=True)  10.8 us
    all_to_all x1, blocking collectives, local(): lax.all_to_all(packed.reshape(S, height, LANES), ('gz', 'gx'), 0, 0, tile...  7.81 us
    pallas_call x6, Pallas kernels, run(): kernel(*[near(a) if spec is vmem else a for a, spec in zip(args, specs)])  4.86 us
    ppermute x3, starting transfers between devices, local(): lax.ppermute(value, every, pairs)  3.33 us
    ppermute x3, waiting for transfers between devices, local(): lax.ppermute(value, every, pairs)  1.37 us
  transfers between devices with their start and end apart: 3, of which 1 were waited for; matrix products, arithmetic and copies ran while one was open for 0% of the time, Pallas kernels for 2%

profile of v8, /device:TPU:0, one launch (start us, length us, event | category | flops | bytes accessed | tf_op | source)
XLA Modules:
  0.0 40.2 jit_solution(11427033745396769404)
XLA Ops:
  0.6 1.2 %pack_kernel.1 = (f32[8,64,128]{2,1,0:T(8,128)S(1)}, f32[8,16,128]{2,1,0:T(8,128)S(1)}, f32[8,16,128]{2,1,0:T(8,128)S(1)}, f32[3,8,16,128]{3,2,1,0:T(8,128)S(1)}) custom-call(s32[8,16,128]{2,1,0:T(8,128)} %refs_0_.1, f32[8,16,128]{2,1,0:T(8,128)} %refs_1_.1, f32[3,8,16,128]{3,2,1,0:T(8,128)} %refs_2_.1, f32[4,8]{1,0:T(4,128)} %bitcast.14, f32[4,8]{1,0:T(4,128)} %bitcast.15, ...), custom_call_target="tpu_custom_call" | custom-call | tf_op jit(solution)/shard_map/pack_kernel/pallas_call | solution.py:592
  1.8 11.3 %all_to_all.21 = f32[8,64,128]{2,1,0:T(8,128)S(1)} all-to-all(f32[8,64,128]{2,1,0:T(8,128)S(1)} %get-tuple-element.21), channel_id=1, replica_groups=mesh['gx'=2,'gy'=4,'gz'=4] {'gz','gx'}, dimensions={0} | all-to-all | bytes 524288 | tf_op jit(solution)/shard_map/all_to_all | solution.py:614
  13.2 0.1 edges_kernel.1
  13.3 0.2 collective-permute-start
  13.5 0.4 collective-permute-start.2
  13.9 2.8 %collective-permute-start.1 = (f32[11,8,128]{2,1,0:T(8,128)S(1)}, f32[11,8,128]{2,1,0:T(8,128)S(1)}, u32[]{:S(2)}, u32[]{:S(2)}) collective-permute-start(f32[11,8,128]{2,1,0:T(8,128)S(1)} %get-tuple-element.33), channel_id=1, source_target_pairs={{0,4},{1,2},{3,19},{18,17},{16,20},{21,22},{23,7},{6,5},{8,12},{9,... | collective-permute-start | bytes 135176 | tf_op jit(solution)/shard_map/ppermute | solution.py:624
  16.6 0.6 %own_kernel.1 = (f32[16,8,128]{2,1,0:T(8,128)S(1)}, f32[16,8,128]{2,1,0:T(8,128)S(1)}, f32[3,16,8,128]{3,2,1,0:T(8,128)S(1)}, f32[4,16,8,128]{3,2,1,0:T(8,128)S(...) custom-call(f32[512,128]{1,0:T(8,128)S(1)} %bitcast.10, ...), custom_call_target="tpu_custom_call" | custom-call | tf_op jit(solution)/shard_map/own_kernel/pallas_call | solution.py:592
  17.3 0.0 collective-permute-done.refs_9_
  17.3 0.0 collective-permute-done.2.refs_11_
  17.3 1.4 %collective-permute-done.1.refs_10_ = f32[11,8,128]{2,1,0:T(8,128)S(1)} collective-permute-done((f32[11,8,128]{2,1,0:T(8,128)S(1)}, f32[11,8,128]{2,1,0:T(8,128)S(1)}, u32[]{:S(2)}, u32[]{:S(2)}) %collective-permute-start.1) | collective-permute-done | bytes 45088 | tf_op jit(solution)/shard_map/ppermute | solution.py:624
  18.7 0.6 %krylov_kernel.1 = (f32[4,26,8,128]{3,2,1,0:T(8,128)S(1)}, f32[16,8,128]{2,1,0:T(8,128)S(1)}, f32[32,128]{1,0:T(8,128)S(1)}) custom-call(f32[16,8,128]{2,1,0:T(8,128)S(1)} %get-tuple-element.23.refs_0_, f32[16,8,128]{2,1,0:T(8,128)S(1)} %get-tuple-element.24.refs_1_, f32[3,16,8,128]{3,2,1,0:T(8,128)S(1)} %get-tuple-element.25.refs_2_.refs_4_, ...), custom_call_target="tpu_custom_call" | custom-call | tf_op jit(solution)/shard_map/krylov_kernel/pallas_call | solution.py:592
  19.3 10.8 %all_to_all.22 = f32[32,1,128]{2,1,0:T(1,128)S(1)} all-to-all(f32[32,1,128]{2,1,0:T(1,128)S(1)} %bitcast.13), channel_id=1, replica_groups=mesh['gx'=2,'gy'=4,'gz'=4] {'gx','gy','gz'}, dimensions={0} | all-to-all | bytes 32768 | tf_op jit(solution)/shard_map/all_to_all | solution.py:644
  30.1 1.2 %render_kernel.1 = f32[320,128]{1,0:T(8,128)S(1)} custom-call(f32[32,128]{1,0:T(8,128)S(1)} %bitcast.12, f32[4,26,8,128]{3,2,1,0:T(8,128)S(1)} %get-tuple-element.35.refs_1_, f32[4,16,8,128]{3,2,1,0:T(8,128)S(1)} %get-tuple-element.26.refs_3_.refs_2_, f32[16,8,128]{2,1,0:T(8,128)S(1)} %get-tuple-element.36.refs_3_, ...), custom_call_target="tpu_custom_call" | custom-call | tf_op jit(solution)/shard_map/render_kernel/pallas_call | solution.py:592
  31.3 7.8 %all_to_all.23.refs_0_ = f32[8,40,128]{2,1,0:T(8,128)S(1)} all-to-all(f32[8,40,128]{2,1,0:T(8,128)S(1)} %bitcast.11), channel_id=1, replica_groups=mesh['gx'=2,'gy'=4,'gz'=4] {'gz','gx'}, dimensions={0} | all-to-all | bytes 327680 | tf_op jit(solution)/shard_map/all_to_all | solution.py:653
  39.1 1.0 %unpack_kernel.1 = (f32[3,8,16,128]{3,2,1,0:T(8,128)}, f32[2,4,16,128]{3,2,1,0:T(8,128)}) custom-call(f32[8,40,128]{2,1,0:T(8,128)S(1)} %all_to_all.23.refs_0_, f32[3,8,16,128]{3,2,1,0:T(8,128)S(1)} %get-tuple-element.38.refs_1_, f32[3,8,16,128]{3,2,1,0:T(8,128)S(1)} %get-tuple-element.39.refs_2_), custom_call_target="tpu_custom_call" | custom-call | tf_op jit(solution)/shard_map/unpack_kernel/pallas_call | solution.py:592
Async XLA Ops:
  13.3 4.0 %collective-permute-start = (f32[11,8,128]{2,1,0:T(8,128)S(1)}, f32[11,8,128]{2,1,0:T(8,128)S(1)}, u32[]{:S(2)}, u32[]{:S(2)}) collective-permute-start(f32[11,8,128]{2,1,0:T(8,128)S(1)} %get-tuple-element.32), channel_id=1, source_target_pairs={{0,1},{2,3},{19,18},{17,16},{20,21},{22,23},{7,6},{5,4},{8,9},{10,... | collective-permute-start | bytes 135176 | tf_op jit(solution)/shard_map/ppermute | solution.py:624
  13.5 3.8 %collective-permute-start.2 = (f32[11,8,128]{2,1,0:T(8,128)S(1)}, f32[11,8,128]{2,1,0:T(8,128)S(1)}, u32[]{:S(2)}, u32[]{:S(2)}) collective-permute-start(f32[11,8,128]{2,1,0:T(8,128)S(1)} %get-tuple-element.33), channel_id=1, source_target_pairs={{20,24},{21,22},{23,7},{6,5},{4,8},{9,10},{11,27},{26,25},{0,1},{2... | collective-permute-start | bytes 135176 | tf_op jit(solution)/shard_map/ppermute | solution.py:624
  13.9 4.8 %collective-permute-start.1 = (f32[11,8,128]{2,1,0:T(8,128)S(1)}, f32[11,8,128]{2,1,0:T(8,128)S(1)}, u32[]{:S(2)}, u32[]{:S(2)}) collective-permute-start(f32[11,8,128]{2,1,0:T(8,128)S(1)} %get-tuple-element.33), channel_id=1, source_target_pairs={{0,4},{1,2},{3,19},{18,17},{16,20},{21,22},{23,7},{6,5},{8,12},{9,... | collective-permute-start | bytes 135176 | tf_op jit(solution)/shard_map/ppermute | solution.py:624

commit v9 on v8

--- a/solution.py
+++ b/solution.py
@@ -6,6 +6,7 @@
 from jax.experimental import pallas as pl
 from jax.experimental.pallas import tpu as pltpu
 from jax.sharding import PartitionSpec as P
+
 
 ITERS = 4
 HALO = ITERS + 1
@@ -585,7 +586,6 @@
                 out_shape=out,
                 scratch_shapes=[pltpu.VMEM(s, F32) for s in scratch],
                 compiler_params=pltpu.CompilerParams(vmem_limit_bytes=limit),
-                name=body.__name__,
             )
 
             def run(*args):
@@ -621,7 +621,9 @@
         runs = hops == 1 and ngy % 2 == 0 and S % 2 == 0
         if runs:
             swaps = [swaps[0]] + [(messages[1], run_swaps(places, 2 * S, start)) for start in (0, S)]
-        swapped = [lax.ppermute(value, every, pairs) for value, pairs in swaps[::-1]][::-1]
+        swapped = []
+        for value, pairs in swaps:
+            swapped.append(lax.ppermute(value, every, pairs))
         *own_values, home_lower = call(
             own_kernel,
             [vmem] * 2,

time: 40.4 us -> 40.4 us (level)
  no operation moved by 1% of the time
where the time goes in v9:
time: 40.4 us; the launch traced here: 40.2 us
  blocking collectives  29.9 us (74%)
  Pallas kernels  4.86 us (12%)
  starting transfers between devices  3.33 us (8%)
  waiting for transfers between devices  1.37 us (3%)
  between operations  0.67 us (2%)
    all_to_all x1, blocking collectives, local(): pencils = lax.all_to_all(blocks, ('gz', 'gx'), 0, 0, tiled=True)  11.3 us
    all_to_all x1, blocking collectives, local(): sums = lax.all_to_all(sums, every, 0, 0, tiled=True)  10.8 us
    all_to_all x1, blocking collectives, local(): lax.all_to_all(packed.reshape(S, height, LANES), ('gz', 'gx'), 0, 0, tile...  7.81 us
    pallas_call x6, Pallas kernels, run(): kernel(*[near(a) if spec is vmem else a for a, spec in zip(args, specs)])  4.86 us
    ppermute x3, starting transfers between devices, local(): swapped.append(lax.ppermute(value, every, pairs))  3.33 us
    ppermute x3, waiting for transfers between devices, local(): swapped.append(lax.ppermute(value, every, pairs))  1.37 us
  transfers between devices with their start and end apart: 3, of which 1 were waited for; matrix products, arithmetic and copies ran while one was open for 0% of the time, Pallas kernels for 2%

profile of v9, /device:TPU:0, one launch (start us, length us, event | category | flops | bytes accessed | tf_op | source)
XLA Modules:
  0.0 40.2 jit_solution(11427033745396769404)
XLA Ops:
  0.6 1.2 %shard_map.77 = (f32[8,64,128]{2,1,0:T(8,128)S(1)}, f32[8,16,128]{2,1,0:T(8,128)S(1)}, f32[8,16,128]{2,1,0:T(8,128)S(1)}, f32[3,8,16,128]{3,2,1,0:T(8,128)S(1)}) custom-call(s32[8,16,128]{2,1,0:T(8,128)} %refs_0_.1, f32[8,16,128]{2,1,0:T(8,128)} %refs_1_.1, f32[3,8,16,128]{3,2,1,0:T(8,128)} %refs_2_.1, f32[4,8]{1,0:T(4,128)} %bitcast.14, f32[4,8]{1,0:T(4,128)} %bitcast.15, ...), custom_call_target="tpu_custom_call" | custom-call | tf_op jit(solution)/shard_map/pallas_call | solution.py:592
  1.8 11.3 %all_to_all.21 = f32[8,64,128]{2,1,0:T(8,128)S(1)} all-to-all(f32[8,64,128]{2,1,0:T(8,128)S(1)} %get-tuple-element.21), channel_id=1, replica_groups=mesh['gx'=2,'gy'=4,'gz'=4] {'gz','gx'}, dimensions={0} | all-to-all | bytes 524288 | tf_op jit(solution)/shard_map/all_to_all | solution.py:614
  13.2 0.1 shard_map.79
  13.3 0.2 collective-permute-start
  13.5 0.4 collective-permute-start.2
  13.9 2.8 %collective-permute-start.1 = (f32[11,8,128]{2,1,0:T(8,128)S(1)}, f32[11,8,128]{2,1,0:T(8,128)S(1)}, u32[]{:S(2)}, u32[]{:S(2)}) collective-permute-start(f32[11,8,128]{2,1,0:T(8,128)S(1)} %get-tuple-element.33), channel_id=1, source_target_pairs={{0,4},{1,2},{3,19},{18,17},{16,20},{21,22},{23,7},{6,5},{8,12},{9,... | collective-permute-start | bytes 135176 | tf_op jit(solution)/shard_map/ppermute | solution.py:626
  16.6 0.6 %shard_map.78 = (f32[16,8,128]{2,1,0:T(8,128)S(1)}, f32[16,8,128]{2,1,0:T(8,128)S(1)}, f32[3,16,8,128]{3,2,1,0:T(8,128)S(1)}, f32[4,16,8,128]{3,2,1,0:T(8,128)S(...) custom-call(f32[512,128]{1,0:T(8,128)S(1)} %bitcast.10, ...), custom_call_target="tpu_custom_call" | custom-call | tf_op jit(solution)/shard_map/pallas_call | solution.py:592
  17.3 0.0 collective-permute-done.refs_9_
  17.3 0.0 collective-permute-done.2.refs_11_
  17.3 1.4 %collective-permute-done.1.refs_10_ = f32[11,8,128]{2,1,0:T(8,128)S(1)} collective-permute-done((f32[11,8,128]{2,1,0:T(8,128)S(1)}, f32[11,8,128]{2,1,0:T(8,128)S(1)}, u32[]{:S(2)}, u32[]{:S(2)}) %collective-permute-start.1) | collective-permute-done | bytes 45088 | tf_op jit(solution)/shard_map/ppermute | solution.py:626
  18.7 0.6 %shard_map.80 = (f32[4,26,8,128]{3,2,1,0:T(8,128)S(1)}, f32[16,8,128]{2,1,0:T(8,128)S(1)}, f32[32,128]{1,0:T(8,128)S(1)}) custom-call(f32[16,8,128]{2,1,0:T(8,128)S(1)} %get-tuple-element.23.refs_0_, f32[16,8,128]{2,1,0:T(8,128)S(1)} %get-tuple-element.24.refs_1_, f32[3,16,8,128]{3,2,1,0:T(8,128)S(1)} %get-tuple-element.25.refs_2_.refs_4_, ...), custom_call_target="tpu_custom_call" | custom-call | tf_op jit(solution)/shard_map/pallas_call | solution.py:592
  19.3 10.8 %all_to_all.22 = f32[32,1,128]{2,1,0:T(1,128)S(1)} all-to-all(f32[32,1,128]{2,1,0:T(1,128)S(1)} %bitcast.13), channel_id=1, replica_groups=mesh['gx'=2,'gy'=4,'gz'=4] {'gx','gy','gz'}, dimensions={0} | all-to-all | bytes 32768 | tf_op jit(solution)/shard_map/all_to_all | solution.py:646
  30.1 1.2 %shard_map.81 = f32[320,128]{1,0:T(8,128)S(1)} custom-call(f32[32,128]{1,0:T(8,128)S(1)} %bitcast.12, f32[4,26,8,128]{3,2,1,0:T(8,128)S(1)} %get-tuple-element.35.refs_1_, f32[4,16,8,128]{3,2,1,0:T(8,128)S(1)} %get-tuple-element.26.refs_3_.refs_2_, f32[16,8,128]{2,1,0:T(8,128)S(1)} %get-tuple-element.36.refs_3_, ...), custom_call_target="tpu_custom_call" | custom-call | tf_op jit(solution)/shard_map/pallas_call | solution.py:592
  31.3 7.8 %all_to_all.23.refs_0_ = f32[8,40,128]{2,1,0:T(8,128)S(1)} all-to-all(f32[8,40,128]{2,1,0:T(8,128)S(1)} %bitcast.11), channel_id=1, replica_groups=mesh['gx'=2,'gy'=4,'gz'=4] {'gz','gx'}, dimensions={0} | all-to-all | bytes 327680 | tf_op jit(solution)/shard_map/all_to_all | solution.py:655
  39.1 1.0 %shard_map.82 = (f32[3,8,16,128]{3,2,1,0:T(8,128)}, f32[2,4,16,128]{3,2,1,0:T(8,128)}) custom-call(f32[8,40,128]{2,1,0:T(8,128)S(1)} %all_to_all.23.refs_0_, f32[3,8,16,128]{3,2,1,0:T(8,128)S(1)} %get-tuple-element.38.refs_1_, f32[3,8,16,128]{3,2,1,0:T(8,128)S(1)} %get-tuple-element.39.refs_2_), custom_call_target="tpu_custom_call" | custom-call | tf_op jit(solution)/shard_map/pallas_call | solution.py:592
Async XLA Ops:
  13.3 4.0 %collective-permute-start = (f32[11,8,128]{2,1,0:T(8,128)S(1)}, f32[11,8,128]{2,1,0:T(8,128)S(1)}, u32[]{:S(2)}, u32[]{:S(2)}) collective-permute-start(f32[11,8,128]{2,1,0:T(8,128)S(1)} %get-tuple-element.32), channel_id=1, source_target_pairs={{0,1},{2,3},{19,18},{17,16},{20,21},{22,23},{7,6},{5,4},{8,9},{10,... | collective-permute-start | bytes 135176 | tf_op jit(solution)/shard_map/ppermute | solution.py:626
  13.5 3.8 %collective-permute-start.2 = (f32[11,8,128]{2,1,0:T(8,128)S(1)}, f32[11,8,128]{2,1,0:T(8,128)S(1)}, u32[]{:S(2)}, u32[]{:S(2)}) collective-permute-start(f32[11,8,128]{2,1,0:T(8,128)S(1)} %get-tuple-element.33), channel_id=1, source_target_pairs={{20,24},{21,22},{23,7},{6,5},{4,8},{9,10},{11,27},{26,25},{0,1},{2... | collective-permute-start | bytes 135176 | tf_op jit(solution)/shard_map/ppermute | solution.py:626
  13.9 4.8 %collective-permute-start.1 = (f32[11,8,128]{2,1,0:T(8,128)S(1)}, f32[11,8,128]{2,1,0:T(8,128)S(1)}, u32[]{:S(2)}, u32[]{:S(2)}) collective-permute-start(f32[11,8,128]{2,1,0:T(8,128)S(1)} %get-tuple-element.33), channel_id=1, source_target_pairs={{0,4},{1,2},{3,19},{18,17},{16,20},{21,22},{23,7},{6,5},{8,12},{9,... | collective-permute-start | bytes 135176 | tf_op jit(solution)/shard_map/ppermute | solution.py:626

commit v10 on v9

--- a/solution.py
+++ b/solution.py
@@ -72,8 +72,7 @@
     return jnp.where(forward, table[c], table[len(table) - 1 - c])
 
 
-def pack_kernel(phase_ref, thermal_ref, velocity_ref, slope_ref, offset_ref, gain_ref, *outs, table, chunk, depth):
-    out_ref, curves_ref, density_ref, kept_ref = outs
+def pack_kernel(phase_ref, thermal_ref, velocity_ref, out_ref, density_ref, kept_ref, *, table, chunk):
     zl, xl, yl = thermal_ref.shape
     density = (1.0 + 9.0 * phase_ref[...].astype(F32)) * thermal_ref[...]
     density_ref[...] = density
@@ -84,10 +83,6 @@
         for c in range(yl // chunk):
             rows = turned[c * chunk : (c + 1) * chunk]
             out_ref[owner(table, c), pl.ds(f, chunk, stride=FIELDS), :] = rows
-    for t in range(curves_ref.shape[0]):
-        curves_ref[t, 0:4, :] = jnp.broadcast_to(-LOG2E * slope_ref[:, t : t + 1], (4, LANES))
-        curves_ref[t, 4:8, :] = jnp.broadcast_to(-LOG2E * offset_ref[:, t : t + 1], (4, LANES))
-        curves_ref[t, 8:9, :] = jnp.broadcast_to(gain_ref[:, t : t + 1] / depth, (1, LANES))
 
 
 class Slot:
@@ -114,7 +109,7 @@
         lane = lax.broadcasted_iota(jnp.int32, shape, 2)
         sub = lax.broadcasted_iota(jnp.int32, shape, 1)
         z, x = lane // xl, lane % xl
-        gz, gx = sub // ngx, sub % ngx
+        gz, gx = sub % ngz, sub // ngz
         self.z_first, self.z_last = z == 0, z == zl - 1
         self.x_first, self.x_last = x == 0, x == xl - 1
         self.z_low = self.z_first & (gz == 0)
@@ -124,18 +119,18 @@
 
     def below_z(self, f):
         near = roll(f, self.xl, 2)
-        return jnp.where(self.z_first, roll(near, self.ngx, 1), near)
+        return jnp.where(self.z_first, roll(near, 1, 1), near)
 
     def above_z(self, f):
         near = roll(f, -self.xl, 2)
-        return jnp.where(self.z_last, roll(near, -self.ngx, 1), near)
+        return jnp.where(self.z_last, roll(near, -1, 1), near)
 
     def below_x(self, f):
-        far = roll(roll(f, 1 - self.xl, 2), 1, 1)
+        far = roll(roll(f, 1 - self.xl, 2), self.ngz, 1)
         return jnp.where(self.x_first, far, roll(f, 1, 2))
 
     def above_x(self, f):
-        far = roll(roll(f, self.xl - 1, 2), -1, 1)
+        far = roll(roll(f, self.xl - 1, 2), -self.ngz, 1)
         return jnp.where(self.x_last, far, roll(f, -1, 2))
 
 
@@ -257,8 +252,8 @@
 
 
 def own_kernel(
-    own_ref, home_ref, density_ref, source_ref, velocity_ref, faces_ref, coef_ref, vec_ref, diag_ref, side_ref, sums_ref, lower_ref,
-    *, ngx, ngz, zl, xl, chunk, step
+    own_ref, home_ref, slope_ref, offset_ref, gain_ref, density_ref, source_ref, velocity_ref, faces_ref, coef_ref, vec_ref, diag_ref,
+    side_ref, sums_ref, lower_ref, curves_ref, *, ngx, ngz, zl, xl, chunk, step, depth
 ):
     move = Shifts(ngx, ngz, zl, xl)
     read = column_reader(own_ref, ngx * ngz, chunk)
@@ -287,6 +282,10 @@
     lower_ref[0] = 2.0 / (d + jnp.concatenate([d[:1], d[:-1]], axis=0))
     lower_ref[1] = 2.0 / (d + roll(d, 1, 1))
     lower_ref[2] = 2.0 / (d + roll(d, 1, 2))
+    for t in range(curves_ref.shape[0]):
+        curves_ref[t, 0:4, :] = jnp.broadcast_to(-LOG2E * slope_ref[:, t : t + 1], (4, LANES))
+        curves_ref[t, 4:8, :] = jnp.broadcast_to(-LOG2E * offset_ref[:, t : t + 1], (4, LANES))
+        curves_ref[t, 8:9, :] = jnp.broadcast_to(gain_ref[:, t : t + 1] / depth, (1, LANES))
 
 
 def krylov_kernel(*refs, ngx, ngz, zl, xl, chunk, hops, margin, step, places, runs):
@@ -483,7 +482,7 @@
         out_ref[pl.ds(slot.faces + r, S, stride=height), :] = side
     turned[...] = flat[...].T.reshape(zl, xl, yl)
 
-    group = ngx * chunk
+    side = ngz * chunk
     band = LANES // 4
     functions = table_ref.shape[0] // ngz
     lane = lax.broadcasted_iota(jnp.int32, (xl, yl), 1)
@@ -508,18 +507,19 @@
             planes = curve_sums(i * functions + t)
             span = 1
             while span < ngz:
-                behind = [roll(plane, -span * group, 1) for plane in planes]
+                behind = [roll(plane, -span * chunk, 1) for plane in planes]
                 planes = [planes[c] + planes[3] * behind[c] for c in range(3)] + [planes[3] * behind[3]]
                 span *= 2
             planes[3] = 1.0 - planes[3]
-            merged = planes[0]
-            for c in range(1, 4):
-                merged = jnp.where(lane >= c * band, roll(planes[c], c * band, 1), merged)
+            planes = [roll(plane, c * band, 1) for c, plane in enumerate(planes)]
+            here = (lane % band) // chunk == t
             for k in range(ngx):
-                here = (lane % band) // chunk == t
-                images[k] = jnp.where(here, roll(merged, (t - k) * chunk, 1), images[k])
+                merged = planes[0]
+                for c in range(1, 4):
+                    merged = jnp.where((lane + (LANES - k * side) % LANES) % LANES // band == c, planes[c], merged)
+                images[k] = jnp.where(here, roll(merged, t * chunk - k * side, 1), images[k])
         for k in range(ngx):
-            place = (i * ngx + k) * height + slot.images
+            place = (k * ngz + i) * height + slot.images
             out_ref[place : place + xl, :] = images[k]
 
 
@@ -563,7 +563,7 @@
 def solution(mesh):
     ngx, ngy, ngz = mesh.shape["gx"], mesh.shape["gy"], mesh.shape["gz"]
     S, devices = ngx * ngz, ngx * ngy * ngz
-    table = [z * ngx + x for x, z in snake(ngx, ngz)]
+    table = [x * ngz + z for x, z in snake(ngx, ngz)]
     places = chain(ngx, ngy, ngz)
 
     def local(phase_field, thermal, velocity, transfer_slope, transfer_offset, transfer_gain):
@@ -605,13 +605,13 @@
         free = pl.BlockSpec()
         tables = (transfer_slope.T, transfer_offset.T, transfer_gain[None, :])
         block = (zl, xl, yl)
-        blocks, curves, home_density, kept = call(
+        blocks, home_density, kept = call(
             pack_kernel,
-            [free] * 6,
-            (placed(S, chunk * FIELDS, L), placed(transfer_gain.shape[0], 16, LANES), placed(*block), placed(3, *block)),
-            table=table, chunk=chunk, depth=zl * ngz,
-        )(phase_field, thermal, velocity, *tables)
-        pencils = lax.all_to_all(blocks, ("gz", "gx"), 0, 0, tiled=True)
+            [free] * 3,
+            (placed(S, chunk * FIELDS, L), placed(*block), placed(3, *block)),
+            table=table, chunk=chunk,
+        )(phase_field, thermal, velocity)
+        pencils = lax.all_to_all(blocks, ("gx", "gz"), 0, 0, tiled=True)
         every = ("gx", "gy", "gz")
         own = pencils.reshape(-1, L)
         sizes = dict(ngx=ngx, ngz=ngz, zl=zl, xl=xl, chunk=chunk)
@@ -624,16 +624,17 @@
         swapped = []
         for value, pairs in swaps:
             swapped.append(lax.ppermute(value, every, pairs))
-        *own_values, home_lower = call(
+        *own_values, home_lower, curves = call(
             own_kernel,
-            [vmem] * 2,
+            [vmem] * 2 + [free] * 3,
             (
                 *[placed(*lead, chunk, S, L) for lead in ((), (), (3,), (4,), (7,), (ITERS,), (), ())],
                 placed(SUMS, S, L),
                 placed(3, *block),
+                placed(transfer_gain.shape[0], 16, LANES),
             ),
-            limit=VMEM_LIMIT, step=step, **sizes,
-        )(own, home_density)
+            limit=VMEM_LIMIT, step=step, depth=zl * ngz, **sizes,
+        )(own, home_density, *tables)
         velocities, faces = own_values[2:4]
         wide = chunk + 2 * HALO
         levels, lower, sums = call(
@@ -652,7 +653,7 @@
             ((chunk + 1, S, L), (yl, L), (zl, xl, yl)),
             step=step, **sizes,
         )(sums, levels, faces, lower, velocities, curves)
-        home = lax.all_to_all(packed.reshape(S, height, LANES), ("gz", "gx"), 0, 0, tiled=True)
+        home = lax.all_to_all(packed.reshape(S, height, LANES), ("gx", "gz"), 0, 0, tiled=True)
         return call(
             unpack_kernel,
             [vmem] * 3,

time: 40.4 us -> 40.4 us (level)
  waiting for transfers between devices: 1.37 us -> 0.63 us
  local copies, waits for them, and re-layouts: 0 us -> 0.7 us
    ppermute x3, waiting for transfers between devices: 1.37 us -> 0.63 us  [local(): swapped.append(lax.ppermute(value, every, pairs))]
    unnamed x0 -> x6, local copies, waits for them, and re-layouts: none -> 0.7 us
where the time goes in v10:
time: 40.4 us; the launch traced here: 40.1 us
  blocking collectives  30 us (74%)
  Pallas kernels  4.88 us (12%)
  starting transfers between devices  3.29 us (8%)
  local copies, waits for them, and re-layouts  0.7 us (2%)
  between operations  0.67 us (2%)
  waiting for transfers between devices  0.63 us (2%)
    all_to_all x1, blocking collectives, local(): pencils = lax.all_to_all(blocks, ('gx', 'gz'), 0, 0, tiled=True)  11.1 us
    all_to_all x1, blocking collectives, local(): sums = lax.all_to_all(sums, every, 0, 0, tiled=True)  11 us
    all_to_all x1, blocking collectives, local(): lax.all_to_all(packed.reshape(S, height, LANES), ('gx', 'gz'), 0, 0, tile...  7.81 us
    pallas_call x6, Pallas kernels, run(): kernel(*[near(a) if spec is vmem else a for a, spec in zip(args, specs)])  4.88 us
    ppermute x3, starting transfers between devices, local(): swapped.append(lax.ppermute(value, every, pairs))  3.29 us
  transfers between devices with their start and end apart: 3, of which 1 were waited for; matrix products, arithmetic and copies ran while one was open for 0% of the time, Pallas kernels for 2%

profile of v10, /device:TPU:0, one launch (start us, length us, event | category | flops | bytes accessed | tf_op | source)
XLA Modules:
  0.0 40.1 jit_solution(3080320527942006474)
XLA Ops:
  0.6 1.1 %shard_map.77 = (f32[8,64,128]{2,1,0:T(8,128)S(1)}, f32[8,16,128]{2,1,0:T(8,128)S(1)}, f32[3,8,16,128]{3,2,1,0:T(8,128)S(1)}) custom-call(s32[8,16,128]{2,1,0:T(8,128)} %refs_0_.1, f32[8,16,128]{2,1,0:T(8,128)} %refs_1_.1, f32[3,8,16,128]{3,2,1,0:T(8,128)} %refs_2_.1), custom_call_target="tpu_custom_call" | custom-call | tf_op jit(solution)/shard_map/pallas_call | solution.py:592
  1.8 11.1 %all_to_all.21 = f32[8,64,128]{2,1,0:T(8,128)S(1)} all-to-all(f32[8,64,128]{2,1,0:T(8,128)S(1)} %get-tuple-element.21), channel_id=1, replica_groups=mesh['gx'=2,'gy'=4,'gz'=4] {'gx','gz'}, dimensions={0} | all-to-all | bytes 524288 | tf_op jit(solution)/shard_map/all_to_all | solution.py:614
  12.9 0.1 shard_map.79
  13.0 0.1 collective-permute-start
  13.1 0.5 %collective-permute-start.2 = (f32[11,8,128]{2,1,0:T(8,128)S(1)}, f32[11,8,128]{2,1,0:T(8,128)S(1)}, u32[]{:S(2)}, u32[]{:S(2)}) collective-permute-start(f32[11,8,128]{2,1,0:T(8,128)S(1)} %get-tuple-element.33), channel_id=1, source_target_pairs={{20,24},{21,22},{23,7},{6,5},{4,8},{9,10},{11,27},{26,25},{0,1},{2... | collective-permute-start | bytes 135176 | tf_op jit(solution)/shard_map/ppermute | solution.py:626
  13.6 2.7 %collective-permute-start.1 = (f32[11,8,128]{2,1,0:T(8,128)S(1)}, f32[11,8,128]{2,1,0:T(8,128)S(1)}, u32[]{:S(2)}, u32[]{:S(2)}) collective-permute-start(f32[11,8,128]{2,1,0:T(8,128)S(1)} %get-tuple-element.33), channel_id=1, source_target_pairs={{0,4},{1,2},{3,19},{18,17},{16,20},{21,22},{23,7},{6,5},{8,12},{9,... | collective-permute-start | bytes 135176 | tf_op jit(solution)/shard_map/ppermute | solution.py:626
  16.3 0.0 copy-start.1
  16.3 0.0 copy-start
  16.3 0.0 copy-start.2
  16.3 0.7 %copy-done.1 = f32[8,4]{0,1:T(4,128)S(1)} copy-done((f32[8,4]{0,1:T(4,128)S(1)}, f32[8,4]{0,1:T(4,128)}, u32[]{:S(2)}) %copy-start.1) | copy-done | bytes 152
  17.0 0.0 copy-done
  17.0 0.0 copy-done.2
  17.0 0.7 %shard_map.78 = (f32[16,8,128]{2,1,0:T(8,128)S(1)}, f32[16,8,128]{2,1,0:T(8,128)S(1)}, f32[3,16,8,128]{3,2,1,0:T(8,128)S(1)}, f32[4,16,8,128]{3,2,1,0:T(8,128)S(...) custom-call(f32[512,128]{1,0:T(8,128)S(1)} %bitcast.10, ...), custom_call_target="tpu_custom_call" | custom-call | tf_op jit(solution)/shard_map/pallas_call | solution.py:592
  17.7 0.0 collective-permute-done.refs_9_
  17.7 0.0 collective-permute-done.2.refs_11_
  17.7 0.6 %collective-permute-done.1.refs_10_ = f32[11,8,128]{2,1,0:T(8,128)S(1)} collective-permute-done((f32[11,8,128]{2,1,0:T(8,128)S(1)}, f32[11,8,128]{2,1,0:T(8,128)S(1)}, u32[]{:S(2)}, u32[]{:S(2)}) %collective-permute-start.1) | collective-permute-done | bytes 45088 | tf_op jit(solution)/shard_map/ppermute | solution.py:626
  18.4 0.7 %shard_map.80 = (f32[4,26,8,128]{3,2,1,0:T(8,128)S(1)}, f32[16,8,128]{2,1,0:T(8,128)S(1)}, f32[32,128]{1,0:T(8,128)S(1)}) custom-call(f32[16,8,128]{2,1,0:T(8,128)S(1)} %get-tuple-element.23.refs_0_, f32[16,8,128]{2,1,0:T(8,128)S(1)} %get-tuple-element.24.refs_1_, f32[3,16,8,128]{3,2,1,0:T(8,128)S(1)} %get-tuple-element.25.refs_2_.refs_4_, ...), custom_call_target="tpu_custom_call" | custom-call | tf_op jit(solution)/shard_map/pallas_call | solution.py:592
  19.0 11.0 %all_to_all.22 = f32[32,1,128]{2,1,0:T(1,128)S(1)} all-to-all(f32[32,1,128]{2,1,0:T(1,128)S(1)} %bitcast.13), channel_id=1, replica_groups=mesh['gx'=2,'gy'=4,'gz'=4] {'gx','gy','gz'}, dimensions={0} | all-to-all | bytes 32768 | tf_op jit(solution)/shard_map/all_to_all | solution.py:647
  30.0 1.2 %shard_map.81 = f32[320,128]{1,0:T(8,128)S(1)} custom-call(f32[32,128]{1,0:T(8,128)S(1)} %bitcast.12, f32[4,26,8,128]{3,2,1,0:T(8,128)S(1)} %get-tuple-element.35.refs_1_, f32[4,16,8,128]{3,2,1,0:T(8,128)S(1)} %get-tuple-element.26.refs_3_.refs_2_, f32[16,8,128]{2,1,0:T(8,128)S(1)} %get-tuple-element.36.refs_3_, ...), custom_call_target="tpu_custom_call" | custom-call | tf_op jit(solution)/shard_map/pallas_call | solution.py:592
  31.3 7.8 %all_to_all.23.refs_0_ = f32[8,40,128]{2,1,0:T(8,128)S(1)} all-to-all(f32[8,40,128]{2,1,0:T(8,128)S(1)} %bitcast.11), channel_id=1, replica_groups=mesh['gx'=2,'gy'=4,'gz'=4] {'gx','gz'}, dimensions={0} | all-to-all | bytes 327680 | tf_op jit(solution)/shard_map/all_to_all | solution.py:656
  39.1 1.0 %shard_map.82 = (f32[3,8,16,128]{3,2,1,0:T(8,128)}, f32[2,4,16,128]{3,2,1,0:T(8,128)}) custom-call(f32[8,40,128]{2,1,0:T(8,128)S(1)} %all_to_all.23.refs_0_, f32[3,8,16,128]{3,2,1,0:T(8,128)S(1)} %get-tuple-element.38.refs_1_, f32[3,8,16,128]{3,2,1,0:T(8,128)S(1)} %get-tuple-element.39.refs_2_), custom_call_target="tpu_custom_call" | custom-call | tf_op jit(solution)/shard_map/pallas_call | solution.py:592
Async XLA Ops:
  13.0 4.7 %collective-permute-start = (f32[11,8,128]{2,1,0:T(8,128)S(1)}, f32[11,8,128]{2,1,0:T(8,128)S(1)}, u32[]{:S(2)}, u32[]{:S(2)}) collective-permute-start(f32[11,8,128]{2,1,0:T(8,128)S(1)} %get-tuple-element.32), channel_id=1, source_target_pairs={{0,1},{2,3},{19,18},{17,16},{20,21},{22,23},{7,6},{5,4},{8,9},{10,... | collective-permute-start | bytes 135176 | tf_op jit(solution)/shard_map/ppermute | solution.py:626
  13.1 4.6 %collective-permute-start.2 = (f32[11,8,128]{2,1,0:T(8,128)S(1)}, f32[11,8,128]{2,1,0:T(8,128)S(1)}, u32[]{:S(2)}, u32[]{:S(2)}) collective-permute-start(f32[11,8,128]{2,1,0:T(8,128)S(1)} %get-tuple-element.33), channel_id=1, source_target_pairs={{20,24},{21,22},{23,7},{6,5},{4,8},{9,10},{11,27},{26,25},{0,1},{2... | collective-permute-start | bytes 135176 | tf_op jit(solution)/shard_map/ppermute | solution.py:626
  13.6 4.7 %collective-permute-start.1 = (f32[11,8,128]{2,1,0:T(8,128)S(1)}, f32[11,8,128]{2,1,0:T(8,128)S(1)}, u32[]{:S(2)}, u32[]{:S(2)}) collective-permute-start(f32[11,8,128]{2,1,0:T(8,128)S(1)} %get-tuple-element.33), channel_id=1, source_target_pairs={{0,4},{1,2},{3,19},{18,17},{16,20},{21,22},{23,7},{6,5},{8,12},{9,... | collective-permute-start | bytes 135176 | tf_op jit(solution)/shard_map/ppermute | solution.py:626
  16.3 0.7 %copy-start.1 = (f32[8,4]{0,1:T(4,128)S(1)}, f32[8,4]{0,1:T(4,128)}, u32[]{:S(2)}) copy-start(f32[8,4]{0,1:T(4,128)} %param.10) | copy-start | bytes 388
  16.3 0.7 %copy-start = (f32[8,4]{0,1:T(4,128)S(1)}, f32[8,4]{0,1:T(4,128)}, u32[]{:S(2)}) copy-start(f32[8,4]{0,1:T(4,128)} %param.9) | copy-start | bytes 388
  16.3 0.7 %copy-start.2 = (f32[8]{0:T(128)S(1)}, f32[8]{0:T(128)}, u32[]{:S(2)}) copy-start(f32[8]{0:T(128)} %param.11) | copy-start | bytes 100

commit v11 on v10

--- a/solution.py
+++ b/solution.py
@@ -156,10 +156,10 @@
 def edges_kernel(own_ref, *out_refs, ngx, ngz, zl, xl, chunk, margin):
     move = Shifts(ngx, ngz, zl, xl)
     read = column_reader(own_ref, ngx * ngz, chunk)
-    messages = []
-    for start in (0, chunk - margin):
+    messages, inner_margin = [], min(margin, HALO - 1)
+    for start, skip in ((0, 0), (chunk - margin, margin - inner_margin)):
         planes = [read(k, 0) for k in range(start, start + margin)]
-        planes += [column(move, read, k, chunk)[1] for k in range(start, start + margin)]
+        planes += [column(move, read, k, chunk)[1] for k in range(start + skip, start + skip + inner_margin)]
         messages.append(jnp.concatenate(planes + [read(0, 3)], axis=0))
     first, last = messages
     for h in range(len(out_refs) // 2):
@@ -328,24 +328,29 @@
         low, high = HALO + low, HALO + high
         return pieces(1 + k, low, step) + pieces(high, E - 1 - k, step)
 
+    inner_margin = min(margin, HALO - 1)
+
     def outer(j, up):
         hop, at = j // chunk, j % chunk
         index = at if up else margin - 1 - at
-        rhs = sides[up, hop, margin + index]
+        if j == HALO - 1:
+            return sides[up, hop, index], None
+        rhs = sides[up, hop, margin + (at if up else inner_margin - 1 - at)]
         if not up and at == 0:
-            rhs = rhs - (velocity_ref[2, 0] if hop == 0 else sides[0, hop - 1, 2 * margin])
+            rhs = rhs - (velocity_ref[2, 0] if hop == 0 else sides[0, hop - 1, margin + inner_margin])
         if up and at == chunk - 1 and hop + 1 < hops:
-            rhs = rhs - sides[1, hop + 1, 2 * margin]
+            rhs = rhs - sides[1, hop + 1, margin + inner_margin]
         return sides[up, hop, index], rhs
 
     for j in range(HALO):
         dens[HALO - 1 - j], low_rhs = outer(j, 0)
         dens[HALO + chunk + j], high_rhs = outer(j, 1)
-        source[HALO - 1 - j], source[HALO + chunk + j] = low_rhs, high_rhs
+        if j < HALO - 1:
+            source[HALO - 1 - j], source[HALO + chunk + j] = low_rhs, high_rhs
     dens[HALO : HALO + chunk] = density_ref[...]
     source[HALO : HALO + chunk] = source_ref[...]
     top = HALO + chunk - 1
-    source[top] = source[top] - sides[1, 0, 2 * margin]
+    source[top] = source[top] - sides[1, 0, margin + inner_margin]
     for k in range(ITERS):
         a, b = inner(k, chunk)
         if a < b:
@@ -615,7 +620,7 @@
         every = ("gx", "gy", "gz")
         own = pencils.reshape(-1, L)
         sizes = dict(ngx=ngx, ngz=ngz, zl=zl, xl=xl, chunk=chunk)
-        message = (2 * margin + 1, S, L)
+        message = (margin + min(margin, HALO - 1) + 1, S, L)
         messages = call(edges_kernel, [vmem], [placed(*message)] * (2 * hops), margin=margin, **sizes)(own)
         swaps = [(messages[i], hop_swaps(places, i // 2 + 1, i % 2)) for i in range(2 * hops)]
         runs = hops == 1 and ngy % 2 == 0 and S % 2 == 0

time: 40.4 us -> 40.3 us (level)
  no operation moved by 1% of the time
where the time goes in v11:
time: 40.3 us; the launch traced here: 40.1 us
  blocking collectives  30 us (74%)
  Pallas kernels  4.87 us (12%)
  starting transfers between devices  3.29 us (8%)
  local copies, waits for them, and re-layouts  0.7 us (2%)
  between operations  0.67 us (2%)
  waiting for transfers between devices  0.59 us (1%)
    all_to_all x1, blocking collectives, local(): pencils = lax.all_to_all(blocks, ('gx', 'gz'), 0, 0, tiled=True)  11.1 us
    all_to_all x1, blocking collectives, local(): sums = lax.all_to_all(sums, every, 0, 0, tiled=True)  11 us
    all_to_all x1, blocking collectives, local(): lax.all_to_all(packed.reshape(S, height, LANES), ('gx', 'gz'), 0, 0, tile...  7.81 us
    pallas_call x6, Pallas kernels, run(): kernel(*[near(a) if spec is vmem else a for a, spec in zip(args, specs)])  4.87 us
    ppermute x3, starting transfers between devices, local(): swapped.append(lax.ppermute(value, every, pairs))  3.29 us
  transfers between devices with their start and end apart: 3, of which 1 were waited for; matrix products, arithmetic and copies ran while one was open for 0% of the time, Pallas kernels for 2%

profile of v11, /device:TPU:0, one launch (start us, length us, event | category | flops | bytes accessed | tf_op | source)
XLA Modules:
  0.0 40.1 jit_solution(13882992428770481438)
XLA Ops:
  0.6 1.1 %shard_map.77 = (f32[8,64,128]{2,1,0:T(8,128)S(1)}, f32[8,16,128]{2,1,0:T(8,128)S(1)}, f32[3,8,16,128]{3,2,1,0:T(8,128)S(1)}) custom-call(s32[8,16,128]{2,1,0:T(8,128)} %refs_0_.1, f32[8,16,128]{2,1,0:T(8,128)} %refs_1_.1, f32[3,8,16,128]{3,2,1,0:T(8,128)} %refs_2_.1), custom_call_target="tpu_custom_call" | custom-call | tf_op jit(solution)/shard_map/pallas_call | solution.py:597
  1.8 11.1 %all_to_all.21 = f32[8,64,128]{2,1,0:T(8,128)S(1)} all-to-all(f32[8,64,128]{2,1,0:T(8,128)S(1)} %get-tuple-element.21), channel_id=1, replica_groups=mesh['gx'=2,'gy'=4,'gz'=4] {'gx','gz'}, dimensions={0} | all-to-all | bytes 524288 | tf_op jit(solution)/shard_map/all_to_all | solution.py:619
  12.9 0.1 shard_map.79
  13.0 0.1 collective-permute-start
  13.1 0.5 %collective-permute-start.2 = (f32[10,8,128]{2,1,0:T(8,128)S(1)}, f32[10,8,128]{2,1,0:T(8,128)S(1)}, u32[]{:S(2)}, u32[]{:S(2)}) collective-permute-start(f32[10,8,128]{2,1,0:T(8,128)S(1)} %get-tuple-element.33), channel_id=1, source_target_pairs={{20,24},{21,22},{23,7},{6,5},{4,8},{9,10},{11,27},{26,25},{0,1},{2... | collective-permute-start | bytes 122888 | tf_op jit(solution)/shard_map/ppermute | solution.py:631
  13.6 2.7 %collective-permute-start.1 = (f32[10,8,128]{2,1,0:T(8,128)S(1)}, f32[10,8,128]{2,1,0:T(8,128)S(1)}, u32[]{:S(2)}, u32[]{:S(2)}) collective-permute-start(f32[10,8,128]{2,1,0:T(8,128)S(1)} %get-tuple-element.33), channel_id=1, source_target_pairs={{0,4},{1,2},{3,19},{18,17},{16,20},{21,22},{23,7},{6,5},{8,12},{9,... | collective-permute-start | bytes 122888 | tf_op jit(solution)/shard_map/ppermute | solution.py:631
  16.3 0.0 copy-start.1
  16.3 0.0 copy-start
  16.3 0.0 copy-start.2
  16.3 0.7 %copy-done.1 = f32[8,4]{0,1:T(4,128)S(1)} copy-done((f32[8,4]{0,1:T(4,128)S(1)}, f32[8,4]{0,1:T(4,128)}, u32[]{:S(2)}) %copy-start.1) | copy-done | bytes 152
  17.0 0.0 copy-done
  17.0 0.0 copy-done.2
  17.0 0.7 %shard_map.78 = (f32[16,8,128]{2,1,0:T(8,128)S(1)}, f32[16,8,128]{2,1,0:T(8,128)S(1)}, f32[3,16,8,128]{3,2,1,0:T(8,128)S(1)}, f32[4,16,8,128]{3,2,1,0:T(8,128)S(...) custom-call(f32[512,128]{1,0:T(8,128)S(1)} %bitcast.10, ...), custom_call_target="tpu_custom_call" | custom-call | tf_op jit(solution)/shard_map/pallas_call | solution.py:597
  17.7 0.0 collective-permute-done.refs_9_
  17.7 0.0 collective-permute-done.2.refs_11_
  17.7 0.6 %collective-permute-done.1.refs_10_ = f32[10,8,128]{2,1,0:T(8,128)S(1)} collective-permute-done((f32[10,8,128]{2,1,0:T(8,128)S(1)}, f32[10,8,128]{2,1,0:T(8,128)S(1)}, u32[]{:S(2)}, u32[]{:S(2)}) %collective-permute-start.1) | collective-permute-done | bytes 40992 | tf_op jit(solution)/shard_map/ppermute | solution.py:631
  18.3 0.7 %shard_map.80 = (f32[4,26,8,128]{3,2,1,0:T(8,128)S(1)}, f32[16,8,128]{2,1,0:T(8,128)S(1)}, f32[32,128]{1,0:T(8,128)S(1)}) custom-call(f32[16,8,128]{2,1,0:T(8,128)S(1)} %get-tuple-element.23.refs_0_, f32[16,8,128]{2,1,0:T(8,128)S(1)} %get-tuple-element.24.refs_1_, f32[3,16,8,128]{3,2,1,0:T(8,128)S(1)} %get-tuple-element.25.refs_2_.refs_4_, ...), custom_call_target="tpu_custom_call" | custom-call | tf_op jit(solution)/shard_map/pallas_call | solution.py:597
  19.0 11.0 %all_to_all.22 = f32[32,1,128]{2,1,0:T(1,128)S(1)} all-to-all(f32[32,1,128]{2,1,0:T(1,128)S(1)} %bitcast.13), channel_id=1, replica_groups=mesh['gx'=2,'gy'=4,'gz'=4] {'gx','gy','gz'}, dimensions={0} | all-to-all | bytes 32768 | tf_op jit(solution)/shard_map/all_to_all | solution.py:652
  30.0 1.2 %shard_map.81 = f32[320,128]{1,0:T(8,128)S(1)} custom-call(f32[32,128]{1,0:T(8,128)S(1)} %bitcast.12, f32[4,26,8,128]{3,2,1,0:T(8,128)S(1)} %get-tuple-element.35.refs_1_, f32[4,16,8,128]{3,2,1,0:T(8,128)S(1)} %get-tuple-element.26.refs_3_.refs_2_, f32[16,8,128]{2,1,0:T(8,128)S(1)} %get-tuple-element.36.refs_3_, ...), custom_call_target="tpu_custom_call" | custom-call | tf_op jit(solution)/shard_map/pallas_call | solution.py:597
  31.2 7.8 %all_to_all.23.refs_0_ = f32[8,40,128]{2,1,0:T(8,128)S(1)} all-to-all(f32[8,40,128]{2,1,0:T(8,128)S(1)} %bitcast.11), channel_id=1, replica_groups=mesh['gx'=2,'gy'=4,'gz'=4] {'gx','gz'}, dimensions={0} | all-to-all | bytes 327680 | tf_op jit(solution)/shard_map/all_to_all | solution.py:661
  39.1 1.0 %shard_map.82 = (f32[3,8,16,128]{3,2,1,0:T(8,128)}, f32[2,4,16,128]{3,2,1,0:T(8,128)}) custom-call(f32[8,40,128]{2,1,0:T(8,128)S(1)} %all_to_all.23.refs_0_, f32[3,8,16,128]{3,2,1,0:T(8,128)S(1)} %get-tuple-element.38.refs_1_, f32[3,8,16,128]{3,2,1,0:T(8,128)S(1)} %get-tuple-element.39.refs_2_), custom_call_target="tpu_custom_call" | custom-call | tf_op jit(solution)/shard_map/pallas_call | solution.py:597
Async XLA Ops:
  13.0 4.7 %collective-permute-start = (f32[10,8,128]{2,1,0:T(8,128)S(1)}, f32[10,8,128]{2,1,0:T(8,128)S(1)}, u32[]{:S(2)}, u32[]{:S(2)}) collective-permute-start(f32[10,8,128]{2,1,0:T(8,128)S(1)} %get-tuple-element.32), channel_id=1, source_target_pairs={{0,1},{2,3},{19,18},{17,16},{20,21},{22,23},{7,6},{5,4},{8,9},{10,... | collective-permute-start | bytes 122888 | tf_op jit(solution)/shard_map/ppermute | solution.py:631
  13.1 4.6 %collective-permute-start.2 = (f32[10,8,128]{2,1,0:T(8,128)S(1)}, f32[10,8,128]{2,1,0:T(8,128)S(1)}, u32[]{:S(2)}, u32[]{:S(2)}) collective-permute-start(f32[10,8,128]{2,1,0:T(8,128)S(1)} %get-tuple-element.33), channel_id=1, source_target_pairs={{20,24},{21,22},{23,7},{6,5},{4,8},{9,10},{11,27},{26,25},{0,1},{2... | collective-permute-start | bytes 122888 | tf_op jit(solution)/shard_map/ppermute | solution.py:631
  13.6 4.7 %collective-permute-start.1 = (f32[10,8,128]{2,1,0:T(8,128)S(1)}, f32[10,8,128]{2,1,0:T(8,128)S(1)}, u32[]{:S(2)}, u32[]{:S(2)}) collective-permute-start(f32[10,8,128]{2,1,0:T(8,128)S(1)} %get-tuple-element.33), channel_id=1, source_target_pairs={{0,4},{1,2},{3,19},{18,17},{16,20},{21,22},{23,7},{6,5},{8,12},{9,... | collective-permute-start | bytes 122888 | tf_op jit(solution)/shard_map/ppermute | solution.py:631
  16.3 0.7 %copy-start.1 = (f32[8,4]{0,1:T(4,128)S(1)}, f32[8,4]{0,1:T(4,128)}, u32[]{:S(2)}) copy-start(f32[8,4]{0,1:T(4,128)} %param.10) | copy-start | bytes 388
  16.3 0.7 %copy-start = (f32[8,4]{0,1:T(4,128)S(1)}, f32[8,4]{0,1:T(4,128)}, u32[]{:S(2)}) copy-start(f32[8,4]{0,1:T(4,128)} %param.9) | copy-start | bytes 388
  16.3 0.7 %copy-start.2 = (f32[8]{0:T(128)S(1)}, f32[8]{0:T(128)}, u32[]{:S(2)}) copy-start(f32[8]{0:T(128)} %param.11) | copy-start | bytes 100
